TPU v7x, 32 devices: a whole 2x2x4 slice. The times are simulated.
32 devices in a mesh: mem: 8 (over z, core), col: 4 (over y, x).
Axes of the slice: x: 2, y: 2, z: 4, core: 2. Of those that a mesh axis runs over, the one named last changes fastest.
Arguments:
- perturbations: bfloat16 [8, 128, 8192], P('mem', None, 'col'), may hold values from -6 to 6
- vertical: bfloat16 [128, 128], replicated, may hold values from -0.5 to 0.5
- blocks: bfloat16 [128, 64, 128], replicated, may hold values from -0.5 to 0.5
- block_scale: float32 [128, 2], replicated, may hold values from 0.5 to 2
- block_cols: int32 [128, 2], replicated, may hold values from 0 to 127
- obs_level: int32 [8192], replicated, may hold values from 0 to 127
- obs_nodes: int32 [8192, 2], replicated, may hold values from 0 to 8191
- obs_weight: float32 [8192], replicated, may hold values from 0.2 to 0.8
- obs_value: float32 [8192], replicated, may hold values from -6 to 6
- obs_precision: float32 [8192], replicated, may hold values from 0.5 to 2
Outputs:
- control: bfloat16 [8, 128, 8192], P('mem', 'col')
- increment: float32 [128, 8192], P('mem', 'col')
All inputs are finite; a program needn't handle non-finite values.
Results may differ from a plain program's by a relative error of at most 0.018.
Values may be sent and summed in bfloat16 or wider, within the bound.
No kernel may reach another device: no remote copies, remote signals or barrier semaphores. Data moves between devices by JAX's collectives and lax.ppermute only.
A program may use at most 64 MiB of HBM per device.

v0:
```python
import math

import jax
import jax.numpy as jnp
from jax import lax
from jax.sharding import PartitionSpec as P

ITERS = 2


def column_table(block_cols, nblocks):
    flat_cols = block_cols.reshape(-1)
    return flat_cols[:, None] == jnp.arange(nblocks, dtype=jnp.int32)[None, :]


def horizontal(field, blocks, block_scale, block_cols):
    members, bands, nodes = field.shape
    nblocks, width, _ = blocks.shape
    kblocks = block_cols.shape[1]
    shaped = blocks.reshape(nblocks, width, kblocks, width)
    table = column_table(block_cols, nblocks).astype(jnp.bfloat16)
    rounded = field.astype(jnp.bfloat16).reshape(members * bands, nblocks, width)
    picked = jnp.einsum("pc,rcj->rpj", table, rounded, preferred_element_type=jnp.float32).astype(
        jnp.bfloat16
    )
    picked = picked.reshape(members * bands, nblocks, kblocks, width)
    terms = jnp.einsum("rikj,iakj->rika", picked, shaped, preferred_element_type=jnp.float32)
    mixed = rounded.astype(jnp.float32) + jnp.sum(terms * block_scale[None, :, :, None], axis=2)
    return mixed.reshape(members, bands, nodes).astype(jnp.bfloat16)


def horizontal_adjoint(moved, blocks, block_scale, block_cols):
    members, bands, nodes = moved.shape
    nblocks, width, _ = blocks.shape
    kblocks = block_cols.shape[1]
    shaped = blocks.reshape(nblocks, width, kblocks, width)
    table = column_table(block_cols, nblocks).astype(jnp.float32)
    flat = moved.reshape(members * bands, nblocks, width)
    terms = jnp.einsum("ria,iakj->rikj", flat, shaped, preferred_element_type=jnp.float32)
    terms = (terms * block_scale[None, :, :, None]).reshape(
        members * bands, nblocks * kblocks, width
    )
    spread = jnp.einsum(
        "pc,rpa->rca",
        table,
        terms,
        precision=lax.Precision.HIGHEST,
        preferred_element_type=jnp.float32,
    )
    return (flat.astype(jnp.float32) + spread).reshape(members, bands, nodes)


def obs_places(obs_level, obs_nodes, which, rows, ncols, level_lo, node_lo):
    local_node = obs_nodes[:, which] - node_lo
    local_level = obs_level - level_lo
    inside = (local_node >= 0) & (local_node < ncols) & (local_level >= 0) & (local_level < rows)
    index = jnp.where(inside, local_level * ncols + local_node, 0)
    return (inside, index)


def observe(field, level_lo, node_lo, obs_level, obs_nodes, obs_weight):
    rows, ncols = field.shape
    flat = field.reshape(-1)
    result = jnp.zeros(obs_weight.shape, jnp.float32)
    for which, weight in ((0, obs_weight), (1, 1.0 - obs_weight)):
        inside, index = obs_places(obs_level, obs_nodes, which, rows, ncols, level_lo, node_lo)
        result = result + jnp.where(inside, weight * flat[index], 0.0)
    return result


def spread_obs(errors, rows, ncols, level_lo, node_lo, obs_level, obs_nodes, obs_weight):
    flat = jnp.zeros((rows * ncols,), jnp.float32)
    for which, weight in ((0, obs_weight), (1, 1.0 - obs_weight)):
        inside, index = obs_places(obs_level, obs_nodes, which, rows, ncols, level_lo, node_lo)
        flat = flat.at[index].add(jnp.where(inside, weight * errors, 0.0))
    return flat.reshape(rows, ncols)


def per_device(
    perturbations,
    vertical,
    blocks,
    block_scale,
    block_cols,
    obs_level,
    obs_nodes,
    obs_weight,
    obs_value,
    obs_precision,
):
    local_members, levels, ncols = perturbations.shape
    members = local_members * lax.axis_size("mem")
    scale_inv = 1.0 / math.sqrt(members)
    node_lo = lax.axis_index("col") * ncols
    part_rows = levels // lax.axis_size("mem")
    level_lo = lax.axis_index("mem") * part_rows

    def adjoint(grad):
        scaled = (perturbations * grad[None] * scale_inv).astype(jnp.bfloat16)
        turned = scaled.astype(jnp.float32) + jnp.einsum(
            "ml,dmn->dln", vertical, scaled, preferred_element_type=jnp.float32
        )
        moved = lax.all_to_all(
            turned.astype(jnp.bfloat16), "col", split_axis=1, concat_axis=2, tiled=True
        )
        return horizontal_adjoint(moved, blocks, block_scale, block_cols)

    def forward_local(field):
        mixed = horizontal(field, blocks, block_scale, block_cols)
        columns = lax.all_to_all(mixed, "col", split_axis=2, concat_axis=1, tiled=True)
        localized = columns.astype(jnp.float32) + jnp.einsum(
            "lm,dmn->dln", vertical, columns, preferred_element_type=jnp.float32
        )
        return jnp.sum(perturbations * localized, axis=0) * scale_inv

    def member_total(field):
        local_sum = forward_local(field)
        return (lax.psum_scatter(local_sum, "mem", scatter_dimension=0, tiled=True), level_lo)

    start_grad = spread_obs(
        obs_precision * obs_value, levels, ncols, 0, node_lo, obs_level, obs_nodes, obs_weight
    )
    residual = adjoint(start_grad)
    direction = residual
    state = jnp.zeros_like(residual)
    norm_now = lax.psum(jnp.sum(residual * residual), ("mem", "col"))
    for step in range(ITERS):
        hessian_total, hessian_low = member_total(direction)
        equiv = lax.psum(
            observe(hessian_total, hessian_low, node_lo, obs_level, obs_nodes, obs_weight),
            ("mem", "col"),
        )
        part_grad = spread_obs(
            obs_precision * equiv,
            part_rows,
            ncols,
            hessian_low,
            node_lo,
            obs_level,
            obs_nodes,
            obs_weight,
        )
        hessian_grad = lax.all_gather(part_grad, "mem", axis=0, tiled=True)
        image = direction + adjoint(hessian_grad)
        final_step = step + 1 == ITERS
        along = lax.psum(jnp.sum(direction * image), ("mem", "col"))
        alpha = norm_now / along
        state = state + alpha * direction
        residual = residual - alpha * image
        if not final_step:
            norm_next = lax.psum(jnp.sum(residual * residual), ("mem", "col"))
        if not final_step:
            direction = residual + norm_next / norm_now * direction
            norm_now = norm_next
    total, low = member_total(state)
    return (state.astype(jnp.bfloat16), total)


def solution(mesh):
    in_specs = (P("mem", None, "col"), P(), P(), P(), P(), P(), P(), P(), P(), P())
    out_specs = (P("mem", "col", None), P("mem", "col"))
    return jax.shard_map(
        per_device, mesh=mesh, in_specs=in_specs, out_specs=out_specs, check_vma=False
    )
```

profile of v0, /device:TPU:0, one launch (start us, length us, event | category | flops | bytes accessed | tf_op | source)
XLA Modules:
  0.0 1314.4 jit_solution(5426057137467677423)
XLA Ops:
  10.6 45.5 %scatter_custom_fusion = f32[262144]{0:T(1024)S(1)} fusion(s32[8192]{0:T(1024)S(1)} %get-tuple-element.30, f32[8192]{0:T(1024)S(1)} %get-tuple-element.24, f32[]{:T(128)} %constant.12.clone.1), kind=kCustom, calls=%fused_computation.97 | custom fusion | flops 8192 | bytes 1048580 | tf_op jit(solution)/shard_map/scatter-add | solution.py:75
  56.1 46.8 %scatter_fusion = f32[262144]{0:T(1024)S(1)} fusion(f32[262144]{0:T(1024)S(1)} %scatter_custom_fusion, s32[8192]{0:T(1024)S(1)} %get-tuple-element.29, f32[8192]{0:T(1024)S(1)} %get-tuple-element.23), kind=kCustom, calls=%fused_computation.5 | custom fusion | flops 8192 | bytes 131072 | tf_op jit(solution)/shard_map/scatter-add | solution.py:75
  110.9 4.7 all-to-all-start
  116.1 4.2 copy.146
  120.3 7.5 copy.148
  134.0 5.0 fusion.30
  139.5 4.0 copy.152
  143.6 6.6 multiply_reduce_fusion.2
  156.9 12.5 reshape.413
  169.4 46.6 %reduce.8 = bf16[8192,32]{1,0:T(8,128)(2,1)} reduce(bf16[8192,1,32]{2,1,0:T(2,128)(2,1)} %bitcast.247, bf16[]{:T(256)} %broadcast.207), dimensions={1}, to_apply=%bitcast.205.reduce_sub_computation | reduce | bytes 1048578
  219.7 12.2 all_to_all.90
  235.2 8.0 copy.158
  249.9 33.0 %reduce-scatter.10.cloned.1.call-done = f32[16,2048]{1,0:T(8,128)} async-done(((f32[128,2048]{1,0:T(8,128)}), f32[16,2048]{1,0:T(8,128)}) %reduce-scatter.10.cloned.1.call-update) | async-done | bytes 131088 | tf_op jit(solution)/shard_map/reduce_scatter | solution.py:118
  283.8 45.5 %gather_fusion = f32[8192]{0:T(1024)S(1)} fusion(f32[32768]{0:T(1024)S(1)} %bitcast.241, s32[8192]{0:T(1024)S(1)} %get-tuple-element.15), kind=kCustom, calls=%fused_computation | custom fusion | bytes 98304 | tf_op jit(solution)/shard_map/gather | solution.py:67
  329.3 45.5 %gather_fusion.1 = f32[8192]{0:T(1024)S(1)} fusion(f32[32768]{0:T(1024)S(1)} %bitcast.242, s32[8192]{0:T(1024)S(1)} %get-tuple-element.20), kind=kCustom, calls=%fused_computation.1 | custom fusion | bytes 98304 | tf_op jit(solution)/shard_map/gather | solution.py:67
  374.9 37.9 %psum.43 = f32[8192]{0:T(1024)S(1)} all-reduce(f32[8192]{0:T(1024)S(1)} %select_add_fusion.1), channel_id=1, replica_groups=mesh['mem'=8,'col'=4] {'mem','col'}, use_global_device_ids=true, to_apply=%region_6.7 | all-reduce | flops 8192 | bytes 65536 | tf_op jit(solution)/shard_map/psum | solution.py:129
  412.8 55.3 %scatter_custom_fusion.2 = f32[32768]{0:T(1024)S(1)} fusion(s32[8192]{0:T(1024)S(1)} %get-tuple-element.16, f32[8192]{0:T(1024)S(1)} %get-tuple-element.28, f32[]{:T(128)} %constant.12.clone.1), kind=kCustom, calls=%fused_computation.109 | custom fusion | flops 8192 | bytes 131076 | tf_op jit(solution)/shard_map/scatter-add | solution.py:75
  468.1 55.4 %scatter_fusion.1 = f32[32768]{0:T(1024)S(1)} fusion(f32[32768]{0:T(1024)S(1)} %scatter_custom_fusion.2, s32[8192]{0:T(1024)S(1)} %get-tuple-element.21, f32[8192]{0:T(1024)S(1)} %get-tuple-element.27), kind=kCustom, calls=%fused_computation.7 | custom fusion | flops 8192 | bytes 131072 | tf_op jit(solution)/shard_map/scatter-add | solution.py:75
  524.3 22.9 %all-gather.3.cloned.1.call-done = f32[128,2048]{1,0:T(8,128)} async-done(((f32[16,2048]{1,0:T(8,128)}), f32[128,2048]{1,0:T(8,128)}) %all-gather.3.cloned.1.call-update) | async-done | bytes 1048592 | tf_op jit(solution)/shard_map/all_gather | solution.py:143
  554.1 12.8 all_to_all.91
  574.6 6.6 multiply_reduce_fusion.4
  581.3 39.5 %all-reduce = (f32[]{:T(128)}, f32[]{:T(128)}) all-reduce(f32[]{:T(128)} %get-tuple-element.11, f32[]{:T(128)} %get-tuple-element.10), channel_id=1, replica_groups=mesh['mem'=8,'col'=4] {'mem','col'}, use_global_device_ids=true, to_apply=%region_3.4 | all-reduce | flops 2 | bytes 16 | tf_op jit(solution)/shard_map/psum | solution.py:126
  623.0 39.8 %psum.45 = f32[]{:T(128)} all-reduce(f32[]{:T(128)} %multiply_reduce_fusion.3), channel_id=1, replica_groups=mesh['mem'=8,'col'=4] {'mem','col'}, use_global_device_ids=true, to_apply=%region_12.13 | all-reduce | flops 1 | bytes 8 | tf_op jit(solution)/shard_map/psum | solution.py:151
  667.1 4.7 copy.170
  671.8 6.6 multiply_reduce_fusion.1
  687.4 12.5 reshape.414
  699.9 46.8 %reduce.10 = bf16[8192,32]{1,0:T(8,128)(2,1)} reduce(bf16[8192,1,32]{2,1,0:T(2,128)(2,1)} %bitcast.249, bf16[]{:T(256)} %broadcast.207), dimensions={1}, to_apply=%bitcast.209.reduce_sub_computation | reduce | bytes 1048578
  750.4 11.4 all_to_all.92
  761.8 4.7 reshape.435
  766.5 8.7 copy.175
  785.2 30.9 %reduce-scatter.12.cloned.1.call-done = f32[16,2048]{1,0:T(8,128)} async-done(((f32[128,2048]{1,0:T(8,128)}), f32[16,2048]{1,0:T(8,128)}) %reduce-scatter.12.cloned.1.call-update) | async-done | bytes 131088 | tf_op jit(solution)/shard_map/reduce_scatter | solution.py:118
  817.0 45.5 %gather_fusion.2 = f32[8192]{0:T(1024)S(1)} fusion(f32[32768]{0:T(1024)S(1)} %bitcast.239, s32[8192]{0:T(1024)S(1)} %get-tuple-element.15), kind=kCustom, calls=%fused_computation.2 | custom fusion | bytes 98304 | tf_op jit(solution)/shard_map/gather | solution.py:67
  862.5 45.5 %gather_fusion.3 = f32[8192]{0:T(1024)S(1)} fusion(f32[32768]{0:T(1024)S(1)} %bitcast.240, s32[8192]{0:T(1024)S(1)} %get-tuple-element.20), kind=kCustom, calls=%fused_computation.3 | custom fusion | bytes 98304 | tf_op jit(solution)/shard_map/gather | solution.py:67
  908.1 38.0 %psum.46 = f32[8192]{0:T(1024)S(1)} all-reduce(f32[8192]{0:T(1024)S(1)} %select_add_fusion), channel_id=1, replica_groups=mesh['mem'=8,'col'=4] {'mem','col'}, use_global_device_ids=true, to_apply=%region_15.16 | all-reduce | flops 8192 | bytes 65536 | tf_op jit(solution)/shard_map/psum | solution.py:129
  946.1 55.3 %scatter_custom_fusion.4 = f32[32768]{0:T(1024)S(1)} fusion(s32[8192]{0:T(1024)S(1)} %get-tuple-element.16, f32[8192]{0:T(1024)S(1)} %get-tuple-element.26, f32[]{:T(128)} %constant.12.clone.1), kind=kCustom, calls=%fused_computation.107 | custom fusion | flops 8192 | bytes 131076 | tf_op jit(solution)/shard_map/scatter-add | solution.py:75
  1001.4 55.4 %scatter_fusion.2 = f32[32768]{0:T(1024)S(1)} fusion(f32[32768]{0:T(1024)S(1)} %scatter_custom_fusion.4, s32[8192]{0:T(1024)S(1)} %get-tuple-element.21, f32[8192]{0:T(1024)S(1)} %get-tuple-element.25), kind=kCustom, calls=%fused_computation.9 | custom fusion | flops 8192 | bytes 131072 | tf_op jit(solution)/shard_map/scatter-add | solution.py:75
  1057.9 22.5 %all-gather.5.cloned.1.call-done = f32[128,2048]{1,0:T(8,128)} async-done(((f32[16,2048]{1,0:T(8,128)}), f32[128,2048]{1,0:T(8,128)}) %all-gather.5.cloned.1.call-update) | async-done | bytes 1048592 | tf_op jit(solution)/shard_map/all_gather | solution.py:143
  1087.0 4.7 reduce.11
  1092.9 12.6 all_to_all.93
  1118.0 5.6 fusion.59
  1123.7 39.6 %psum.47 = f32[]{:T(128)} all-reduce(f32[]{:T(128)} %fusion.59), channel_id=1, replica_groups=mesh['mem'=8,'col'=4] {'mem','col'}, use_global_device_ids=true, to_apply=%region_19.20 | all-reduce | flops 1 | bytes 8 | tf_op jit(solution)/shard_map/psum | solution.py:146
  1169.2 6.6 multiply_reduce_fusion
  1179.4 5.3 copy.207
  1184.7 12.5 reshape.415
  1197.2 46.7 %reduce.12 = bf16[8192,32]{1,0:T(8,128)(2,1)} reduce(bf16[8192,1,32]{2,1,0:T(2,128)(2,1)} %bitcast.246, bf16[]{:T(256)} %broadcast.207), dimensions={1}, to_apply=%bitcast.213.reduce_sub_computation | reduce | bytes 1048578
  1247.7 11.2 all_to_all.94
  1262.3 8.0 copy.192
  1286.2 21.4 %reduce-scatter.14.cloned.1.call-done = f32[16,2048]{1,0:T(8,128)} async-done(((f32[128,2048]{1,0:T(8,128)}), f32[16,2048]{1,0:T(8,128)}) %reduce-scatter.14.cloned.1.call-update) | async-done | bytes 131088
  (117 shorter events, 135.0 us)
Async XLA Ops:
  7.2 97.1 %copy-start = (bf16[128,128]{1,0:T(8,128)(2,1)S(1)}, bf16[128,128]{1,0:T(8,128)(2,1)}, u32[]{:S(2)}) copy-start(bf16[128,128]{1,0:T(8,128)(2,1)} %param.11) | copy-start | bytes 98308
  102.9 1.0 copy-start.4
  110.9 17.3 %all-to-all-start = ((bf16[4,2,32768]{2,1,0:T(2,128)(2,1)}), bf16[4,2,32768]{2,1,0:T(2,128)(2,1)S(1)}, u32[]{:S(2)}, u32[]{:S(2)}) async-start(bf16[4,2,32768]{2,1,0:T(2,128)(2,1)} %reshape.428), calls=%async_computation | async-start | bytes 1048576 | tf_op jit(solution)/shard_map/all_to_all | solution.py:103
  115.7 167.2 %reduce-scatter.10.cloned.1.call-start = ((), (), s32[]{:S(2)}) async-start(), calls=%async_computation.11 | async-start | bytes 1179648 | tf_op jit(solution)/shard_map/reduce_scatter | solution.py:118
  120.3 7.5 copy-start.6
  120.3 7.6 copy-start.7
  249.8 297.4 %all-gather.3.cloned.1.call-start = ((), (), s32[]{:S(2)}) async-start(), calls=%async_computation.9 | async-start | bytes 1179648 | tf_op jit(solution)/shard_map/all_gather | solution.py:143
  329.3 45.6 %copy-start.3 = (f32[8192]{0:T(1024)S(1)}, f32[8192]{0:T(1024)}, u32[]{:S(2)}) copy-start(f32[8192]{0:T(1024)} %param.17) | copy-start | bytes 98308
  329.3 83.5 %copy-start.5 = (f32[8192]{0:T(1024)S(1)}, f32[8192]{0:T(1024)}, u32[]{:S(2)}) copy-start(f32[8192]{0:T(1024)} %param.19) | copy-start | bytes 98308
  524.2 291.8 %reduce-scatter.12.cloned.1.call-start = ((), (), s32[]{:S(2)}) async-start(), calls=%async_computation.12 | async-start | bytes 1179648 | tf_op jit(solution)/shard_map/reduce_scatter | solution.py:118
  581.3 81.6 %copy-start.1 = (f32[32,128,64]{1,2,0:T(8,128)}, f32[32,128,64]{1,2,0:T(8,128)S(1)}, u32[]{:S(2)}) copy-start(f32[32,128,64]{1,2,0:T(8,128)S(1)} %get-tuple-element.14) | copy-start | bytes 3145732
  785.1 295.4 %all-gather.5.cloned.1.call-start = ((), (), s32[]{:S(2)}) async-start(), calls=%async_computation.10 | async-start | bytes 1179648 | tf_op jit(solution)/shard_map/all_gather | solution.py:143
  1057.5 250.1 %reduce-scatter.14.cloned.1.call-start = ((), (), s32[]{:S(2)}) async-start(), calls=%async_computation.13 | async-start | bytes 1179648
  1276.9 4.1 copy-start.2
Sparse Core Ops, SparseCore 0:
  249.9 32.8 reduce-scatter.9
  524.4 22.8 all-gather.2
  785.2 30.7 reduce-scatter.11
  1057.6 22.8 all-gather.4
  1277.0 30.5 reduce-scatter.13
where the time goes:
time: 1320 us; the launch traced here: 1310 us
  other arithmetic  479 us (36%)
  local copies, waits for them, and re-layouts  368 us (28%)
  blocking collectives  255 us (19%)
  waiting for transfers between devices  131 us (10%)
  matrix products  57.6 us (4%)
  between operations  18.6 us (1%)
    scatter-add x6, other arithmetic, spread_obs(): flat = flat.at[index].add(jnp.where(inside, weight * errors, 0.0))  314 us
    gather x4, local copies, waits for them, and re-layouts, observe(): result = result + jnp.where(inside, weight * flat[index], 0.0)  182 us
    unnamed x6, other arithmetic  152 us
    psum x2, blocking collectives, per_device(): lax.psum(observe(hessian_total, hessian_low, node_lo, obs_level, obs_node...  75.9 us
    reduce_scatter x2, waiting for transfers between devices, member_total(): lax.psum_scatter(local_sum, 'mem', scatter_dimension=0, tiled=True)  63.8 us
    convert_element_type x6, local copies, waits for them, and re-layouts, horizontal(): return mixed.reshape(members, bands, nodes).astype(jnp.bfloat16)  50.7 us
    unnamed x41, local copies, waits for them, and re-layouts  45.5 us
    all_gather x2, waiting for transfers between devices, per_device(): hessian_grad = lax.all_gather(part_grad, 'mem', axis=0, tiled=True)  45.5 us
  transfers between devices with their start and end apart: 6, of which 5 were waited for; matrix products, arithmetic and copies ran while one was open for 2% of the time, Pallas kernels for 0%

commit v1 on v0

v1 whole, which is shorter than its diff:
```python
import functools
import math

import jax
import jax.numpy as jnp
from jax import lax
from jax.experimental import pallas as pl
from jax.experimental.pallas import tpu as pltpu
from jax.sharding import PartitionSpec as P

ITERS = 2
LANES = 128
WIDE = 512
CHUNK = 512
HALF = 256


def one_hot(keys, rows, values):
    n = keys.shape[1]
    parts = []
    for low in range(0, rows, HALF):
        size = min(HALF, rows - low)
        row = lax.broadcasted_iota(jnp.int32, (size, n), 0).astype(jnp.float32).astype(jnp.bfloat16)
        key = jnp.broadcast_to((keys - low).astype(jnp.float32).astype(jnp.bfloat16), (size, n))
        val = jnp.broadcast_to(values, (size, n))
        parts.append(jnp.where(row == key, val, jnp.zeros_like(val)))
    return parts[0] if len(parts) == 1 else jnp.concatenate(parts, axis=0)


def places(level, node, node_lo, levels, ncols):
    wide = min(WIDE, ncols)
    local = node - node_lo
    inside = (local >= 0) & (local < ncols)
    row = jnp.where(inside, (local // wide) * levels + level, -1024)
    lane = jnp.where(inside, local % wide, -1024)
    return row, lane


def adjoint_kernel(
    node_ref, level_ref, n1_ref, n2_ref, weight_ref, err_ref, pert_ref, vert_ref, out_ref, total
):
    levels, ncols = pert_ref.shape
    bands = out_ref.shape[1]
    members = node_ref[1]
    wide = min(WIDE, ncols)
    chunks = ncols // wide
    node_lo = node_ref[0]
    total[...] = jnp.zeros_like(total)

    def step(c, carry):
        level = level_ref[pl.ds(c, 1), :]
        weight = weight_ref[pl.ds(c, 1), :]
        err = err_ref[pl.ds(c, 1), :]
        rows, lanes = [], []
        for ref, w in ((n1_ref, weight), (n2_ref, 1.0 - weight)):
            row, lane = places(level, ref[pl.ds(c, 1), :], node_lo, levels, ncols)
            rows.append(one_hot(row, chunks * levels, (w * err).astype(jnp.bfloat16)))
            lanes.append(one_hot(lane, wide, jnp.ones_like(w).astype(jnp.bfloat16)))
        total[...] += lax.dot_general(
            jnp.concatenate(rows, axis=1),
            jnp.concatenate(lanes, axis=1),
            (((1,), (1,)), ((), ())),
            preferred_element_type=jnp.float32,
        )
        return carry

    lax.fori_loop(0, level_ref.shape[0], step, 0)
    scale_inv = 1.0 / jnp.sqrt(jnp.full((1, wide), members, jnp.int32).astype(jnp.float32))
    for c in range(chunks):
        part = slice(c * wide, (c + 1) * wide)
        grad = total[c * levels : (c + 1) * levels, :]
        scaled = (pert_ref[:, part].astype(jnp.float32) * grad * scale_inv).astype(jnp.bfloat16)
        turned = scaled.astype(jnp.float32) + lax.dot_general(
            vert_ref[...], scaled, (((0,), (0,)), ((), ())), preferred_element_type=jnp.float32
        )
        for b in range(out_ref.shape[0]):
            out_ref[b, :, part] = turned[b * bands : (b + 1) * bands, :].astype(jnp.bfloat16)


def horizontal_kernel(cols_ref, moved_ref, mats_ref, resid_ref, mixed_ref, spread, picked):
    parts, bands, ncols = moved_ref.shape
    pairs = mats_ref.shape[0]
    per_part = ncols // LANES
    half = LANES // 2
    low = lax.broadcasted_iota(jnp.int32, (bands, LANES), 1) < half
    spread[...] = jnp.zeros_like(spread)

    def tile_of(p):
        lane = pl.multiple_of((p % per_part) * LANES, LANES)
        return p // per_part, pl.ds(lane, LANES)

    def scatter(p, carry):
        part, lanes = tile_of(p)
        terms = jnp.dot(moved_ref[part, :, lanes], mats_ref[p], preferred_element_type=jnp.float32)
        for q in range(2):
            term = terms[:, q * LANES : (q + 1) * LANES]
            for k in range(2):
                col = cols_ref[4 * p + 2 * q + k]
                kept = jnp.where(low, term, 0.0) if k == 0 else jnp.where(low, 0.0, term)
                slot = (col & 1) ^ k
                spread[slot, col >> 1] += kept
        return carry

    lax.fori_loop(0, pairs, scatter, 0)

    def join(p, carry):
        part, lanes = tile_of(p)
        resid = (
            moved_ref[part, :, lanes].astype(jnp.float32)
            + spread[0, p]
            + pltpu.roll(spread[1, p], half, 1)
        )
        resid_ref[:, pl.ds(pl.multiple_of(p * LANES, LANES), LANES)] = resid
        picked[0, p] = resid.astype(jnp.bfloat16).astype(jnp.float32)
        picked[1, p] = pltpu.roll(resid, half, 1).astype(jnp.bfloat16).astype(jnp.float32)
        return carry

    lax.fori_loop(0, pairs, join, 0)

    def gather(p, carry):
        part, lanes = tile_of(p)
        sources = []
        for q in range(2):
            first = cols_ref[4 * p + 2 * q]
            second = cols_ref[4 * p + 2 * q + 1]
            sources.append(
                jnp.where(low, picked[first & 1, first >> 1], picked[(second & 1) ^ 1, second >> 1])
            )
        terms = lax.dot_general(
            jnp.concatenate(sources, axis=1).astype(jnp.bfloat16),
            mats_ref[p],
            (((1,), (1,)), ((), ())),
            preferred_element_type=jnp.float32,
        )
        mixed_ref[part, :, lanes] = (picked[0, p] + terms).astype(jnp.bfloat16)
        return carry

    lax.fori_loop(0, pairs, gather, 0)


def forward_kernel(
    node_ref, level_ref, n1_ref, n2_ref, weight_ref, mixed_ref, pert_ref, vert_ref, field_ref, obs_ref, table
):
    levels, ncols = pert_ref.shape
    wide = min(WIDE, ncols)
    chunks = ncols // wide
    node_lo = node_ref[0]
    members = node_ref[1]
    scale_inv = 1.0 / jnp.sqrt(jnp.full((1, wide), members, jnp.int32).astype(jnp.float32))
    for c in range(chunks):
        part = slice(c * wide, (c + 1) * wide)
        mixed = mixed_ref[:, part]
        localized = mixed.astype(jnp.float32) + jnp.dot(
            vert_ref[...], mixed, preferred_element_type=jnp.float32
        )
        field = pert_ref[:, part].astype(jnp.float32) * localized * scale_inv
        field_ref[:, part] = field
        table[c * levels : (c + 1) * levels, :] = field.astype(jnp.bfloat16)

    def step(c, carry):
        level = level_ref[pl.ds(c, 1), :]
        weight = weight_ref[pl.ds(c, 1), :]
        result = jnp.zeros(weight.shape, jnp.float32)
        for ref, w in ((n1_ref, weight), (n2_ref, 1.0 - weight)):
            row, lane = places(level, ref[pl.ds(c, 1), :], node_lo, levels, ncols)
            hot = one_hot(lane, wide, jnp.ones_like(w).astype(jnp.bfloat16))
            lines = jnp.dot(table[...], hot, preferred_element_type=jnp.float32)
            number = lax.broadcasted_iota(jnp.int32, lines.shape, 0)
            kept = jnp.where(number == row, lines, 0.0)
            result = result + w * jnp.sum(kept, axis=0, keepdims=True)
        obs_ref[pl.ds(c, 1), :] = result
        return carry

    lax.fori_loop(0, level_ref.shape[0], step, 0)


def everywhere(x):
    for axis in ("col", "mem"):
        n = lax.axis_size(axis)
        sent = jnp.broadcast_to(x[None], (n,) + x.shape)
        x = jnp.sum(lax.all_to_all(sent, axis, 0, 0, tiled=True), axis=0)
    return x


def per_device(
    perturbations,
    vertical,
    blocks,
    block_scale,
    block_cols,
    obs_level,
    obs_nodes,
    obs_weight,
    obs_value,
    obs_precision,
):
    local_members, levels, ncols = perturbations.shape
    assert local_members == 1
    nblocks, width, depth = blocks.shape
    assert 2 * width == LANES and depth == LANES
    members = local_members * lax.axis_size("mem")
    ncol = lax.axis_size("col")
    nmem = lax.axis_size("mem")
    bands = levels // ncol
    pairs = nblocks // 2
    pert = perturbations[0]
    info = jnp.stack([lax.axis_index("col") * ncols, jnp.int32(members)]).astype(jnp.int32)
    rows = obs_level.shape[0] // CHUNK

    scaled = (blocks.astype(jnp.float32) * jnp.repeat(block_scale, width, axis=1)[:, None, :]).astype(
        jnp.bfloat16
    ).reshape(pairs, 2, width, depth)
    mats = jnp.concatenate(
        [
            jnp.pad(scaled[:, 0], ((0, 0), (0, 0), (0, depth))),
            jnp.pad(scaled[:, 1], ((0, 0), (0, 0), (depth, 0))),
        ],
        axis=1,
    )
    cols = block_cols.reshape(-1)
    level, first, second, weight, value, precision = (
        a.reshape(rows, CHUNK)
        for a in (obs_level, obs_nodes[:, 0], obs_nodes[:, 1], obs_weight, obs_value, obs_precision)
    )

    vmem = pl.BlockSpec(memory_space=pltpu.VMEM)
    smem = pl.BlockSpec(memory_space=pltpu.SMEM)
    wide = min(WIDE, ncols)

    adjoint = pl.pallas_call(
        adjoint_kernel,
        out_shape=jax.ShapeDtypeStruct((ncol, bands, ncols), jnp.bfloat16),
        in_specs=[smem] + [vmem] * 7,
        out_specs=vmem,
        scratch_shapes=[pltpu.VMEM((ncols // wide * levels, wide), jnp.float32)],
        name="adjoint",
    )
    middle = pl.pallas_call(
        horizontal_kernel,
        out_shape=(
            jax.ShapeDtypeStruct((bands, nblocks * width), jnp.float32),
            jax.ShapeDtypeStruct((ncol, bands, ncols), jnp.bfloat16),
        ),
        in_specs=[smem] + [vmem] * 2,
        out_specs=(vmem, vmem),
        scratch_shapes=[
            pltpu.VMEM((2, pairs, bands, LANES), jnp.float32),
            pltpu.VMEM((2, pairs, bands, LANES), jnp.float32),
        ],
        name="horizontal",
    )
    forward = pl.pallas_call(
        forward_kernel,
        out_shape=(
            jax.ShapeDtypeStruct((levels, ncols), jnp.float32),
            jax.ShapeDtypeStruct((rows, CHUNK), jnp.float32),
        ),
        in_specs=[smem] + [vmem] * 7,
        out_specs=(vmem, vmem),
        scratch_shapes=[pltpu.VMEM((ncols // wide * levels, wide), jnp.bfloat16)],
        name="forward",
    )

    def gram(errors):
        sent = adjoint(info, level, first, second, weight, errors, pert, vertical)
        moved = lax.all_to_all(sent, "col", 0, 0, tiled=True)
        resid, mixed = middle(cols, moved, mats)
        columns = lax.all_to_all(mixed, "col", 0, 0, tiled=True).reshape(levels, ncols)
        field, partial = forward(info, level, first, second, weight, columns, pert, vertical)
        return resid, field, everywhere(partial)

    errors = precision * value
    fields, resids = [], []
    shares = []
    for step in range(ITERS):
        resid, field, seen = gram(errors)
        resids.append(resid)
        fields.append(field)
        norm_next = jnp.sum(errors * seen)
        if step == 0:
            guide, image = errors, seen
            mix = [jnp.float32(1.0)]
        else:
            beta = norm_next / norm_now
            guide, image = errors + beta * guide, seen + beta * image
            mix = [beta * m for m in mix] + [jnp.float32(1.0)]
        norm_now = norm_next
        along = jnp.sum(guide * image) + jnp.sum(precision * image * image)
        alpha = norm_now / along
        shares = [s + alpha * m for s, m in zip(shares + [jnp.float32(0.0)], mix)]
        errors = errors - alpha * (guide + precision * image)
    state = sum(c * r for c, r in zip(shares, resids))
    total = sum(c * f for c, f in zip(shares, fields)).astype(jnp.bfloat16)
    pieces = lax.all_to_all(
        total.reshape(nmem, levels // nmem, ncols), "mem", 0, 0, tiled=True
    )
    increment = jnp.sum(pieces.astype(jnp.float32), axis=0)
    return (state.astype(jnp.bfloat16)[None], increment)


def solution(mesh):
    in_specs = (P("mem", None, "col"), P(), P(), P(), P(), P(), P(), P(), P(), P())
    out_specs = (P("mem", "col", None), P("mem", "col"))
    return jax.shard_map(
        per_device, mesh=mesh, in_specs=in_specs, out_specs=out_specs, check_vma=False
    )
```

time: 1320 us -> 254 us (0.19)
  other arithmetic: 479 us -> 10.5 us
  local copies, waits for them, and re-layouts: 368 us -> 11.6 us
  blocking collectives: 255 us -> 78.6 us
  Pallas kernels: 0 us -> 121 us
  waiting for transfers between devices: 131 us -> 16.9 us
  matrix products: 57.6 us -> 0 us
    scatter-add x6 -> x0, other arithmetic: 314 us -> none  [spread_obs(): flat = flat.at[index].add(jnp.where(inside, weight * errors, 0.0))]
    psum x5 -> x0, blocking collectives: 195 us -> none  [the longest x2 75.9 us: per_device(): lax.psum(observe(hessian_total, hessian_low, node_lo, obs_level, obs_node...]
    gather x4 -> x0, local copies, waits for them, and re-layouts: 182 us -> none  [observe(): result = result + jnp.where(inside, weight * flat[index], 0.0)]
    unnamed x6 -> x0, other arithmetic: 152 us -> none
    pallas_call x0 -> x6, Pallas kernels: none -> 121 us  [the longest x2 63.1 us: gram(): resid, mixed = middle(cols, moved, mats)]
    convert_element_type x15 -> x0, local copies, waits for them, and re-layouts: 72.9 us -> none  [the longest x6 50.7 us: horizontal(): return mixed.reshape(members, bands, nodes).astype(jnp.bfloat16)]
    reduce_scatter x2 -> x0, waiting for transfers between devices: 63.8 us -> none  [member_total(): lax.psum_scatter(local_sum, 'mem', scatter_dimension=0, tiled=True)]
    dot_general x18 -> x0, matrix products: 57.6 us -> none  [the longest x3 19.8 us: horizontal(): jnp.einsum('rikj,iakj->rika', picked, shaped, preferred_element_type=jnp....]
  transfers between devices with their start and end apart: 6 -> 2, of which waited for: 5 -> 2; matrix products, arithmetic and copies ran while one was open for 2% -> 2% of each run, Pallas kernels for 0% -> 0%
where the time goes in v1:
time: 254 us; the launch traced here: 253 us
  Pallas kernels  121 us (48%)
  blocking collectives  78.6 us (31%)
  waiting for transfers between devices  16.9 us (7%)
  local copies, waits for them, and re-layouts  11.6 us (5%)
  other arithmetic  10.5 us (4%)
  starting transfers between devices  8.69 us (3%)
  between operations  5.79 us (2%)
    pallas_call x2, Pallas kernels, gram(): resid, mixed = middle(cols, moved, mats)  63.1 us
    all_to_all x4, blocking collectives, everywhere(): x = jnp.sum(lax.all_to_all(sent, axis, 0, 0, tiled=True), axis=0)  42.5 us
    pallas_call x2, Pallas kernels, gram(): sent = adjoint(info, level, first, second, weight, errors, pert, vertical)  28.8 us
    pallas_call x2, Pallas kernels, gram(): forward(info, level, first, second, weight, columns, pert, vertical)  28.7 us
    all_to_all x2, blocking collectives, gram(): lax.all_to_all(mixed, 'col', 0, 0, tiled=True).reshape(levels, ncols)  23.5 us
    all_to_all x1, waiting for transfers between devices, per_device(): lax.all_to_all(total.reshape(nmem, levels // nmem, ncols), 'mem', 0, 0, t...  14.3 us
    all_to_all x1, blocking collectives, gram(): moved = lax.all_to_all(sent, 'col', 0, 0, tiled=True)  12.6 us
    all_to_all x1, starting transfers between devices, gram(): moved = lax.all_to_all(sent, 'col', 0, 0, tiled=True)  5.19 us
  transfers between devices with their start and end apart: 2, of which 2 were waited for; matrix products, arithmetic and copies ran while one was open for 2% of the time, Pallas kernels for 0%

profile of v1, /device:TPU:0, one launch (start us, length us, event | category | flops | bytes accessed | tf_op | source)
XLA Modules:
  0.0 252.8 jit_solution(682291115794036780)
XLA Ops:
  0.6 0.0 copy-start.1
  0.6 1.5 reshape.44.level_ref
  2.2 1.4 reshape.45.weight_ref
  3.5 0.8 reshape.47
  4.3 0.8 reshape.48
  5.1 1.1 slice_reduce_fusion
  6.1 0.6 reshape_squeeze.7.n2_ref
  6.7 0.6 reshape_squeeze.6.n1_ref
  7.4 0.6 pad_add_fusion.node_ref
  8.0 0.6 mul.106.err_ref
  8.6 14.4 %adjoint.2 = bf16[4,32,2048]{2,1,0:T(8,128)(2,1)} custom-call(s32[2]{0:T(128)} %pad_add_fusion.node_ref, s32[16,512]{1,0:T(8,128)} %reshape.44.level_ref, s32[16,512]{1,0:T(8,128)} %reshape_squeeze.6.n1_ref, s32[16,512]{1,0:T(8,128)} %reshape_squeeze.7.n2_ref, f32[16,512]{1,0:T(8,128)} %reshape.45.weight_ref, f32[16,512]{1,0:T(8,128)} %mul.106.err_ref, ...), custom_call_target="tpu_custom_call" | custom-call | tf_op jit(solution)/shard_map/adjoint/pallas_call | solution.py:265
  23.0 5.2 %all-to-all-start = ((bf16[4,32,2048]{2,1,0:T(8,128)(2,1)}), bf16[4,32,2048]{2,1,0:T(8,128)(2,1)S(1)}, u32[]{:S(2)}, u32[]{:S(2)}) async-start(bf16[4,32,2048]{2,1,0:T(8,128)(2,1)} %adjoint.2), calls=%async_computation | async-start | bytes 1048576 | tf_op jit(solution)/shard_map/all_to_all | solution.py:266
  28.2 0.7 broadcast_in_dim.12
  28.9 0.1 copy.18
  29.0 0.8 copy.17
  29.8 0.7 reshape.46.cols_ref
  30.5 0.0 copy-done.1
  30.5 0.6 multiply_convert_fusion
  31.1 0.2 slice_bitcast_fusion.1
  31.3 2.3 fusion.2.mats_ref
  33.6 2.6 %all-to-all-done.moved_ref = bf16[4,32,2048]{2,1,0:T(8,128)(2,1)S(1)} async-done(((bf16[4,32,2048]{2,1,0:T(8,128)(2,1)}), bf16[4,32,2048]{2,1,0:T(8,128)(2,1)S(1)}, u32[]{:S(2)}, u32[]{:S(2)}) %all-to-all-start) | async-done | bytes 524320 | tf_op jit(solution)/shard_map/all_to_all | solution.py:266
  36.2 0.8 copy-done
  37.0 31.5 %horizontal.2 = (f32[32,8192]{1,0:T(8,128)}, bf16[4,32,2048]{2,1,0:T(8,128)(2,1)}) custom-call(s32[256]{0:T(256)} %reshape.46.cols_ref, bf16[4,32,2048]{2,1,0:T(8,128)(2,1)} %copy-done, bf16[64,128,256]{2,1,0:T(8,128)(2,1)} %fusion.2.mats_ref), custom_call_target="tpu_custom_call" | custom-call | tf_op jit(solution)/shard_map/horizontal/pallas_call | solution.py:267
  68.6 11.9 %all_to_all.45 = bf16[4,32,2048]{2,1,0:T(8,128)(2,1)} all-to-all(bf16[4,32,2048]{2,1,0:T(8,128)(2,1)} %get-tuple-element.10), channel_id=1, replica_groups=mesh['mem'=8,'col'=4] {'col'}, dimensions={0} | all-to-all | bytes 1048576 | tf_op jit(solution)/shard_map/all_to_all | solution.py:268
  80.5 14.4 %forward.2 = (f32[128,2048]{1,0:T(8,128)}, f32[16,512]{1,0:T(8,128)}) custom-call(s32[2]{0:T(128)} %pad_add_fusion.node_ref, s32[16,512]{1,0:T(8,128)} %reshape.44.level_ref, s32[16,512]{1,0:T(8,128)} %reshape_squeeze.6.n1_ref, s32[16,512]{1,0:T(8,128)} %reshape_squeeze.7.n2_ref, f32[16,512]{1,0:T(8,128)} %reshape.45.weight_ref, bf16[128,2048]{1,0:T(8,128)(2,1)} %bitcast.27, ...), custom_call_target="tpu_custom_call" | custom-call | tf_op jit(solution)/shard_map/forward/pallas_call | solution.py:269
  94.8 0.8 broadcast_in_dim.13
  95.6 7.4 %all_to_all.46 = f32[4,16,512]{2,1,0:T(8,128)S(1)} all-to-all(f32[4,16,512]{2,1,0:T(8,128)S(1)} %broadcast_in_dim.13), channel_id=1, replica_groups=mesh['mem'=8,'col'=4] {'col'}, dimensions={0} | all-to-all | bytes 262144 | tf_op jit(solution)/shard_map/all_to_all | solution.py:181
  103.0 14.4 %all_to_all.47 = f32[8,16,512]{2,1,0:T(8,128)S(1)} all-to-all(f32[8,16,512]{2,1,0:T(8,128)S(1)} %broadcast_in_dim.14), channel_id=1, replica_groups=mesh['mem'=8,'col'=4] {'mem'}, dimensions={0} | all-to-all | bytes 524288 | tf_op jit(solution)/shard_map/all_to_all | solution.py:181
  117.5 0.0 copy-done.5
  117.5 0.6 multiply_reduce_fusion.2
  119.9 0.6 multiply_subtract_fusion.err_ref
  120.5 14.4 %adjoint.3 = bf16[4,32,2048]{2,1,0:T(8,128)(2,1)} custom-call(s32[2]{0:T(128)} %pad_add_fusion.node_ref, s32[16,512]{1,0:T(8,128)} %reshape.44.level_ref, s32[16,512]{1,0:T(8,128)} %reshape_squeeze.6.n1_ref, s32[16,512]{1,0:T(8,128)} %reshape_squeeze.7.n2_ref, f32[16,512]{1,0:T(8,128)} %reshape.45.weight_ref, f32[16,512]{1,0:T(8,128)} %multiply_subtract_fusion.err_ref, ...), custom_call_target="tpu_custom_call" | custom-call | tf_op jit(solution)/shard_map/adjoint/pallas_call | solution.py:265
  134.9 12.6 %all_to_all.48.moved_ref = bf16[4,32,2048]{2,1,0:T(8,128)(2,1)} all-to-all(bf16[4,32,2048]{2,1,0:T(8,128)(2,1)} %adjoint.3), channel_id=1, replica_groups=mesh['mem'=8,'col'=4] {'col'}, dimensions={0} | all-to-all | bytes 1048576 | tf_op jit(solution)/shard_map/all_to_all | solution.py:266
  147.5 31.6 %horizontal.3 = (f32[32,8192]{1,0:T(8,128)}, bf16[4,32,2048]{2,1,0:T(8,128)(2,1)}) custom-call(s32[256]{0:T(256)} %reshape.46.cols_ref, bf16[4,32,2048]{2,1,0:T(8,128)(2,1)} %all_to_all.48.moved_ref, bf16[64,128,256]{2,1,0:T(8,128)(2,1)} %fusion.2.mats_ref), custom_call_target="tpu_custom_call" | custom-call | tf_op jit(solution)/shard_map/horizontal/pallas_call | solution.py:267
  179.1 11.6 %all_to_all.49 = bf16[4,32,2048]{2,1,0:T(8,128)(2,1)} all-to-all(bf16[4,32,2048]{2,1,0:T(8,128)(2,1)} %get-tuple-element.12), channel_id=1, replica_groups=mesh['mem'=8,'col'=4] {'col'}, dimensions={0} | all-to-all | bytes 1048576 | tf_op jit(solution)/shard_map/all_to_all | solution.py:268
  190.7 14.4 %forward.3 = (f32[128,2048]{1,0:T(8,128)}, f32[16,512]{1,0:T(8,128)}) custom-call(s32[2]{0:T(128)} %pad_add_fusion.node_ref, s32[16,512]{1,0:T(8,128)} %reshape.44.level_ref, s32[16,512]{1,0:T(8,128)} %reshape_squeeze.6.n1_ref, s32[16,512]{1,0:T(8,128)} %reshape_squeeze.7.n2_ref, f32[16,512]{1,0:T(8,128)} %reshape.45.weight_ref, bf16[128,2048]{1,0:T(8,128)(2,1)} %bitcast.26, ...), custom_call_target="tpu_custom_call" | custom-call | tf_op jit(solution)/shard_map/forward/pallas_call | solution.py:269
  205.0 0.8 broadcast_in_dim.15
  205.8 7.4 %all_to_all.50 = f32[4,16,512]{2,1,0:T(8,128)S(1)} all-to-all(f32[4,16,512]{2,1,0:T(8,128)S(1)} %broadcast_in_dim.15), channel_id=1, replica_groups=mesh['mem'=8,'col'=4] {'col'}, dimensions={0} | all-to-all | bytes 262144 | tf_op jit(solution)/shard_map/all_to_all | solution.py:181
  213.3 13.3 %all_to_all.51 = f32[8,16,512]{2,1,0:T(8,128)S(1)} all-to-all(f32[8,16,512]{2,1,0:T(8,128)S(1)} %broadcast_in_dim.16), channel_id=1, replica_groups=mesh['mem'=8,'col'=4] {'mem'}, dimensions={0} | all-to-all | bytes 524288 | tf_op jit(solution)/shard_map/all_to_all | solution.py:181
  226.6 0.6 multiply_reduce_fusion.1
  228.4 0.7 fusion.4
  231.1 2.2 add_convert_fusion
  233.3 3.5 %all-to-all-start.8 = ((bf16[8,16,2048]{2,1,0:T(8,128)(2,1)}), bf16[8,16,2048]{2,1,0:T(8,128)(2,1)S(1)}, u32[]{:S(2)}, u32[]{:S(2)}) async-start(bf16[8,16,2048]{2,1,0:T(8,128)(2,1)} %bitcast.9), calls=%async_computation.8 | async-start | bytes 1048576 | tf_op jit(solution)/shard_map/all_to_all | solution.py:294
  236.8 0.0 copy-done.2
  236.8 0.0 copy-done.4
  236.8 0.9 fusion.3
  237.7 14.3 %all-to-all-done.8 = bf16[8,16,2048]{2,1,0:T(8,128)(2,1)S(1)} async-done(((bf16[8,16,2048]{2,1,0:T(8,128)(2,1)}), bf16[8,16,2048]{2,1,0:T(8,128)(2,1)S(1)}, u32[]{:S(2)}, u32[]{:S(2)}) %all-to-all-start.8) | async-done | bytes 524320 | tf_op jit(solution)/shard_map/all_to_all | solution.py:294
  252.0 0.7 convert_reduce_fusion
  (18 shorter events, 0.1 us)
Async XLA Ops:
  0.6 29.9 %copy-start.1 = (bf16[128,64,128]{2,1,0:T(8,128)(2,1)S(1)}, bf16[128,64,128]{2,1,0:T(8,128)(2,1)}, u32[]{:S(2)}) copy-start(bf16[128,64,128]{2,1,0:T(8,128)(2,1)} %param.12) | copy-start | bytes 6291460
  23.0 13.2 %all-to-all-start = ((bf16[4,32,2048]{2,1,0:T(8,128)(2,1)}), bf16[4,32,2048]{2,1,0:T(8,128)(2,1)S(1)}, u32[]{:S(2)}, u32[]{:S(2)}) async-start(bf16[4,32,2048]{2,1,0:T(8,128)(2,1)} %adjoint.2), calls=%async_computation | async-start | bytes 1048576 | tf_op jit(solution)/shard_map/all_to_all | solution.py:266
  33.6 83.9 %copy-start.5 = (f32[8192]{0:T(1024)S(1)}, f32[8192]{0:T(1024)}, u32[]{:S(2)}) copy-start(f32[8192]{0:T(1024)} %param.19) | copy-start | bytes 98308
  33.6 83.9 %copy-start.7 = (f32[8192]{0:T(1024)S(1)}, f32[8192]{0:T(1024)}, u32[]{:S(2)}) copy-start(f32[8192]{0:T(1024)} %param.18) | copy-start | bytes 98308
  33.6 86.3 %copy-start.6 = (f32[16,512]{1,0:T(8,128)S(1)}, f32[16,512]{1,0:T(8,128)}, u32[]{:S(2)}) copy-start(f32[16,512]{1,0:T(8,128)} %mul.106.err_ref) | copy-start | bytes 98308
  36.2 0.8 copy-start
  147.5 83.6 %copy-start.3 = (f32[128,2048]{1,0:T(8,128)S(1)}, f32[128,2048]{1,0:T(8,128)}, u32[]{:S(2)}) copy-start(f32[128,2048]{1,0:T(8,128)} %get-tuple-element.16) | copy-start | bytes 3145732
  179.1 57.7 %copy-start.2 = (f32[32,8192]{1,0:T(8,128)S(1)}, f32[32,8192]{1,0:T(8,128)}, u32[]{:S(2)}) copy-start(f32[32,8192]{1,0:T(8,128)} %get-tuple-element.14) | copy-start | bytes 3145732
  179.1 57.7 %copy-start.4 = (f32[32,8192]{1,0:T(8,128)S(1)}, f32[32,8192]{1,0:T(8,128)}, u32[]{:S(2)}) copy-start(f32[32,8192]{1,0:T(8,128)} %get-tuple-element.15) | copy-start | bytes 3145732
  233.3 18.8 %all-to-all-start.8 = ((bf16[8,16,2048]{2,1,0:T(8,128)(2,1)}), bf16[8,16,2048]{2,1,0:T(8,128)(2,1)S(1)}, u32[]{:S(2)}, u32[]{:S(2)}) async-start(bf16[8,16,2048]{2,1,0:T(8,128)(2,1)} %bitcast.9), calls=%async_computation.8 | async-start | bytes 1048576 | tf_op jit(solution)/shard_map/all_to_all | solution.py:294

commit v2 on v1

v2 whole, which is shorter than its diff:
```python
import math

import jax
import jax.numpy as jnp
from jax import lax
from jax.experimental import pallas as pl
from jax.experimental.pallas import tpu as pltpu
from jax.sharding import PartitionSpec as P

ITERS = 2
LANES = 128
WIDE = 512
CHUNK = 512
HALF = 256
UNROLL = 8


def one_hot(keys, rows, values):
    n = keys.shape[1]
    parts = []
    for low in range(0, rows, HALF):
        size = min(HALF, rows - low)
        row = lax.broadcasted_iota(jnp.int32, (size, n), 0).astype(jnp.float32).astype(jnp.bfloat16)
        key = jnp.broadcast_to((keys - low).astype(jnp.float32).astype(jnp.bfloat16), (size, n))
        val = jnp.broadcast_to(values, (size, n))
        parts.append(jnp.where(row == key, val, jnp.zeros_like(val)))
    return parts[0] if len(parts) == 1 else jnp.concatenate(parts, axis=0)


def places(level, node, node_lo, levels, ncols):
    wide = min(WIDE, ncols)
    local = node - node_lo
    inside = (local >= 0) & (local < ncols)
    row = jnp.where(inside, (local // wide) * levels + level, -1024)
    lane = jnp.where(inside, local % wide, -1024)
    return row, lane


def adjoint_kernel(level_ref, nodes_ref, weight_ref, err_ref, pert_ref, vert_ref, out_ref, total):
    levels, ncols = pert_ref.shape
    bands = out_ref.shape[1]
    members = lax.axis_size("mem")
    wide = min(WIDE, ncols)
    chunks = ncols // wide
    node_lo = lax.axis_index("col") * ncols
    total[...] = jnp.zeros_like(total)

    def step(c, carry):
        span = pl.ds(pl.multiple_of(c * CHUNK, CHUNK), CHUNK)
        level = level_ref[:, span]
        weight = weight_ref[:, span]
        err = err_ref[:, span]
        rows, lanes = [], []
        for which, w in ((0, weight), (1, 1.0 - weight)):
            node = nodes_ref[which : which + 1, span]
            row, lane = places(level, node, node_lo, levels, ncols)
            rows.append(one_hot(row, chunks * levels, (w * err).astype(jnp.bfloat16)))
            lanes.append(one_hot(lane, wide, jnp.ones_like(w).astype(jnp.bfloat16)))
        total[...] += lax.dot_general(
            jnp.concatenate(rows, axis=1),
            jnp.concatenate(lanes, axis=1),
            (((1,), (1,)), ((), ())),
            preferred_element_type=jnp.float32,
        )
        return carry

    lax.fori_loop(0, level_ref.shape[1] // CHUNK, step, 0)
    scale_inv = 1.0 / math.sqrt(members)
    for c in range(chunks):
        part = slice(c * wide, (c + 1) * wide)
        grad = total[c * levels : (c + 1) * levels, :]
        scaled = (pert_ref[:, part].astype(jnp.float32) * grad * scale_inv).astype(jnp.bfloat16)
        turned = scaled.astype(jnp.float32) + lax.dot_general(
            vert_ref[...], scaled, (((0,), (0,)), ((), ())), preferred_element_type=jnp.float32
        )
        for b in range(out_ref.shape[0]):
            out_ref[b, :, part] = turned[b * bands : (b + 1) * bands, :].astype(jnp.bfloat16)


def horizontal_kernel(cols_ref, moved_ref, mats_ref, resid_ref, mixed_ref, terms, first, second, picked):
    parts, bands, ncols = moved_ref.shape
    pairs = mats_ref.shape[0]
    per_part = ncols // LANES
    half = LANES // 2
    lane = lax.broadcasted_iota(jnp.int32, (bands, LANES), 1)
    low = lane < half
    low16 = lane.astype(jnp.float32).astype(jnp.bfloat16) < half
    sums = (first, second)
    for s in sums:
        s[...] = jnp.zeros_like(s)

    def tile_of(p):
        at = pl.multiple_of((p % per_part) * LANES, LANES)
        return p // per_part, pl.ds(at, LANES)

    def product(p, carry):
        part, lanes = tile_of(p)
        both = jnp.dot(moved_ref[part, :, lanes], mats_ref[p], preferred_element_type=jnp.float32)
        terms[2 * p] = both[:, :LANES]
        terms[2 * p + 1] = both[:, LANES:]
        return carry

    lax.fori_loop(0, pairs, product, 0, unroll=UNROLL)

    def scatter(i, carry):
        term = terms[i]
        for k in range(2):
            col = cols_ref[k, i]
            sums[k][(col & 1) ^ k, col >> 1] += term
        return carry

    lax.fori_loop(0, 2 * pairs, scatter, 0, unroll=UNROLL)

    def join(p, carry):
        part, lanes = tile_of(p)
        here = jnp.where(low, first[0, p], second[0, p])
        there = jnp.where(low, first[1, p], second[1, p])
        resid = moved_ref[part, :, lanes].astype(jnp.float32) + here + pltpu.roll(there, half, 1)
        resid_ref[:, pl.ds(pl.multiple_of(p * LANES, LANES), LANES)] = resid
        picked[0, p] = resid.astype(jnp.bfloat16)
        picked[1, p] = pltpu.roll(resid, half, 1).astype(jnp.bfloat16)
        return carry

    lax.fori_loop(0, pairs, join, 0, unroll=UNROLL)

    def gather(p, carry):
        part, lanes = tile_of(p)
        sources = []
        for q in range(2):
            one = cols_ref[0, 2 * p + q]
            two = cols_ref[1, 2 * p + q]
            sources.append(jnp.where(low16, picked[one & 1, one >> 1], picked[(two & 1) ^ 1, two >> 1]))
        both = lax.dot_general(
            jnp.concatenate(sources, axis=1),
            mats_ref[p],
            (((1,), (1,)), ((), ())),
            preferred_element_type=jnp.float32,
        )
        mixed_ref[part, :, lanes] = (picked[0, p].astype(jnp.float32) + both).astype(jnp.bfloat16)
        return carry

    lax.fori_loop(0, pairs, gather, 0, unroll=UNROLL)


def forward_kernel(level_ref, nodes_ref, weight_ref, mixed_ref, pert_ref, vert_ref, field_ref, obs_ref, table):
    levels, ncols = pert_ref.shape
    members = lax.axis_size("mem")
    wide = min(WIDE, ncols)
    chunks = ncols // wide
    node_lo = lax.axis_index("col") * ncols
    core = lax.axis_index("mem") % 2
    scale_inv = 1.0 / math.sqrt(members)
    for c in range(chunks):
        part = slice(c * wide, (c + 1) * wide)
        mixed = mixed_ref[:, part]
        localized = mixed.astype(jnp.float32) + jnp.dot(
            vert_ref[...], mixed, preferred_element_type=jnp.float32
        )
        field = (pert_ref[:, part].astype(jnp.float32) * localized * scale_inv).astype(jnp.bfloat16)
        table[c * levels : (c + 1) * levels, :] = field
        if len(field_ref.shape) == 2:
            field_ref[:, part] = field
        else:
            _, chips, rows, _ = field_ref.shape
            for s in range(2 * chips):
                field_ref[(s % 2) ^ core, s // 2, :, part] = field[s * rows : (s + 1) * rows, :]

    def step(c, carry):
        span = pl.ds(pl.multiple_of(c * CHUNK, CHUNK), CHUNK)
        level = level_ref[:, span]
        weight = weight_ref[:, span]
        result = jnp.zeros(weight.shape, jnp.float32)
        for which, w in ((0, weight), (1, 1.0 - weight)):
            node = nodes_ref[which : which + 1, span]
            row, lane = places(level, node, node_lo, levels, ncols)
            hot = one_hot(lane, wide, jnp.ones_like(w).astype(jnp.bfloat16))
            lines = jnp.dot(table[...], hot, preferred_element_type=jnp.float32)
            number = lax.broadcasted_iota(jnp.int32, lines.shape, 0)
            kept = jnp.where(number == row, lines, 0.0)
            result = result + w * jnp.sum(kept, axis=0, keepdims=True)
        obs_ref[:, span] = result
        return carry

    lax.fori_loop(0, level_ref.shape[1] // CHUNK, step, 0)


def swap(x, axis, offset):
    n = lax.axis_size(axis)
    return lax.ppermute(x, axis, [(i, i ^ offset) for i in range(n)])


def total_over(x, axis, offsets):
    return sum([swap(x, axis, k) for k in offsets], x)


def everywhere(x):
    x = total_over(x, "mem", (1,))
    x = total_over(x, "col", range(1, lax.axis_size("col")))
    return total_over(x, "mem", range(2, lax.axis_size("mem"), 2))


def scatter_members(field):
    if field.ndim == 2:
        nmem = lax.axis_size("mem")
        field = field.reshape(nmem, field.shape[0] // nmem, field.shape[1])
        pieces = lax.all_to_all(field, "mem", 0, 0, tiled=True)
        return jnp.sum(pieces.astype(jnp.float32), axis=0)
    mine = (field[0].astype(jnp.float32) + swap(field[1], "mem", 1).astype(jnp.float32)).astype(jnp.bfloat16)
    chips = mine.shape[0]
    chip = lax.axis_index("mem") // 2
    total = lax.dynamic_index_in_dim(mine, chip, 0, keepdims=False).astype(jnp.float32)
    for k in range(1, chips):
        piece = lax.dynamic_index_in_dim(mine, chip ^ k, 0, keepdims=False)
        total = total + swap(piece, "mem", 2 * k).astype(jnp.float32)
    return total


def per_device(
    perturbations,
    vertical,
    blocks,
    block_scale,
    block_cols,
    obs_level,
    obs_nodes,
    obs_weight,
    obs_value,
    obs_precision,
):
    local_members, levels, ncols = perturbations.shape
    assert local_members == 1
    nblocks, width, depth = blocks.shape
    assert 2 * width == LANES and depth == LANES
    ncol = lax.axis_size("col")
    nmem = lax.axis_size("mem")
    bands = levels // ncol
    pairs = nblocks // 2
    nobs = obs_level.shape[0]
    pert = perturbations[0]

    scaled = (blocks.astype(jnp.float32) * jnp.repeat(block_scale, width, axis=1)[:, None, :]).astype(
        jnp.bfloat16
    ).reshape(pairs, 2, width, depth)
    mats = jnp.concatenate(
        [
            jnp.pad(scaled[:, 0], ((0, 0), (0, 0), (0, depth))),
            jnp.pad(scaled[:, 1], ((0, 0), (0, 0), (depth, 0))),
        ],
        axis=1,
    )
    cols = block_cols.T
    nodes = obs_nodes.T
    level, weight, value, precision = (
        a.reshape(1, nobs) for a in (obs_level, obs_weight, obs_value, obs_precision)
    )

    vmem = pl.BlockSpec(memory_space=pltpu.VMEM)
    smem = pl.BlockSpec(memory_space=pltpu.SMEM)
    wide = min(WIDE, ncols)
    slices = levels // nmem

    adjoint = pl.pallas_call(
        adjoint_kernel,
        out_shape=jax.ShapeDtypeStruct((ncol, bands, ncols), jnp.bfloat16),
        in_specs=[vmem] * 6,
        out_specs=vmem,
        scratch_shapes=[pltpu.VMEM((ncols // wide * levels, wide), jnp.float32)],
        name="adjoint",
    )
    middle = pl.pallas_call(
        horizontal_kernel,
        out_shape=(
            jax.ShapeDtypeStruct((bands, nblocks * width), jnp.float32),
            jax.ShapeDtypeStruct((ncol, bands, ncols), jnp.bfloat16),
        ),
        in_specs=[smem] + [vmem] * 2,
        out_specs=(vmem, vmem),
        scratch_shapes=[
            pltpu.VMEM((2 * pairs, bands, LANES), jnp.float32),
            pltpu.VMEM((2, pairs, bands, LANES), jnp.float32),
            pltpu.VMEM((2, pairs, bands, LANES), jnp.float32),
            pltpu.VMEM((2, pairs, bands, LANES), jnp.bfloat16),
        ],
        name="horizontal",
    )
    field_shape = (2, nmem // 2, slices, ncols) if slices % 16 == 0 else (levels, ncols)
    forward = pl.pallas_call(
        forward_kernel,
        out_shape=(
            jax.ShapeDtypeStruct(field_shape, jnp.bfloat16),
            jax.ShapeDtypeStruct((1, nobs), jnp.float32),
        ),
        in_specs=[vmem] * 6,
        out_specs=(vmem, vmem),
        scratch_shapes=[pltpu.VMEM((ncols // wide * levels, wide), jnp.bfloat16)],
        name="forward",
    )

    def gram(errors):
        sent = adjoint(level, nodes, weight, errors, pert, vertical)
        moved = lax.all_to_all(sent, "col", 0, 0, tiled=True)
        resid, mixed = middle(cols, moved, mats)
        columns = lax.all_to_all(mixed, "col", 0, 0, tiled=True).reshape(levels, ncols)
        field, partial = forward(level, nodes, weight, columns, pert, vertical)
        return resid, scatter_members(field), everywhere(partial)

    errors = precision * value
    fields, resids = [], []
    shares = []
    for step in range(ITERS):
        resid, field, seen = gram(errors)
        resids.append(resid)
        fields.append(field)
        norm_next = jnp.sum(errors * seen)
        if step == 0:
            guide, image = errors, seen
            mix = [jnp.float32(1.0)]
        else:
            beta = norm_next / norm_now
            guide, image = errors + beta * guide, seen + beta * image
            mix = [beta * m for m in mix] + [jnp.float32(1.0)]
        norm_now = norm_next
        along = jnp.sum(guide * image) + jnp.sum(precision * image * image)
        alpha = norm_now / along
        shares = [s + alpha * m for s, m in zip(shares + [jnp.float32(0.0)], mix)]
        errors = errors - alpha * (guide + precision * image)
    state = sum(c * r for c, r in zip(shares, resids))
    increment = sum(c * f for c, f in zip(shares, fields))
    return (state.astype(jnp.bfloat16)[None], increment)


def solution(mesh):
    in_specs = (P("mem", None, "col"), P(), P(), P(), P(), P(), P(), P(), P(), P())
    out_specs = (P("mem", "col", None), P("mem", "col"))
    return jax.shard_map(
        per_device, mesh=mesh, in_specs=in_specs, out_specs=out_specs, check_vma=False
    )
```

time: 254 us -> 181 us (0.71)
  blocking collectives: 78.6 us -> 23.2 us
  Pallas kernels: 121 us -> 77.2 us
  starting transfers between devices: 8.69 us -> 32.8 us
  local copies, waits for them, and re-layouts: 11.6 us -> 4.28 us
  waiting for transfers between devices: 16.9 us -> 24.1 us
  other arithmetic: 10.5 us -> 13.2 us
    pallas_call x2, Pallas kernels: 63.1 us -> 19.8 us  [gram(): resid, mixed = middle(cols, moved, mats)]
    all_to_all x4 -> x0, blocking collectives: 42.5 us -> none  [everywhere(): x = jnp.sum(lax.all_to_all(sent, axis, 0, 0, tiled=True), axis=0)]
    ppermute x0 -> x22, starting transfers between devices: none -> 24 us  [swap(): return lax.ppermute(x, axis, [(i, i ^ offset) for i in range(n)])]
    ppermute x0 -> x22, waiting for transfers between devices: none -> 15.7 us  [swap(): return lax.ppermute(x, axis, [(i, i ^ offset) for i in range(n)])]
    all_to_all x2 -> x1, blocking collectives: 23.5 us -> 11.9 us  [gram(): lax.all_to_all(mixed, 'col', 0, 0, tiled=True).reshape(levels, ncols)]
    all_to_all x1, waiting for transfers between devices: 14.3 us -> 5.8 us  [gram(): lax.all_to_all(mixed, 'col', 0, 0, tiled=True).reshape(levels, ncols)]
    reshape x5 -> x0, local copies, waits for them, and re-layouts: 5.15 us -> none  [the longest x4 4.41 us: per_device(): a.reshape(rows, CHUNK)]
  transfers between devices with their start and end apart: 2 -> 24, of which waited for: 2 -> 13; matrix products, arithmetic and copies ran while one was open for 2% -> 6% of each run, Pallas kernels for 0% -> 8%
where the time goes in v2:
time: 181 us
  Pallas kernels  77.2 us (43%)
  starting transfers between devices  32.8 us (18%)
  waiting for transfers between devices  24.1 us (13%)
  blocking collectives  23.2 us (13%)
  other arithmetic  13.2 us (7%)
  between operations  5.83 us (3%)
  local copies, waits for them, and re-layouts  4.28 us (2%)
    pallas_call x2, Pallas kernels, gram(): sent = adjoint(level, nodes, weight, errors, pert, vertical)  28.9 us
    pallas_call x2, Pallas kernels, gram(): field, partial = forward(level, nodes, weight, columns, pert, vertical)  28.4 us
    ppermute x22, starting transfers between devices, swap(): return lax.ppermute(x, axis, [(i, i ^ offset) for i in range(n)])  24 us
    pallas_call x2, Pallas kernels, gram(): resid, mixed = middle(cols, moved, mats)  19.8 us
    ppermute x22, waiting for transfers between devices, swap(): return lax.ppermute(x, axis, [(i, i ^ offset) for i in range(n)])  15.7 us
    all_to_all x1, blocking collectives, gram(): lax.all_to_all(mixed, 'col', 0, 0, tiled=True).reshape(levels, ncols)  11.9 us
    all_to_all x1, blocking collectives, gram(): moved = lax.all_to_all(sent, 'col', 0, 0, tiled=True)  11.3 us
    all_to_all x1, waiting for transfers between devices, gram(): lax.all_to_all(mixed, 'col', 0, 0, tiled=True).reshape(levels, ncols)  5.8 us
  transfers between devices with their start and end apart: 24, of which 13 were waited for; matrix products, arithmetic and copies ran while one was open for 6% of the time, Pallas kernels for 8%

profile of v2, /device:TPU:0, one launch (start us, length us, event | category | flops | bytes accessed | tf_op | source)
XLA Modules:
  0.0 180.6 jit_solution(13980541929450022167)
XLA Ops:
  0.6 1.4 mul.86
  2.0 14.5 %adjoint.2 = bf16[4,32,2048]{2,1,0:T(8,128)(2,1)} custom-call(s32[1,8192]{1,0:T(1,128)} %bitcast.64, s32[2,8192]{1,0:T(2,128)} %bitcast.57, f32[1,8192]{1,0:T(1,128)} %bitcast.68, f32[1,8192]{1,0:T(1,128)} %bitcast.61, bf16[128,2048]{1,0:T(8,128)(2,1)} %bitcast.50, bf16[128,128]{1,0:T(8,128)(2,1)} %vert_ref.7), custom_call_target="tpu_custom_call" | custom-call | tf_op jit(solution)/shard_map/adjoint/pallas_call | solution.py:300
  16.5 5.2 %all-to-all-start = ((bf16[4,32,2048]{2,1,0:T(8,128)(2,1)}), bf16[4,32,2048]{2,1,0:T(8,128)(2,1)S(1)}, u32[]{:S(2)}, u32[]{:S(2)}) async-start(bf16[4,32,2048]{2,1,0:T(8,128)(2,1)} %adjoint.2), calls=%async_computation | async-start | bytes 1048576 | tf_op jit(solution)/shard_map/all_to_all | solution.py:301
  21.7 0.7 broadcast_in_dim.6
  22.5 2.2 %multiply_convert_fusion = bf16[128,64,128]{2,1,0:T(8,128)(2,1)S(1)} fusion(bf16[128,64,128]{2,1,0:T(8,128)(2,1)} %param.12, f32[128,128]{1,0:T(8,128)S(1)} %copy.13), kind=kLoop, calls=%fused_computation.5 | loop fusion | flops 3145728 | bytes 4259840 | tf_op jit(solution)/shard_map/convert_element_type | solution.py:241
  24.8 2.3 %fusion.2.mats_ref = bf16[64,128,256]{2,1,0:T(8,128)(2,1)} fusion(bf16[64,64,128]{2,1,0:T(8,128)(2,1)S(1)} %get-tuple-element.26, bf16[64,64,128]{2,1,0:T(8,128)(2,1)S(1)} %get-tuple-element.25), kind=kLoop, calls=%fused_computation.4 | loop fusion | flops 16777216 | bytes 6291456 | tf_op jit(solution)/shard_map/concatenate | solution.py:244
  27.1 2.6 %all-to-all-done.moved_ref = bf16[4,32,2048]{2,1,0:T(8,128)(2,1)S(1)} async-done(((bf16[4,32,2048]{2,1,0:T(8,128)(2,1)}), bf16[4,32,2048]{2,1,0:T(8,128)(2,1)S(1)}, u32[]{:S(2)}, u32[]{:S(2)}) %all-to-all-start) | async-done | bytes 524320 | tf_op jit(solution)/shard_map/all_to_all | solution.py:301
  29.7 0.8 copy-done
  30.5 9.9 %horizontal.2 = (f32[32,8192]{1,0:T(8,128)}, bf16[4,32,2048]{2,1,0:T(8,128)(2,1)}) custom-call(s32[2,128]{1,0:T(2,128)} %bitcast.77, bf16[4,32,2048]{2,1,0:T(8,128)(2,1)} %copy-done, bf16[64,128,256]{2,1,0:T(8,128)(2,1)} %fusion.2.mats_ref), custom_call_target="tpu_custom_call" | custom-call | tf_op jit(solution)/shard_map/horizontal/pallas_call | solution.py:302
  40.4 11.9 %all_to_all.20 = bf16[4,32,2048]{2,1,0:T(8,128)(2,1)} all-to-all(bf16[4,32,2048]{2,1,0:T(8,128)(2,1)} %get-tuple-element.10), channel_id=1, replica_groups=mesh['mem'=8,'col'=4] {'col'}, dimensions={0} | all-to-all | bytes 1048576 | tf_op jit(solution)/shard_map/all_to_all | solution.py:303
  52.3 14.2 %forward.2 = (bf16[2,4,16,2048]{3,2,1,0:T(8,128)(2,1)}, f32[1,8192]{1,0:T(1,128)}) custom-call(s32[1,8192]{1,0:T(1,128)} %bitcast.65, s32[2,8192]{1,0:T(2,128)} %bitcast.58, f32[1,8192]{1,0:T(1,128)} %bitcast.69, bf16[128,2048]{1,0:T(8,128)(2,1)} %bitcast.56, bf16[128,2048]{1,0:T(8,128)(2,1)} %bitcast.51, bf16[128,128]{1,0:T(8,128)(2,1)} %vert_ref.7), custom_call_target="tpu_custom_call" | custom-call | tf_op jit(solution)/shard_map/forward/pallas_call | solution.py:304
  66.5 1.4 collective-permute-done
  67.9 0.8 add.112
  68.7 1.0 collective-permute-start.3
  69.7 1.5 collective-permute-start.2
  71.2 1.1 collective-permute-start.1
  72.3 1.6 collective-permute-done.3
  74.0 1.1 collective-permute-done.1
  75.1 3.7 %collective-permute-start.6 = (f32[1,8192]{1,0:T(1,128)S(1)}, f32[1,8192]{1,0:T(1,128)S(1)}, u32[]{:S(2)}, u32[]{:S(2)}) collective-permute-start(f32[1,8192]{1,0:T(1,128)S(1)} %add_add_fusion.3), channel_id=1, source_target_pairs={{0,24},{4,28},{8,16},{12,20},{16,8},{20,12},{24,0},{28,4},{1,25},{... | collective-permute-start | bytes 98312 | tf_op jit(solution)/shard_map/ppermute | solution.py:189
  78.8 0.8 collective-permute-start.4
  79.6 1.3 collective-permute-done.6
  80.9 2.7 %collective-permute-done.5 = f32[1,8192]{1,0:T(1,128)S(1)} collective-permute-done((f32[1,8192]{1,0:T(1,128)S(1)}, f32[1,8192]{1,0:T(1,128)S(1)}, u32[]{:S(2)}, u32[]{:S(2)}) %collective-permute-start.5) | collective-permute-done | bytes 32800 | tf_op jit(solution)/shard_map/ppermute | solution.py:189
  83.7 0.8 multiply_reduce_fusion.2
  87.0 14.5 %adjoint.3 = bf16[4,32,2048]{2,1,0:T(8,128)(2,1)} custom-call(s32[1,8192]{1,0:T(1,128)} %bitcast.66, s32[2,8192]{1,0:T(2,128)} %bitcast.59, f32[1,8192]{1,0:T(1,128)} %bitcast.70, f32[1,8192]{1,0:T(1,128)} %multiply_subtract_fusion.err_ref, bf16[128,2048]{1,0:T(8,128)(2,1)} %bitcast.52, bf16[128,128]{1,0:T(8,128)(2,1)} %vert_ref.7), custom_call_target="tpu_custom_call" | custom-call | tf_op jit(solution)/shard_map/adjoint/pallas_call | solution.py:300
  101.4 11.3 %all_to_all.21.moved_ref = bf16[4,32,2048]{2,1,0:T(8,128)(2,1)} all-to-all(bf16[4,32,2048]{2,1,0:T(8,128)(2,1)} %adjoint.3), channel_id=1, replica_groups=mesh['mem'=8,'col'=4] {'col'}, dimensions={0} | all-to-all | bytes 1048576 | tf_op jit(solution)/shard_map/all_to_all | solution.py:301
  112.8 9.9 %horizontal.3 = (f32[32,8192]{1,0:T(8,128)}, bf16[4,32,2048]{2,1,0:T(8,128)(2,1)}) custom-call(s32[2,128]{1,0:T(2,128)} %bitcast.78, bf16[4,32,2048]{2,1,0:T(8,128)(2,1)} %all_to_all.21.moved_ref, bf16[64,128,256]{2,1,0:T(8,128)(2,1)} %fusion.2.mats_ref), custom_call_target="tpu_custom_call" | custom-call | tf_op jit(solution)/shard_map/horizontal/pallas_call | solution.py:302
  122.7 3.6 %all-to-all-start.3 = ((bf16[4,32,2048]{2,1,0:T(8,128)(2,1)}), bf16[4,32,2048]{2,1,0:T(8,128)(2,1)S(1)}, u32[]{:S(2)}, u32[]{:S(2)}) async-start(bf16[4,32,2048]{2,1,0:T(8,128)(2,1)} %get-tuple-element.12), calls=%async_computation.3 | async-start | bytes 1048576 | tf_op jit(solution)/shard_map/all_to_all | solution.py:303
  126.3 0.7 slice_bitcast_fusion.3
  127.1 5.8 %all-to-all-done.3 = bf16[4,32,2048]{2,1,0:T(8,128)(2,1)S(1)} async-done(((bf16[4,32,2048]{2,1,0:T(8,128)(2,1)}), bf16[4,32,2048]{2,1,0:T(8,128)(2,1)S(1)}, u32[]{:S(2)}, u32[]{:S(2)}) %all-to-all-start.3) | async-done | bytes 524320 | tf_op jit(solution)/shard_map/all_to_all | solution.py:303
  132.9 0.8 copy-done.1
  133.7 14.2 %forward.3 = (bf16[2,4,16,2048]{3,2,1,0:T(8,128)(2,1)}, f32[1,8192]{1,0:T(1,128)}) custom-call(s32[1,8192]{1,0:T(1,128)} %bitcast.67, s32[2,8192]{1,0:T(2,128)} %bitcast.60, f32[1,8192]{1,0:T(1,128)} %bitcast.71, bf16[128,2048]{1,0:T(8,128)(2,1)} %bitcast.55, bf16[128,2048]{1,0:T(8,128)(2,1)} %bitcast.53, bf16[128,128]{1,0:T(8,128)(2,1)} %vert_ref.7), custom_call_target="tpu_custom_call" | custom-call | tf_op jit(solution)/shard_map/forward/pallas_call | solution.py:304
  147.9 1.3 collective-permute-done.7
  149.3 0.8 add.121
  150.1 1.5 collective-permute-start.10
  151.6 1.5 collective-permute-start.9
  153.7 3.5 %collective-permute-start.17 = (bf16[16,2048]{1,0:T(8,128)(2,1)S(1)}, bf16[16,2048]{1,0:T(8,128)(2,1)S(1)}, u32[]{:S(2)}, u32[]{:S(2)}) collective-permute-start(bf16[16,2048]{1,0:T(8,128)(2,1)S(1)} %get-tuple-element.28), channel_id=1, source_target_pairs={{0,24},{4,28},{8,16},{12,20},{16,8},{20,12},{24,0},{28,4},{1,25},{... | collective-permute-start | bytes 196616 | tf_op jit(solution)/shard_map/ppermute | solution.py:189
  157.3 1.3 collective-permute-start.13
  159.2 2.5 %collective-permute-start.11 = (f32[1,8192]{1,0:T(1,128)S(1)}, f32[1,8192]{1,0:T(1,128)S(1)}, u32[]{:S(2)}, u32[]{:S(2)}) collective-permute-start(f32[1,8192]{1,0:T(1,128)S(1)} %add_add_fusion.1), channel_id=1, source_target_pairs={{0,8},{4,12},{8,0},{12,4},{16,24},{20,28},{24,16},{28,20},{1,9},{5... | collective-permute-start | bytes 98312 | tf_op jit(solution)/shard_map/ppermute | solution.py:189
  161.7 1.0 slice_bitcast_fusion.2
  163.8 0.7 multiply_reduce_fusion.1
  165.7 0.7 fusion.13
  168.3 1.0 fusion.4
  169.4 2.3 %collective-permute-start.19 = (bf16[16,2048]{1,0:T(8,128)(2,1)S(1)}, bf16[16,2048]{1,0:T(8,128)(2,1)S(1)}, u32[]{:S(2)}, u32[]{:S(2)}) collective-permute-start(bf16[16,2048]{1,0:T(8,128)(2,1)S(1)} %get-tuple-element.30), channel_id=1, source_target_pairs={{0,8},{4,12},{8,0},{12,4},{16,24},{20,28},{24,16},{28,20},{1,9},{5... | collective-permute-start | bytes 196616 | tf_op jit(solution)/shard_map/ppermute | solution.py:189
  171.7 1.5 collective-permute-start.21
  173.3 0.9 fusion.3
  174.2 3.7 %collective-permute-done.21 = bf16[16,2048]{1,0:T(8,128)(2,1)S(1)} collective-permute-done((bf16[16,2048]{1,0:T(8,128)(2,1)S(1)}, bf16[16,2048]{1,0:T(8,128)(2,1)S(1)}, u32[]{:S(2)}, u32[]{:S(2)}) %collective-permute-start.21) | collective-permute-done | bytes 65568 | tf_op jit(solution)/shard_map/ppermute | solution.py:189
  177.8 2.0 %collective-permute-done.20 = bf16[16,2048]{1,0:T(8,128)(2,1)S(1)} collective-permute-done((bf16[16,2048]{1,0:T(8,128)(2,1)S(1)}, bf16[16,2048]{1,0:T(8,128)(2,1)S(1)}, u32[]{:S(2)}, u32[]{:S(2)}) %collective-permute-start.20) | collective-permute-done | bytes 65568 | tf_op jit(solution)/shard_map/ppermute | solution.py:189
  179.9 0.7 fusion.9
  (47 shorter events, 3.7 us)
Async XLA Ops:
  16.5 13.2 %all-to-all-start = ((bf16[4,32,2048]{2,1,0:T(8,128)(2,1)}), bf16[4,32,2048]{2,1,0:T(8,128)(2,1)S(1)}, u32[]{:S(2)}, u32[]{:S(2)}) async-start(bf16[4,32,2048]{2,1,0:T(8,128)(2,1)} %adjoint.2), calls=%async_computation | async-start | bytes 1048576 | tf_op jit(solution)/shard_map/all_to_all | solution.py:301
  27.1 56.5 %copy-start.4 = (f32[8192]{0:T(1024)S(1)}, f32[8192]{0:T(1024)}, u32[]{:S(2)}) copy-start(f32[8192]{0:T(1024)} %mul.86) | copy-start | bytes 98308
  27.1 56.5 %copy-start.6 = (f32[8192]{0:T(1024)S(1)}, f32[8192]{0:T(1024)}, u32[]{:S(2)}) copy-start(f32[8192]{0:T(1024)} %param.19) | copy-start | bytes 98308
  29.7 0.8 copy-start
  66.5 1.4 collective-permute-start
  68.7 5.1 %collective-permute-start.3 = (f32[1,8192]{1,0:T(1,128)S(1)}, f32[1,8192]{1,0:T(1,128)S(1)}, u32[]{:S(2)}, u32[]{:S(2)}) collective-permute-start(f32[1,8192]{1,0:T(1,128)S(1)} %add.112), channel_id=1, source_target_pairs={{0,3},{1,2},{2,1},{3,0},{4,7},{5,6},{6,5},{7,4},{8,11},{9,10},{10,... | collective-permute-start | bytes 98312 | tf_op jit(solution)/shard_map/ppermute | solution.py:189
  69.7 4.3 %collective-permute-start.2 = (f32[1,8192]{1,0:T(1,128)S(1)}, f32[1,8192]{1,0:T(1,128)S(1)}, u32[]{:S(2)}, u32[]{:S(2)}) collective-permute-start(f32[1,8192]{1,0:T(1,128)S(1)} %add.112), channel_id=1, source_target_pairs={{0,2},{1,3},{2,0},{3,1},{4,6},{5,7},{6,4},{7,5},{8,10},{9,11},{10,... | collective-permute-start | bytes 98312 | tf_op jit(solution)/shard_map/ppermute | solution.py:189
  71.2 3.9 %collective-permute-start.1 = (f32[1,8192]{1,0:T(1,128)S(1)}, f32[1,8192]{1,0:T(1,128)S(1)}, u32[]{:S(2)}, u32[]{:S(2)}) collective-permute-start(f32[1,8192]{1,0:T(1,128)S(1)} %add.112), channel_id=1, source_target_pairs={{0,1},{1,0},{2,3},{3,2},{4,5},{5,4},{6,7},{7,6},{8,9},{9,8},{10,11... | collective-permute-start | bytes 98312 | tf_op jit(solution)/shard_map/ppermute | solution.py:189
  75.1 5.8 %collective-permute-start.6 = (f32[1,8192]{1,0:T(1,128)S(1)}, f32[1,8192]{1,0:T(1,128)S(1)}, u32[]{:S(2)}, u32[]{:S(2)}) collective-permute-start(f32[1,8192]{1,0:T(1,128)S(1)} %add_add_fusion.3), channel_id=1, source_target_pairs={{0,24},{4,28},{8,16},{12,20},{16,8},{20,12},{24,0},{28,4},{1,25},{... | collective-permute-start | bytes 98312 | tf_op jit(solution)/shard_map/ppermute | solution.py:189
  78.8 4.8 %collective-permute-start.5 = (f32[1,8192]{1,0:T(1,128)S(1)}, f32[1,8192]{1,0:T(1,128)S(1)}, u32[]{:S(2)}, u32[]{:S(2)}) collective-permute-start(f32[1,8192]{1,0:T(1,128)S(1)} %add_add_fusion.3), channel_id=1, source_target_pairs={{0,16},{4,20},{8,24},{12,28},{16,0},{20,4},{24,8},{28,12},{1,17},{... | collective-permute-start | bytes 98312 | tf_op jit(solution)/shard_map/ppermute | solution.py:189
  78.8 4.8 %collective-permute-start.4 = (f32[1,8192]{1,0:T(1,128)S(1)}, f32[1,8192]{1,0:T(1,128)S(1)}, u32[]{:S(2)}, u32[]{:S(2)}) collective-permute-start(f32[1,8192]{1,0:T(1,128)S(1)} %add_add_fusion.3), channel_id=1, source_target_pairs={{0,8},{4,12},{8,0},{12,4},{16,24},{20,28},{24,16},{28,20},{1,9},{5... | collective-permute-start | bytes 98312 | tf_op jit(solution)/shard_map/ppermute | solution.py:189
  83.7 42.7 %copy-start.5 = (bf16[2,4,16,2048]{3,2,1,0:T(8,128)(2,1)S(1)}, bf16[2,4,16,2048]{3,2,1,0:T(8,128)(2,1)}, u32[]{:S(2)}) copy-start(bf16[2,4,16,2048]{3,2,1,0:T(8,128)(2,1)} %get-tuple-element.16) | copy-start | bytes 1572868
  112.8 51.0 %copy-start.7 = (f32[1,8192]{1,0:T(1,128)S(1)}, f32[1,8192]{1,0:T(1,128)}, u32[]{:S(2)}) copy-start(f32[1,8192]{1,0:T(1,128)} %multiply_subtract_fusion.err_ref) | copy-start | bytes 98308
  122.7 50.5 %copy-start.2 = (f32[32,8192]{1,0:T(8,128)S(1)}, f32[32,8192]{1,0:T(8,128)}, u32[]{:S(2)}) copy-start(f32[32,8192]{1,0:T(8,128)} %get-tuple-element.14) | copy-start | bytes 3145732
  122.7 50.5 %copy-start.3 = (f32[32,8192]{1,0:T(8,128)S(1)}, f32[32,8192]{1,0:T(8,128)}, u32[]{:S(2)}) copy-start(f32[32,8192]{1,0:T(8,128)} %get-tuple-element.15) | copy-start | bytes 3145732
  122.7 10.2 %all-to-all-start.3 = ((bf16[4,32,2048]{2,1,0:T(8,128)(2,1)}), bf16[4,32,2048]{2,1,0:T(8,128)(2,1)S(1)}, u32[]{:S(2)}, u32[]{:S(2)}) async-start(bf16[4,32,2048]{2,1,0:T(8,128)(2,1)} %get-tuple-element.12), calls=%async_computation.3 | async-start | bytes 1048576 | tf_op jit(solution)/shard_map/all_to_all | solution.py:303
  127.0 20.8 %collective-permute-start.14 = (bf16[4,16,2048]{2,1,0:T(8,128)(2,1)}, bf16[4,16,2048]{2,1,0:T(8,128)(2,1)S(1)}, u32[]{:S(2)}, u32[]{:S(2)}) collective-permute-start(bf16[4,16,2048]{2,1,0:T(8,128)(2,1)} %slice_bitcast_fusion.3), channel_id=1, source_target_pairs={{0,4},{4,0},{8,12},{12,8},{16,20},{20,16},{24,28},{28,24},{1,5},{5... | collective-permute-start | bytes 786440 | tf_op jit(solution)/shard_map/ppermute | solution.py:189
  132.9 0.8 copy-start.1
  147.9 1.4 collective-permute-start.7
  150.1 7.1 %collective-permute-start.10 = (f32[1,8192]{1,0:T(1,128)S(1)}, f32[1,8192]{1,0:T(1,128)S(1)}, u32[]{:S(2)}, u32[]{:S(2)}) collective-permute-start(f32[1,8192]{1,0:T(1,128)S(1)} %add.121), channel_id=1, source_target_pairs={{0,3},{1,2},{2,1},{3,0},{4,7},{5,6},{6,5},{7,4},{8,11},{9,10},{10,... | collective-permute-start | bytes 98312 | tf_op jit(solution)/shard_map/ppermute | solution.py:189
  151.6 5.6 %collective-permute-start.9 = (f32[1,8192]{1,0:T(1,128)S(1)}, f32[1,8192]{1,0:T(1,128)S(1)}, u32[]{:S(2)}, u32[]{:S(2)}) collective-permute-start(f32[1,8192]{1,0:T(1,128)S(1)} %add.121), channel_id=1, source_target_pairs={{0,2},{1,3},{2,0},{3,1},{4,6},{5,7},{6,4},{7,5},{8,10},{9,11},{10,... | collective-permute-start | bytes 98312 | tf_op jit(solution)/shard_map/ppermute | solution.py:189
  153.1 4.1 %collective-permute-start.8 = (f32[1,8192]{1,0:T(1,128)S(1)}, f32[1,8192]{1,0:T(1,128)S(1)}, u32[]{:S(2)}, u32[]{:S(2)}) collective-permute-start(f32[1,8192]{1,0:T(1,128)S(1)} %add.121), channel_id=1, source_target_pairs={{0,1},{1,0},{2,3},{3,2},{4,5},{5,4},{6,7},{7,6},{8,9},{9,8},{10,11... | collective-permute-start | bytes 98312 | tf_op jit(solution)/shard_map/ppermute | solution.py:189
  153.7 19.5 %collective-permute-start.15 = (bf16[16,2048]{1,0:T(8,128)(2,1)S(1)}, bf16[16,2048]{1,0:T(8,128)(2,1)S(1)}, u32[]{:S(2)}, u32[]{:S(2)}) collective-permute-start(bf16[16,2048]{1,0:T(8,128)(2,1)S(1)} %get-tuple-element.27), channel_id=1, source_target_pairs={{0,8},{4,12},{8,0},{12,4},{16,24},{20,28},{24,16},{28,20},{1,9},{5... | collective-permute-start | bytes 196616 | tf_op jit(solution)/shard_map/ppermute | solution.py:189
  153.7 20.4 %collective-permute-start.17 = (bf16[16,2048]{1,0:T(8,128)(2,1)S(1)}, bf16[16,2048]{1,0:T(8,128)(2,1)S(1)}, u32[]{:S(2)}, u32[]{:S(2)}) collective-permute-start(bf16[16,2048]{1,0:T(8,128)(2,1)S(1)} %get-tuple-element.28), channel_id=1, source_target_pairs={{0,24},{4,28},{8,16},{12,20},{16,8},{20,12},{24,0},{28,4},{1,25},{... | collective-permute-start | bytes 196616 | tf_op jit(solution)/shard_map/ppermute | solution.py:189
  157.3 5.8 %collective-permute-start.13 = (f32[1,8192]{1,0:T(1,128)S(1)}, f32[1,8192]{1,0:T(1,128)S(1)}, u32[]{:S(2)}, u32[]{:S(2)}) collective-permute-start(f32[1,8192]{1,0:T(1,128)S(1)} %add_add_fusion.1), channel_id=1, source_target_pairs={{0,24},{4,28},{8,16},{12,20},{16,8},{20,12},{24,0},{28,4},{1,25},{... | collective-permute-start | bytes 98312 | tf_op jit(solution)/shard_map/ppermute | solution.py:189
  158.6 5.1 %collective-permute-start.12 = (f32[1,8192]{1,0:T(1,128)S(1)}, f32[1,8192]{1,0:T(1,128)S(1)}, u32[]{:S(2)}, u32[]{:S(2)}) collective-permute-start(f32[1,8192]{1,0:T(1,128)S(1)} %add_add_fusion.1), channel_id=1, source_target_pairs={{0,16},{4,20},{8,24},{12,28},{16,0},{20,4},{24,8},{28,12},{1,17},{... | collective-permute-start | bytes 98312 | tf_op jit(solution)/shard_map/ppermute | solution.py:189
  159.2 4.5 %collective-permute-start.11 = (f32[1,8192]{1,0:T(1,128)S(1)}, f32[1,8192]{1,0:T(1,128)S(1)}, u32[]{:S(2)}, u32[]{:S(2)}) collective-permute-start(f32[1,8192]{1,0:T(1,128)S(1)} %add_add_fusion.1), channel_id=1, source_target_pairs={{0,8},{4,12},{8,0},{12,4},{16,24},{20,28},{24,16},{28,20},{1,9},{5... | collective-permute-start | bytes 98312 | tf_op jit(solution)/shard_map/ppermute | solution.py:189
  163.1 11.1 %collective-permute-start.16 = (bf16[16,2048]{1,0:T(8,128)(2,1)S(1)}, bf16[16,2048]{1,0:T(8,128)(2,1)S(1)}, u32[]{:S(2)}, u32[]{:S(2)}) collective-permute-start(bf16[16,2048]{1,0:T(8,128)(2,1)S(1)} %get-tuple-element.29), channel_id=1, source_target_pairs={{0,16},{4,20},{8,24},{12,28},{16,0},{20,4},{24,8},{28,12},{1,17},{... | collective-permute-start | bytes 196616 | tf_op jit(solution)/shard_map/ppermute | solution.py:189
  163.7 4.7 %collective-permute-start.18 = (bf16[4,16,2048]{2,1,0:T(8,128)(2,1)S(1)}, bf16[4,16,2048]{2,1,0:T(8,128)(2,1)S(1)}, u32[]{:S(2)}, u32[]{:S(2)}) collective-permute-start(bf16[4,16,2048]{2,1,0:T(8,128)(2,1)S(1)} %slice_bitcast_fusion.2), channel_id=1, source_target_pairs={{0,4},{4,0},{8,12},{12,8},{16,20},{20,16},{24,28},{28,24},{1,5},{5... | collective-permute-start | bytes 786440 | tf_op jit(solution)/shard_map/ppermute | solution.py:189
  169.4 4.8 %collective-permute-start.19 = (bf16[16,2048]{1,0:T(8,128)(2,1)S(1)}, bf16[16,2048]{1,0:T(8,128)(2,1)S(1)}, u32[]{:S(2)}, u32[]{:S(2)}) collective-permute-start(bf16[16,2048]{1,0:T(8,128)(2,1)S(1)} %get-tuple-element.30), channel_id=1, source_target_pairs={{0,8},{4,12},{8,0},{12,4},{16,24},{20,28},{24,16},{28,20},{1,9},{5... | collective-permute-start | bytes 196616 | tf_op jit(solution)/shard_map/ppermute | solution.py:189
  171.7 6.1 %collective-permute-start.21 = (bf16[16,2048]{1,0:T(8,128)(2,1)S(1)}, bf16[16,2048]{1,0:T(8,128)(2,1)S(1)}, u32[]{:S(2)}, u32[]{:S(2)}) collective-permute-start(bf16[16,2048]{1,0:T(8,128)(2,1)S(1)} %get-tuple-element.31), channel_id=1, source_target_pairs={{0,24},{4,28},{8,16},{12,20},{16,8},{20,12},{24,0},{28,4},{1,25},{... | collective-permute-start | bytes 196616 | tf_op jit(solution)/shard_map/ppermute | solution.py:189
  173.2 6.7 %collective-permute-start.20 = (bf16[16,2048]{1,0:T(8,128)(2,1)S(1)}, bf16[16,2048]{1,0:T(8,128)(2,1)S(1)}, u32[]{:S(2)}, u32[]{:S(2)}) collective-permute-start(bf16[16,2048]{1,0:T(8,128)(2,1)S(1)} %get-tuple-element.32), channel_id=1, source_target_pairs={{0,16},{4,20},{8,24},{12,28},{16,0},{20,4},{24,8},{28,12},{1,17},{... | collective-permute-start | bytes 196616 | tf_op jit(solution)/shard_map/ppermute | solution.py:189

commit v3 on v2

v3 whole, which is shorter than its diff:
```python
import functools
import math

import jax
import jax.numpy as jnp
from jax import lax
from jax.experimental import pallas as pl
from jax.experimental.pallas import tpu as pltpu
from jax.sharding import PartitionSpec as P

ITERS = 2
LANES = 128
WIDE = 256
ROWS = 256
CHUNK = 1024
UNROLL = 8


def grouping(levels, ncols):
    wide = min(WIDE, ncols)
    chunks = ncols // wide
    group = max(8, min(levels, ROWS // chunks))
    return wide, chunks, group


def one_hot(keys, numbers, values):
    key = jnp.broadcast_to(keys.astype(jnp.bfloat16), numbers.shape)
    val = jnp.broadcast_to(values, numbers.shape)
    return jnp.where(numbers == key, val, jnp.zeros_like(val))


def row_numbers(rows, n):
    return lax.broadcasted_iota(jnp.int32, (rows, n), 0).astype(jnp.float32).astype(jnp.bfloat16)


def span_of(c):
    return pl.ds(pl.multiple_of(c * CHUNK, CHUNK), CHUNK)


def total_of(x):
    return jnp.sum(x, axis=1, keepdims=True)


def advance(seen_refs, precision, errors, previous):
    seen = seen_refs[0][...]
    for ref in seen_refs[1:]:
        seen = seen + ref[...]
    norm = total_of(errors * seen)
    if previous is None:
        beta = jnp.zeros_like(norm)
        guide, image = errors, seen
    else:
        beta = norm / previous[2]
        guide, image = errors + beta * previous[0], seen + beta * previous[1]
    along = total_of(guide * image) + total_of(precision * image * image)
    return norm / along, beta, guide, image, norm


def adjoint_kernel(*refs, seen, first):
    starts_ref, keys_ref, weight_ref, precision_ref, err_ref, pert_ref, vert_ref = refs[:7]
    refs = refs[7:]
    levels, ncols = pert_ref.shape
    members = lax.axis_size("mem")
    wide, chunks, group = grouping(levels, ncols)
    rows = chunks * group
    if seen:
        before, refs = (None, refs) if first else ([r[...] for r in refs[:3]], refs[3:])
        seen_refs, refs = refs[:seen], refs[seen:]
        out_ref, new_ref, alpha_ref, beta_ref, guide_ref, image_ref, norm_ref, total, field = refs
        if before is not None:
            before[2] = before[2][:, :1]
        errors, precision = err_ref[...], precision_ref[...]
        alpha, beta, guide, image, norm = advance(seen_refs, precision, errors, before)
        new_ref[...] = errors - alpha * (guide + precision * image)
        guide_ref[...] = guide
        image_ref[...] = image
        for ref, value in ((alpha_ref, alpha), (beta_ref, beta), (norm_ref, norm)):
            ref[...] = jnp.broadcast_to(value, ref.shape)
    else:
        out_ref, new_ref, total, field = refs
        new_ref[...] = precision_ref[...] * err_ref[...]
    bands = out_ref.shape[1]
    numbers = row_numbers(rows, CHUNK)
    places = row_numbers(wide, CHUNK)
    ones = jnp.ones((1, CHUNK), jnp.bfloat16)

    def collect(g, carry):
        total[...] = jnp.zeros_like(total)
        base = (g * rows).astype(jnp.float32)

        def step(c, carry):
            span = span_of(c)
            weight = weight_ref[:, span]
            err = new_ref[:, span]
            above, beside = [], []
            for which, w in ((0, weight), (1, 1.0 - weight)):
                row = keys_ref[2 * which : 2 * which + 1, span] - base
                above.append(one_hot(row, numbers, (w * err).astype(jnp.bfloat16)))
                beside.append(one_hot(keys_ref[2 * which + 1 : 2 * which + 2, span], places, ones))
            total[...] += lax.dot_general(
                jnp.concatenate(above, axis=1),
                jnp.concatenate(beside, axis=1),
                (((1,), (1,)), ((), ())),
                preferred_element_type=jnp.float32,
            )
            return carry

        lax.fori_loop(starts_ref[g] // CHUNK, (starts_ref[g + 1] + CHUNK - 1) // CHUNK, step, 0)
        here = pl.ds(pl.multiple_of(g * group, group), group)
        for c in range(chunks):
            field[here, c * wide : (c + 1) * wide] = total[c * group : (c + 1) * group, :]
        return carry

    lax.fori_loop(0, levels // group, collect, 0)

    scale_inv = 1.0 / math.sqrt(members)
    for c in range(chunks):
        part = slice(c * wide, (c + 1) * wide)
        scaled = (pert_ref[:, part].astype(jnp.float32) * field[:, part] * scale_inv).astype(jnp.bfloat16)
        turned = scaled.astype(jnp.float32) + lax.dot_general(
            vert_ref[...], scaled, (((0,), (0,)), ((), ())), preferred_element_type=jnp.float32
        )
        for b in range(out_ref.shape[0]):
            out_ref[b, :, part] = turned[b * bands : (b + 1) * bands, :].astype(jnp.bfloat16)


def horizontal_kernel(cols_ref, moved_ref, mats_ref, resid_ref, mixed_ref, terms, first, second, picked):
    parts, bands, ncols = moved_ref.shape
    pairs = mats_ref.shape[0]
    per_part = ncols // LANES
    half = LANES // 2
    lane = lax.broadcasted_iota(jnp.int32, (bands, LANES), 1)
    low = lane < half
    low16 = lane.astype(jnp.float32).astype(jnp.bfloat16) < half
    sums = (first, second)
    for s in sums:
        s[...] = jnp.zeros_like(s)

    def tile_of(p):
        at = pl.multiple_of((p % per_part) * LANES, LANES)
        return p // per_part, pl.ds(at, LANES)

    def product(p, carry):
        part, lanes = tile_of(p)
        both = jnp.dot(moved_ref[part, :, lanes], mats_ref[p], preferred_element_type=jnp.float32)
        terms[2 * p] = both[:, :LANES]
        terms[2 * p + 1] = both[:, LANES:]
        return carry

    lax.fori_loop(0, pairs, product, 0, unroll=UNROLL)

    def scatter(i, carry):
        term = terms[i]
        for k in range(2):
            col = cols_ref[k, i]
            sums[k][(col & 1) ^ k, col >> 1] += term
        return carry

    lax.fori_loop(0, 2 * pairs, scatter, 0, unroll=UNROLL)

    def join(p, carry):
        part, lanes = tile_of(p)
        here = jnp.where(low, first[0, p], second[0, p])
        there = jnp.where(low, first[1, p], second[1, p])
        resid = moved_ref[part, :, lanes].astype(jnp.float32) + here + pltpu.roll(there, half, 1)
        resid_ref[:, pl.ds(pl.multiple_of(p * LANES, LANES), LANES)] = resid
        picked[0, p] = resid.astype(jnp.bfloat16)
        picked[1, p] = pltpu.roll(resid, half, 1).astype(jnp.bfloat16)
        return carry

    lax.fori_loop(0, pairs, join, 0, unroll=UNROLL)

    def gather(p, carry):
        part, lanes = tile_of(p)
        sources = []
        for q in range(2):
            one = cols_ref[0, 2 * p + q]
            two = cols_ref[1, 2 * p + q]
            sources.append(jnp.where(low16, picked[one & 1, one >> 1], picked[(two & 1) ^ 1, two >> 1]))
        both = lax.dot_general(
            jnp.concatenate(sources, axis=1),
            mats_ref[p],
            (((1,), (1,)), ((), ())),
            preferred_element_type=jnp.float32,
        )
        mixed_ref[part, :, lanes] = (picked[0, p].astype(jnp.float32) + both).astype(jnp.bfloat16)
        return carry

    lax.fori_loop(0, pairs, gather, 0, unroll=UNROLL)


def forward_kernel(starts_ref, keys_ref, weight_ref, mixed_ref, pert_ref, vert_ref, field_ref, obs_ref):
    levels, ncols = pert_ref.shape
    members = lax.axis_size("mem")
    wide, chunks, group = grouping(levels, ncols)
    rows = chunks * group
    scale_inv = 1.0 / math.sqrt(members)
    for c in range(chunks):
        part = slice(c * wide, (c + 1) * wide)
        mixed = mixed_ref[:, part]
        localized = mixed.astype(jnp.float32) + jnp.dot(
            vert_ref[...], mixed, preferred_element_type=jnp.float32
        )
        field = (pert_ref[:, part].astype(jnp.float32) * localized * scale_inv).astype(jnp.bfloat16)
        for g in range(levels // group):
            field_ref[g, c * group : (c + 1) * group, :] = field[g * group : (g + 1) * group, :]

    obs_ref[...] = jnp.zeros_like(obs_ref)
    places = row_numbers(wide, CHUNK)
    ones = jnp.ones((1, CHUNK), jnp.bfloat16)
    numbers = lax.broadcasted_iota(jnp.int32, (rows, CHUNK), 0).astype(jnp.float32)
    def collect(g, carry):
        base = (g * rows).astype(jnp.float32)

        def step(c, carry):
            span = span_of(c)
            weight = weight_ref[:, span]
            result = obs_ref[:, span]
            for which, w in ((0, weight), (1, 1.0 - weight)):
                row = keys_ref[2 * which : 2 * which + 1, span] - base
                hot = one_hot(keys_ref[2 * which + 1 : 2 * which + 2, span], places, ones)
                lines = jnp.dot(field_ref[g], hot, preferred_element_type=jnp.float32)
                kept = jnp.where(numbers == row, lines, 0.0)
                result = result + w * jnp.sum(kept, axis=0, keepdims=True)
            obs_ref[:, span] = result
            return carry

        lax.fori_loop(starts_ref[g] // CHUNK, (starts_ref[g + 1] + CHUNK - 1) // CHUNK, step, 0)
        return carry

    lax.fori_loop(0, levels // group, collect, 0)


def finish_kernel(*refs, seen, group, wide):
    precision_ref, err_ref, guide_ref, image_ref, norm_ref = refs[:5]
    refs = refs[5:]
    seen_refs, refs = refs[:seen], refs[seen:]
    state_ref, field_ref = refs[-2:]
    refs = refs[:-2]
    steps = len(refs) // 4 + 1
    alphas, betas, rest = refs[: steps - 1], refs[steps - 1 : 2 * steps - 2], refs[2 * steps - 2 :]
    resids, fields = rest[:steps], rest[steps:]
    before = (guide_ref[...], image_ref[...], norm_ref[:, :1])
    alpha, beta, _, _, _ = advance(seen_refs, precision_ref[...], err_ref[...], before)
    alphas = [a[:, :1] for a in alphas] + [alpha]
    betas = [b[:, :1] for b in betas] + [beta]
    mix, shares = [], []
    for a, b in zip(alphas, betas):
        mix = [b * m for m in mix] + [jnp.ones_like(a)]
        shares = [s + a * m for s, m in zip(shares + [jnp.zeros_like(a)], mix)]
    state = shares[0] * resids[0][...]
    for share, resid in zip(shares[1:], resids[1:]):
        state = state + share * resid[...]
    state_ref[...] = state.astype(jnp.bfloat16)
    groups, rows, _ = fields[0].shape
    core = lax.axis_index("mem") % 2
    for g in range(groups):
        total = shares[0] * fields[0][g].astype(jnp.float32)
        for share, field in zip(shares[1:], fields[1:]):
            total = total + share * field[g].astype(jnp.float32)
        total = total.astype(jnp.bfloat16)
        for c in range(rows // group):
            part = slice(c * wide, (c + 1) * wide)
            if len(field_ref.shape) == 2:
                field_ref[g * group : (g + 1) * group, part] = total[c * group : (c + 1) * group, :]
            else:
                size = field_ref.shape[2]
                for s in range(group // size):
                    number = g * (group // size) + s
                    field_ref[(number % 2) ^ core, number // 2, :, part] = total[
                        c * group + s * size : c * group + (s + 1) * size, :
                    ]


def swap(x, axis, offset):
    n = lax.axis_size(axis)
    return lax.ppermute(x, axis, [(i, i ^ offset) for i in range(n)])


def total_over(x, axis, offsets):
    return sum([swap(x, axis, k) for k in offsets], x)


def shares_everywhere(x):
    x = total_over(x, "mem", (1,))
    x = total_over(x, "col", range(1, lax.axis_size("col")))
    return [x] + [swap(x, "mem", k) for k in range(2, lax.axis_size("mem"), 2)]


def scatter_members(field):
    if field.ndim == 2:
        nmem = lax.axis_size("mem")
        field = field.reshape(nmem, field.shape[0] // nmem, field.shape[1])
        pieces = lax.all_to_all(field, "mem", 0, 0, tiled=True)
        return jnp.sum(pieces.astype(jnp.float32), axis=0)
    mine = (field[0].astype(jnp.float32) + swap(field[1], "mem", 1).astype(jnp.float32)).astype(jnp.bfloat16)
    chips = mine.shape[0]
    chip = lax.axis_index("mem") // 2
    total = lax.dynamic_index_in_dim(mine, chip, 0, keepdims=False).astype(jnp.float32)
    for k in range(1, chips):
        piece = lax.dynamic_index_in_dim(mine, chip ^ k, 0, keepdims=False)
        total = total + swap(piece, "mem", 2 * k).astype(jnp.float32)
    return total


def per_device(
    perturbations,
    vertical,
    blocks,
    block_scale,
    block_cols,
    obs_level,
    obs_nodes,
    obs_weight,
    obs_value,
    obs_precision,
):
    local_members, levels, ncols = perturbations.shape
    assert local_members == 1
    nblocks, width, depth = blocks.shape
    assert 2 * width == LANES and depth == LANES
    ncol = lax.axis_size("col")
    nmem = lax.axis_size("mem")
    bands = levels // ncol
    pairs = nblocks // 2
    nodes = nblocks * width
    nobs = obs_level.shape[0]
    pert = perturbations[0]
    wide, chunks, group = grouping(levels, ncols)
    rows = chunks * group
    slices = levels // nmem

    order = obs_level * nobs + jnp.arange(nobs, dtype=jnp.int32)
    both = obs_nodes[:, 0] * nodes + obs_nodes[:, 1]
    order, both, weight, value, precision = lax.sort(
        (order, both, obs_weight, obs_value, obs_precision), num_keys=1, is_stable=False
    )
    level = order // nobs
    keys = []
    for node in (both // nodes, both % nodes):
        local = node - lax.axis_index("col") * ncols
        inside = (local >= 0) & (local < ncols)
        row = (level // group) * rows + (local // wide) * group + level % group
        keys += [jnp.where(inside, row, -(1 << 20)), jnp.where(inside, local % wide, 0)]
    keys = jnp.stack(keys).astype(jnp.float32)
    bounds = jnp.arange(levels // group + 1, dtype=jnp.int32) * group
    starts = jnp.sum((obs_level[None, :] < bounds[:, None]).astype(jnp.int32), axis=1)
    weight, value, precision = (a.reshape(1, nobs) for a in (weight, value, precision))

    scaled = (blocks.astype(jnp.float32) * jnp.repeat(block_scale, width, axis=1)[:, None, :]).astype(
        jnp.bfloat16
    ).reshape(pairs, 2, width, depth)
    mats = jnp.concatenate(
        [
            jnp.pad(scaled[:, 0], ((0, 0), (0, 0), (0, depth))),
            jnp.pad(scaled[:, 1], ((0, 0), (0, 0), (depth, 0))),
        ],
        axis=1,
    )
    cols = block_cols.T

    vmem = pl.BlockSpec(memory_space=pltpu.VMEM)
    smem = pl.BlockSpec(memory_space=pltpu.SMEM)
    vector = jax.ShapeDtypeStruct((1, nobs), jnp.float32)
    number = jax.ShapeDtypeStruct((1, LANES), jnp.float32)
    moved_shape = jax.ShapeDtypeStruct((ncol, bands, ncols), jnp.bfloat16)

    def adjoint(errors, seen, before):
        count = len(seen)
        outs = (moved_shape, vector) + ((number, number, vector, vector, number) if count else ())
        extra = (list(before) if before is not None else []) + list(seen)
        return pl.pallas_call(
            functools.partial(adjoint_kernel, seen=count, first=before is None),
            out_shape=outs,
            in_specs=[smem] + [vmem] * (6 + len(extra)),
            out_specs=(vmem,) * len(outs),
            scratch_shapes=[
                pltpu.VMEM((rows, wide), jnp.float32),
                pltpu.VMEM((levels, ncols), jnp.float32),
            ],
            name="adjoint",
        )(starts, keys, weight, precision, errors, pert, vertical, *extra)

    middle = pl.pallas_call(
        horizontal_kernel,
        out_shape=(jax.ShapeDtypeStruct((bands, nodes), jnp.float32), moved_shape),
        in_specs=[smem] + [vmem] * 2,
        out_specs=(vmem, vmem),
        scratch_shapes=[
            pltpu.VMEM((2 * pairs, bands, LANES), jnp.float32),
            pltpu.VMEM((2, pairs, bands, LANES), jnp.float32),
            pltpu.VMEM((2, pairs, bands, LANES), jnp.float32),
            pltpu.VMEM((2, pairs, bands, LANES), jnp.bfloat16),
        ],
        name="horizontal",
    )
    forward = pl.pallas_call(
        forward_kernel,
        out_shape=(
            jax.ShapeDtypeStruct((levels // group, rows, wide), jnp.bfloat16),
            vector,
        ),
        in_specs=[smem] + [vmem] * 5,
        out_specs=(vmem, vmem),
        name="forward",
    )

    errors, seen, before = value, (), None
    alphas, betas, fields, resids = [], [], [], []
    for step in range(ITERS):
        if step == 0:
            sent, errors = adjoint(errors, seen, None)
        else:
            sent, errors, alpha, beta, *before = adjoint(errors, seen, before)
            alphas.append(alpha)
            betas.append(beta)
        moved = lax.all_to_all(sent, "col", 0, 0, tiled=True)
        resid, mixed = middle(cols, moved, mats)
        columns = lax.all_to_all(mixed, "col", 0, 0, tiled=True).reshape(levels, ncols)
        field, partial = forward(starts, keys, weight, columns, pert, vertical)
        seen = shares_everywhere(partial)
        resids.append(resid)
        fields.append(field)

    split = slices % 16 == 0 and group % slices == 0
    field_shape = (2, nmem // 2, slices, ncols) if split else (levels, ncols)
    args = [precision, errors, *before, *seen, *alphas, *betas, *resids, *fields]
    state, total = pl.pallas_call(
        functools.partial(finish_kernel, seen=len(seen), group=group, wide=wide),
        out_shape=(
            jax.ShapeDtypeStruct((bands, nodes), jnp.bfloat16),
            jax.ShapeDtypeStruct(field_shape, jnp.bfloat16),
        ),
        in_specs=[vmem] * len(args),
        out_specs=(vmem, vmem),
        name="finish",
    )(*args)
    return (state[None], scatter_members(total))


def solution(mesh):
    in_specs = (P("mem", None, "col"), P(), P(), P(), P(), P(), P(), P(), P(), P())
    out_specs = (P("mem", "col", None), P("mem", "col"))
    return jax.shard_map(
        per_device, mesh=mesh, in_specs=in_specs, out_specs=out_specs, check_vma=False
    )
```

time: 181 us -> 166 us (0.917)
  Pallas kernels: 77.2 us -> 54.4 us
  blocking collectives: 23.2 us -> 34.6 us
  starting transfers between devices: 32.8 us -> 25.7 us
  between operations: 5.83 us -> 0.82 us
  other arithmetic: 13.2 us -> 17.9 us
  waiting for transfers between devices: 24.1 us -> 27.6 us
    pallas_call x6 -> x7, Pallas kernels: 77.2 us -> 54.4 us  [the longest x2 19.8 us: per_device(): resid, mixed = middle(cols, moved, mats)]
    all_to_all x2 -> x3, blocking collectives: 23.2 us -> 34.6 us  [the longest x2 23.2 us: per_device(): lax.all_to_all(mixed, 'col', 0, 0, tiled=True).reshape(levels, ncols)]
    ppermute x22 -> x18, waiting for transfers between devices: 15.7 us -> 23.5 us  [swap(): return lax.ppermute(x, axis, [(i, i ^ offset) for i in range(n)])]
    sort x0 -> x1, other arithmetic: none -> 7.27 us  [per_device(): lax.sort((order, both, obs_weight, obs_value, obs_precision), num_keys=1,...]
    all_to_all x2 -> x1, waiting for transfers between devices: 8.36 us -> 4.11 us  [per_device(): moved = lax.all_to_all(sent, 'col', 0, 0, tiled=True)]
    all_to_all x2 -> x1, starting transfers between devices: 8.79 us -> 5.2 us  [per_device(): moved = lax.all_to_all(sent, 'col', 0, 0, tiled=True)]
    ppermute x22 -> x18, starting transfers between devices: 24 us -> 20.5 us  [swap(): return lax.ppermute(x, axis, [(i, i ^ offset) for i in range(n)])]
  transfers between devices with their start and end apart: 24 -> 19, of which waited for: 13 -> 15; matrix products, arithmetic and copies ran while one was open for 6% -> 2% of each run, Pallas kernels for 8% -> 0%
where the time goes in v3:
time: 166 us; the launch traced here: 165 us
  Pallas kernels  54.4 us (33%)
  blocking collectives  34.6 us (21%)
  waiting for transfers between devices  27.6 us (17%)
  starting transfers between devices  25.7 us (15%)
  other arithmetic  17.9 us (11%)
  local copies, waits for them, and re-layouts  3.97 us (2%)
    ppermute x18, waiting for transfers between devices, swap(): return lax.ppermute(x, axis, [(i, i ^ offset) for i in range(n)])  23.5 us
    all_to_all x2, blocking collectives, per_device(): lax.all_to_all(mixed, 'col', 0, 0, tiled=True).reshape(levels, ncols)  23.2 us
    ppermute x18, starting transfers between devices, swap(): return lax.ppermute(x, axis, [(i, i ^ offset) for i in range(n)])  20.5 us
    pallas_call x2, Pallas kernels, per_device(): resid, mixed = middle(cols, moved, mats)  19.8 us
    pallas_call x2, Pallas kernels, adjoint(): pl.pallas_call(functools.partial(adjoint_kernel, seen=count, first=before...  15.7 us
    pallas_call x2, Pallas kernels, per_device(): field, partial = forward(starts, keys, weight, columns, pert, vertical)  15.3 us
    all_to_all x1, blocking collectives, per_device(): moved = lax.all_to_all(sent, 'col', 0, 0, tiled=True)  11.3 us
    sort x1, other arithmetic, per_device(): lax.sort((order, both, obs_weight, obs_value, obs_precision), num_keys=1,...  7.27 us
  transfers between devices with their start and end apart: 19, of which 15 were waited for; matrix products, arithmetic and copies ran while one was open for 2% of the time, Pallas kernels for 0%

profile of v3, /device:TPU:0, one launch (start us, length us, event | category | flops | bytes accessed | tf_op | source)
XLA Modules:
  0.0 165.0 jit_solution(11404291714496517135)
XLA Ops:
  0.7 1.1 slice_add_fusion
  1.7 0.8 iota_add_fusion
  2.5 1.6 convert_reduce_fusion.refs_0_.starts_ref
  4.1 7.3 %sort.33 = (s32[8192]{0:T(1024)S(1)}, s32[8192]{0:T(1024)S(1)}, f32[8192]{0:T(1024)}, f32[8192]{0:T(1024)}, f32[8192]{0:T(1024)}) sort(s32[8192]{0:T(1024)S(1)} %iota_add_fusion, s32[8192]{0:T(1024)S(1)} %bitcast.52, f32[8192]{0:T(1024)} %param.17, f32[8192]{0:T(1024)} %param.18, f32[8192]{0:T(1024)} %param.19), dimensions={0}, to_apply=%region_0.0 | sort | flops 106496 | bytes 327680 | tf_op jit(solution)/shard_map/sort | solution.py:335
  11.5 0.8 add_convert_fusion.refs_1_.keys_ref
  12.3 7.7 %adjoint.2 = (bf16[4,32,2048]{2,1,0:T(8,128)(2,1)}, f32[1,8192]{1,0:T(1,128)}) custom-call(s32[5]{0:T(128)} %convert_reduce_fusion.refs_0_.starts_ref, f32[4,8192]{1,0:T(4,128)} %add_convert_fusion.refs_1_.keys_ref, f32[1,8192]{1,0:T(1,128)} %bitcast.44, f32[1,8192]{1,0:T(1,128)} %bitcast.48, f32[1,8192]{1,0:T(1,128)} %bitcast.57, ...), custom_call_target="tpu_custom_call" | custom-call | tf_op jit(solution)/shard_map/adjoint/pallas_call | solution.py:372
  20.0 5.2 %all-to-all-start = ((bf16[4,32,2048]{2,1,0:T(8,128)(2,1)}), bf16[4,32,2048]{2,1,0:T(8,128)(2,1)S(1)}, u32[]{:S(2)}, u32[]{:S(2)}) async-start(bf16[4,32,2048]{2,1,0:T(8,128)(2,1)} %get-tuple-element.32), calls=%async_computation | async-start | bytes 1048576 | tf_op jit(solution)/shard_map/all_to_all | solution.py:417
  25.2 0.7 broadcast_in_dim.16
  26.0 0.6 multiply_convert_fusion
  26.8 2.3 %fusion.2.mats_ref = bf16[64,128,256]{2,1,0:T(8,128)(2,1)} fusion(bf16[64,64,128]{2,1,0:T(8,128)(2,1)S(1)} %get-tuple-element.51, bf16[64,64,128]{2,1,0:T(8,128)(2,1)S(1)} %get-tuple-element.50), kind=kLoop, calls=%fused_computation.4 | loop fusion | flops 16777216 | bytes 6291456 | tf_op jit(solution)/shard_map/concatenate | solution.py:353
  29.1 4.1 %all-to-all-done.moved_ref = bf16[4,32,2048]{2,1,0:T(8,128)(2,1)S(1)} async-done(((bf16[4,32,2048]{2,1,0:T(8,128)(2,1)}), bf16[4,32,2048]{2,1,0:T(8,128)(2,1)S(1)}, u32[]{:S(2)}, u32[]{:S(2)}) %all-to-all-start) | async-done | bytes 524320 | tf_op jit(solution)/shard_map/all_to_all | solution.py:417
  33.2 0.8 copy-done
  34.0 9.9 %horizontal.2 = (f32[32,8192]{1,0:T(8,128)}, bf16[4,32,2048]{2,1,0:T(8,128)(2,1)}) custom-call(s32[2,128]{1,0:T(2,128)} %bitcast.58, bf16[4,32,2048]{2,1,0:T(8,128)(2,1)} %copy-done, bf16[64,128,256]{2,1,0:T(8,128)(2,1)} %fusion.2.mats_ref), custom_call_target="tpu_custom_call" | custom-call | tf_op jit(solution)/shard_map/horizontal/pallas_call | solution.py:418
  43.9 11.9 %all_to_all.20 = bf16[4,32,2048]{2,1,0:T(8,128)(2,1)} all-to-all(bf16[4,32,2048]{2,1,0:T(8,128)(2,1)} %get-tuple-element.33), channel_id=1, replica_groups=mesh['mem'=8,'col'=4] {'col'}, dimensions={0} | all-to-all | bytes 1048576 | tf_op jit(solution)/shard_map/all_to_all | solution.py:419
  55.8 7.7 %forward.2 = (bf16[4,256,256]{2,1,0:T(8,128)(2,1)}, f32[1,8192]{1,0:T(1,128)}) custom-call(s32[5]{0:T(128)} %convert_reduce_fusion.refs_0_.starts_ref, f32[4,8192]{1,0:T(4,128)} %add_convert_fusion.refs_1_.keys_ref, f32[1,8192]{1,0:T(1,128)} %bitcast.45, bf16[128,2048]{1,0:T(8,128)(2,1)} %bitcast.43, bf16[128,2048]{1,0:T(8,128)(2,1)} %bitcast.39, ...), custom_call_target="tpu_custom_call" | custom-call | tf_op jit(solution)/shard_map/forward/pallas_call | solution.py:420
  63.5 1.4 collective-permute-done
  64.9 0.8 add.111
  65.7 1.0 collective-permute-start.1
  67.2 2.0 %collective-permute-start.3 = (f32[1,8192]{1,0:T(1,128)S(1)}, f32[1,8192]{1,0:T(1,128)S(1)}, u32[]{:S(2)}, u32[]{:S(2)}) collective-permute-start(f32[1,8192]{1,0:T(1,128)S(1)} %add.111), channel_id=1, source_target_pairs={{0,3},{1,2},{2,1},{3,0},{4,7},{5,6},{6,5},{7,4},{8,11},{9,10},{10,... | collective-permute-start | bytes 98312 | tf_op jit(solution)/shard_map/ppermute | solution.py:277
  69.7 1.2 collective-permute-done.2
  70.9 1.1 collective-permute-done.3
  72.1 1.7 %collective-permute-start.4 = (f32[1,8192]{1,0:T(1,128)S(1)}, f32[1,8192]{1,0:T(1,128)S(1)}, u32[]{:S(2)}, u32[]{:S(2)}) collective-permute-start(f32[1,8192]{1,0:T(1,128)S(1)} %add_add_fusion.1.refs_7_), channel_id=1, source_target_pairs={{0,8},{4,12},{8,0},{12,4},{16,24},{20,28},{24,16},{28,20},{1,9},{5... | collective-permute-start | bytes 98312 | tf_op jit(solution)/shard_map/ppermute | solution.py:277
  73.8 2.6 %collective-permute-start.5 = (f32[1,8192]{1,0:T(1,128)S(1)}, f32[1,8192]{1,0:T(1,128)S(1)}, u32[]{:S(2)}, u32[]{:S(2)}) collective-permute-start(f32[1,8192]{1,0:T(1,128)S(1)} %add_add_fusion.1.refs_7_), channel_id=1, source_target_pairs={{0,16},{4,20},{8,24},{12,28},{16,0},{20,4},{24,8},{28,12},{1,17},{... | collective-permute-start | bytes 98312 | tf_op jit(solution)/shard_map/ppermute | solution.py:277
  76.6 2.6 %collective-permute-done.5.refs_9_ = f32[1,8192]{1,0:T(1,128)S(1)} collective-permute-done((f32[1,8192]{1,0:T(1,128)S(1)}, f32[1,8192]{1,0:T(1,128)S(1)}, u32[]{:S(2)}, u32[]{:S(2)}) %collective-permute-start.5) | collective-permute-done | bytes 32800 | tf_op jit(solution)/shard_map/ppermute | solution.py:277
  79.2 2.9 %collective-permute-done.6.refs_10_ = f32[1,8192]{1,0:T(1,128)S(1)} collective-permute-done((f32[1,8192]{1,0:T(1,128)S(1)}, f32[1,8192]{1,0:T(1,128)S(1)}, u32[]{:S(2)}, u32[]{:S(2)}) %collective-permute-start.6) | collective-permute-done | bytes 32800 | tf_op jit(solution)/shard_map/ppermute | solution.py:277
  82.7 7.9 %adjoint.3 = (bf16[4,32,2048]{2,1,0:T(8,128)(2,1)}, f32[1,8192]{1,0:T(1,128)}, f32[1,128]{1,0:T(1,128)}, f32[1,128]{1,0:T(1,128)}, f32[1,8192]{1,0:T(1,128)}, /*index=5*/f32[1,8192]{1,0:T(1,128)}, f32[1,128]{1,0:T(1,128)}) custom-call(s32[5]{0:T(128)} %convert_reduce_fusion.refs_0_.starts_ref, f32[4,8192]{1,0:T(4,128)} %add_convert_fusion.refs_1_.keys_ref, ...), custom_call_target="tpu_custom_call" | custom-call | tf_op jit(solution)/shard_map/adjoint/pallas_call | solution.py:372
  90.6 11.3 %all_to_all.21.moved_ref = bf16[4,32,2048]{2,1,0:T(8,128)(2,1)} all-to-all(bf16[4,32,2048]{2,1,0:T(8,128)(2,1)} %get-tuple-element.39), channel_id=1, replica_groups=mesh['mem'=8,'col'=4] {'col'}, dimensions={0} | all-to-all | bytes 1048576 | tf_op jit(solution)/shard_map/all_to_all | solution.py:417
  102.0 9.9 %horizontal.3 = (f32[32,8192]{1,0:T(8,128)}, bf16[4,32,2048]{2,1,0:T(8,128)(2,1)}) custom-call(s32[2,128]{1,0:T(2,128)} %bitcast.59, bf16[4,32,2048]{2,1,0:T(8,128)(2,1)} %all_to_all.21.moved_ref, bf16[64,128,256]{2,1,0:T(8,128)(2,1)} %fusion.2.mats_ref), custom_call_target="tpu_custom_call" | custom-call | tf_op jit(solution)/shard_map/horizontal/pallas_call | solution.py:418
  111.8 11.3 %all_to_all.22 = bf16[4,32,2048]{2,1,0:T(8,128)(2,1)} all-to-all(bf16[4,32,2048]{2,1,0:T(8,128)(2,1)} %get-tuple-element.40), channel_id=1, replica_groups=mesh['mem'=8,'col'=4] {'col'}, dimensions={0} | all-to-all | bytes 1048576 | tf_op jit(solution)/shard_map/all_to_all | solution.py:419
  123.2 7.6 %forward.3 = (bf16[4,256,256]{2,1,0:T(8,128)(2,1)}, f32[1,8192]{1,0:T(1,128)}) custom-call(s32[5]{0:T(128)} %convert_reduce_fusion.refs_0_.starts_ref, f32[4,8192]{1,0:T(4,128)} %add_convert_fusion.refs_1_.keys_ref, f32[1,8192]{1,0:T(1,128)} %bitcast.47, bf16[128,2048]{1,0:T(8,128)(2,1)} %bitcast.42, bf16[128,2048]{1,0:T(8,128)(2,1)} %bitcast.41, ...), custom_call_target="tpu_custom_call" | custom-call | tf_op jit(solution)/shard_map/forward/pallas_call | solution.py:420
  130.8 1.4 collective-permute-done.7
  132.2 0.8 add.115
  133.0 1.0 collective-permute-start.10
  134.0 1.5 collective-permute-start.8
  135.5 1.1 collective-permute-start.9
  136.6 1.6 collective-permute-done.10
  138.2 1.2 collective-permute-done.9
  139.5 0.9 collective-permute-start.12
  140.4 3.5 %collective-permute-start.13 = (f32[1,8192]{1,0:T(1,128)S(1)}, f32[1,8192]{1,0:T(1,128)S(1)}, u32[]{:S(2)}, u32[]{:S(2)}) collective-permute-start(f32[1,8192]{1,0:T(1,128)S(1)} %add_add_fusion.refs_5_), channel_id=1, source_target_pairs={{0,24},{4,28},{8,16},{12,20},{16,8},{20,12},{24,0},{28,4},{1,25},{... | collective-permute-start | bytes 98312 | tf_op jit(solution)/shard_map/ppermute | solution.py:277
  144.4 1.7 %collective-permute-done.13.refs_8_ = f32[1,8192]{1,0:T(1,128)S(1)} collective-permute-done((f32[1,8192]{1,0:T(1,128)S(1)}, f32[1,8192]{1,0:T(1,128)S(1)}, u32[]{:S(2)}, u32[]{:S(2)}) %collective-permute-start.13) | collective-permute-done | bytes 32800 | tf_op jit(solution)/shard_map/ppermute | solution.py:277
  146.8 3.7 %finish.1 = (bf16[32,8192]{1,0:T(8,128)(2,1)}, bf16[2,4,16,2048]{3,2,1,0:T(8,128)(2,1)}) custom-call(f32[1,8192]{1,0:T(1,128)} %bitcast.50, f32[1,8192]{1,0:T(1,128)} %get-tuple-element.35.refs_1_, f32[1,8192]{1,0:T(1,128)} %get-tuple-element.36.refs_2_, f32[1,8192]{1,0:T(1,128)} %get-tuple-element.37.refs_3_, f32[1,128]{1,0:T(1,128)} %get-tuple-element.38.refs_4_, ...), custom_call_target="tpu_custom_call" | custom-call | tf_op jit(solution)/shard_map/finish/pallas_call | solution.py:428
  150.4 1.0 slice_bitcast_fusion.2
  151.5 1.5 collective-permute-done.14
  153.0 1.0 fusion.3
  154.4 3.8 %collective-permute-start.16 = (bf16[16,2048]{1,0:T(8,128)(2,1)S(1)}, bf16[16,2048]{1,0:T(8,128)(2,1)S(1)}, u32[]{:S(2)}, u32[]{:S(2)}) collective-permute-start(bf16[16,2048]{1,0:T(8,128)(2,1)S(1)} %get-tuple-element.54), channel_id=1, source_target_pairs={{0,16},{4,20},{8,24},{12,28},{16,0},{20,4},{24,8},{28,12},{1,17},{... | collective-permute-start | bytes 196616 | tf_op jit(solution)/shard_map/ppermute | solution.py:277
  158.5 3.7 %collective-permute-done.16 = bf16[16,2048]{1,0:T(8,128)(2,1)S(1)} collective-permute-done((bf16[16,2048]{1,0:T(8,128)(2,1)S(1)}, bf16[16,2048]{1,0:T(8,128)(2,1)S(1)}, u32[]{:S(2)}, u32[]{:S(2)}) %collective-permute-start.16) | collective-permute-done | bytes 65568 | tf_op jit(solution)/shard_map/ppermute | solution.py:277
  162.2 2.1 %collective-permute-done.17 = bf16[16,2048]{1,0:T(8,128)(2,1)S(1)} collective-permute-done((bf16[16,2048]{1,0:T(8,128)(2,1)S(1)}, bf16[16,2048]{1,0:T(8,128)(2,1)S(1)}, u32[]{:S(2)}, u32[]{:S(2)}) %collective-permute-start.17) | collective-permute-done | bytes 65568 | tf_op jit(solution)/shard_map/ppermute | solution.py:277
  164.3 0.7 fusion.5
  (40 shorter events, 4.3 us)
Async XLA Ops:
  0.6 25.4 %copy-start.1 = (bf16[128,64,128]{2,1,0:T(8,128)(2,1)S(1)}, bf16[128,64,128]{2,1,0:T(8,128)(2,1)}, u32[]{:S(2)}) copy-start(bf16[128,64,128]{2,1,0:T(8,128)(2,1)} %param.12) | copy-start | bytes 6291460
  20.0 13.2 %all-to-all-start = ((bf16[4,32,2048]{2,1,0:T(8,128)(2,1)}), bf16[4,32,2048]{2,1,0:T(8,128)(2,1)S(1)}, u32[]{:S(2)}, u32[]{:S(2)}) async-start(bf16[4,32,2048]{2,1,0:T(8,128)(2,1)} %get-tuple-element.32), calls=%async_computation | async-start | bytes 1048576 | tf_op jit(solution)/shard_map/all_to_all | solution.py:417
  33.2 0.8 copy-start
  63.5 1.4 collective-permute-start
  65.7 4.0 %collective-permute-start.1 = (f32[1,8192]{1,0:T(1,128)S(1)}, f32[1,8192]{1,0:T(1,128)S(1)}, u32[]{:S(2)}, u32[]{:S(2)}) collective-permute-start(f32[1,8192]{1,0:T(1,128)S(1)} %add.111), channel_id=1, source_target_pairs={{0,1},{1,0},{2,3},{3,2},{4,5},{5,4},{6,7},{7,6},{8,9},{9,8},{10,11... | collective-permute-start | bytes 98312 | tf_op jit(solution)/shard_map/ppermute | solution.py:277
  66.7 4.3 %collective-permute-start.2 = (f32[1,8192]{1,0:T(1,128)S(1)}, f32[1,8192]{1,0:T(1,128)S(1)}, u32[]{:S(2)}, u32[]{:S(2)}) collective-permute-start(f32[1,8192]{1,0:T(1,128)S(1)} %add.111), channel_id=1, source_target_pairs={{0,2},{1,3},{2,0},{3,1},{4,6},{5,7},{6,4},{7,5},{8,10},{9,11},{10,... | collective-permute-start | bytes 98312 | tf_op jit(solution)/shard_map/ppermute | solution.py:277
  67.2 4.8 %collective-permute-start.3 = (f32[1,8192]{1,0:T(1,128)S(1)}, f32[1,8192]{1,0:T(1,128)S(1)}, u32[]{:S(2)}, u32[]{:S(2)}) collective-permute-start(f32[1,8192]{1,0:T(1,128)S(1)} %add.111), channel_id=1, source_target_pairs={{0,3},{1,2},{2,1},{3,0},{4,7},{5,6},{6,5},{7,4},{8,11},{9,10},{10,... | collective-permute-start | bytes 98312 | tf_op jit(solution)/shard_map/ppermute | solution.py:277
  72.1 10.0 %copy-start.3 = (f32[1,8192]{1,0:T(1,128)}, f32[1,8192]{1,0:T(1,128)S(1)}, u32[]{:S(2)}) copy-start(f32[1,8192]{1,0:T(1,128)S(1)} %add_add_fusion.1.refs_7_) | copy-start | bytes 98308
  72.1 4.5 %collective-permute-start.4 = (f32[1,8192]{1,0:T(1,128)S(1)}, f32[1,8192]{1,0:T(1,128)S(1)}, u32[]{:S(2)}, u32[]{:S(2)}) collective-permute-start(f32[1,8192]{1,0:T(1,128)S(1)} %add_add_fusion.1.refs_7_), channel_id=1, source_target_pairs={{0,8},{4,12},{8,0},{12,4},{16,24},{20,28},{24,16},{28,20},{1,9},{5... | collective-permute-start | bytes 98312 | tf_op jit(solution)/shard_map/ppermute | solution.py:277
  73.8 5.4 %collective-permute-start.5 = (f32[1,8192]{1,0:T(1,128)S(1)}, f32[1,8192]{1,0:T(1,128)S(1)}, u32[]{:S(2)}, u32[]{:S(2)}) collective-permute-start(f32[1,8192]{1,0:T(1,128)S(1)} %add_add_fusion.1.refs_7_), channel_id=1, source_target_pairs={{0,16},{4,20},{8,24},{12,28},{16,0},{20,4},{24,8},{28,12},{1,17},{... | collective-permute-start | bytes 98312 | tf_op jit(solution)/shard_map/ppermute | solution.py:277
  76.4 5.7 %collective-permute-start.6 = (f32[1,8192]{1,0:T(1,128)S(1)}, f32[1,8192]{1,0:T(1,128)S(1)}, u32[]{:S(2)}, u32[]{:S(2)}) collective-permute-start(f32[1,8192]{1,0:T(1,128)S(1)} %add_add_fusion.1.refs_7_), channel_id=1, source_target_pairs={{0,24},{4,28},{8,16},{12,20},{16,8},{20,12},{24,0},{28,4},{1,25},{... | collective-permute-start | bytes 98312 | tf_op jit(solution)/shard_map/ppermute | solution.py:277
  76.6 5.5 %copy-start.7 = (f32[1,8192]{1,0:T(1,128)}, f32[1,8192]{1,0:T(1,128)S(1)}, u32[]{:S(2)}) copy-start(f32[1,8192]{1,0:T(1,128)S(1)} %collective-permute-done.4.refs_8_) | copy-start | bytes 98308
  79.2 2.9 %copy-start.8 = (f32[1,8192]{1,0:T(1,128)}, f32[1,8192]{1,0:T(1,128)S(1)}, u32[]{:S(2)}) copy-start(f32[1,8192]{1,0:T(1,128)S(1)} %collective-permute-done.5.refs_9_) | copy-start | bytes 98308
  82.1 0.6 copy-start.9
  130.8 1.4 collective-permute-start.7
  133.0 5.2 %collective-permute-start.10 = (f32[1,8192]{1,0:T(1,128)S(1)}, f32[1,8192]{1,0:T(1,128)S(1)}, u32[]{:S(2)}, u32[]{:S(2)}) collective-permute-start(f32[1,8192]{1,0:T(1,128)S(1)} %add.115), channel_id=1, source_target_pairs={{0,3},{1,2},{2,1},{3,0},{4,7},{5,6},{6,5},{7,4},{8,11},{9,10},{10,... | collective-permute-start | bytes 98312 | tf_op jit(solution)/shard_map/ppermute | solution.py:277
  134.0 4.2 %collective-permute-start.8 = (f32[1,8192]{1,0:T(1,128)S(1)}, f32[1,8192]{1,0:T(1,128)S(1)}, u32[]{:S(2)}, u32[]{:S(2)}) collective-permute-start(f32[1,8192]{1,0:T(1,128)S(1)} %add.115), channel_id=1, source_target_pairs={{0,1},{1,0},{2,3},{3,2},{4,5},{5,4},{6,7},{7,6},{8,9},{9,8},{10,11... | collective-permute-start | bytes 98312 | tf_op jit(solution)/shard_map/ppermute | solution.py:277
  135.5 3.9 %collective-permute-start.9 = (f32[1,8192]{1,0:T(1,128)S(1)}, f32[1,8192]{1,0:T(1,128)S(1)}, u32[]{:S(2)}, u32[]{:S(2)}) collective-permute-start(f32[1,8192]{1,0:T(1,128)S(1)} %add.115), channel_id=1, source_target_pairs={{0,2},{1,3},{2,0},{3,1},{4,6},{5,7},{6,4},{7,5},{8,10},{9,11},{10,... | collective-permute-start | bytes 98312 | tf_op jit(solution)/shard_map/ppermute | solution.py:277
  139.5 6.7 %copy-start.2 = (f32[1,8192]{1,0:T(1,128)}, f32[1,8192]{1,0:T(1,128)S(1)}, u32[]{:S(2)}) copy-start(f32[1,8192]{1,0:T(1,128)S(1)} %add_add_fusion.refs_5_) | copy-start | bytes 98308
  139.5 4.5 %collective-permute-start.11 = (f32[1,8192]{1,0:T(1,128)S(1)}, f32[1,8192]{1,0:T(1,128)S(1)}, u32[]{:S(2)}, u32[]{:S(2)}) collective-permute-start(f32[1,8192]{1,0:T(1,128)S(1)} %add_add_fusion.refs_5_), channel_id=1, source_target_pairs={{0,8},{4,12},{8,0},{12,4},{16,24},{20,28},{24,16},{28,20},{1,9},{5... | collective-permute-start | bytes 98312 | tf_op jit(solution)/shard_map/ppermute | solution.py:277
  139.5 4.9 %collective-permute-start.12 = (f32[1,8192]{1,0:T(1,128)S(1)}, f32[1,8192]{1,0:T(1,128)S(1)}, u32[]{:S(2)}, u32[]{:S(2)}) collective-permute-start(f32[1,8192]{1,0:T(1,128)S(1)} %add_add_fusion.refs_5_), channel_id=1, source_target_pairs={{0,16},{4,20},{8,24},{12,28},{16,0},{20,4},{24,8},{28,12},{1,17},{... | collective-permute-start | bytes 98312 | tf_op jit(solution)/shard_map/ppermute | solution.py:277
  140.4 5.7 %collective-permute-start.13 = (f32[1,8192]{1,0:T(1,128)S(1)}, f32[1,8192]{1,0:T(1,128)S(1)}, u32[]{:S(2)}, u32[]{:S(2)}) collective-permute-start(f32[1,8192]{1,0:T(1,128)S(1)} %add_add_fusion.refs_5_), channel_id=1, source_target_pairs={{0,24},{4,28},{8,16},{12,20},{16,8},{20,12},{24,0},{28,4},{1,25},{... | collective-permute-start | bytes 98312 | tf_op jit(solution)/shard_map/ppermute | solution.py:277
  143.9 2.2 %copy-start.4 = (f32[1,8192]{1,0:T(1,128)}, f32[1,8192]{1,0:T(1,128)S(1)}, u32[]{:S(2)}) copy-start(f32[1,8192]{1,0:T(1,128)S(1)} %collective-permute-done.11.refs_6_) | copy-start | bytes 98308
  144.4 1.7 %copy-start.5 = (f32[1,8192]{1,0:T(1,128)}, f32[1,8192]{1,0:T(1,128)S(1)}, u32[]{:S(2)}) copy-start(f32[1,8192]{1,0:T(1,128)S(1)} %collective-permute-done.12.refs_7_) | copy-start | bytes 98308
  146.2 0.6 copy-start.6
  151.4 1.6 collective-permute-start.14
  154.1 4.5 %collective-permute-start.15 = (bf16[16,2048]{1,0:T(8,128)(2,1)S(1)}, bf16[16,2048]{1,0:T(8,128)(2,1)S(1)}, u32[]{:S(2)}, u32[]{:S(2)}) collective-permute-start(bf16[16,2048]{1,0:T(8,128)(2,1)S(1)} %get-tuple-element.52), channel_id=1, source_target_pairs={{0,8},{4,12},{8,0},{12,4},{16,24},{20,28},{24,16},{28,20},{1,9},{5... | collective-permute-start | bytes 196616 | tf_op jit(solution)/shard_map/ppermute | solution.py:277
  154.4 7.8 %collective-permute-start.16 = (bf16[16,2048]{1,0:T(8,128)(2,1)S(1)}, bf16[16,2048]{1,0:T(8,128)(2,1)S(1)}, u32[]{:S(2)}, u32[]{:S(2)}) collective-permute-start(bf16[16,2048]{1,0:T(8,128)(2,1)S(1)} %get-tuple-element.54), channel_id=1, source_target_pairs={{0,16},{4,20},{8,24},{12,28},{16,0},{20,4},{24,8},{28,12},{1,17},{... | collective-permute-start | bytes 196616 | tf_op jit(solution)/shard_map/ppermute | solution.py:277
  158.2 6.2 %collective-permute-start.17 = (bf16[16,2048]{1,0:T(8,128)(2,1)S(1)}, bf16[16,2048]{1,0:T(8,128)(2,1)S(1)}, u32[]{:S(2)}, u32[]{:S(2)}) collective-permute-start(bf16[16,2048]{1,0:T(8,128)(2,1)S(1)} %get-tuple-element.53), channel_id=1, source_target_pairs={{0,24},{4,28},{8,16},{12,20},{16,8},{20,12},{24,0},{28,4},{1,25},{... | collective-permute-start | bytes 196616 | tf_op jit(solution)/shard_map/ppermute | solution.py:277

commit v4 on v3

--- a/solution.py
+++ b/solution.py
@@ -14,6 +14,7 @@
 ROWS = 256
 CHUNK = 1024
 UNROLL = 8
+VMEM_BYTES = 24 << 20
 
 
 def grouping(levels, ncols):
@@ -272,6 +273,21 @@
                     ]
 
 
+def local_call(kernel, outs, args, name, scratch=(), scalars=1):
+    vmem = pl.BlockSpec(memory_space=pltpu.VMEM)
+    smem = pl.BlockSpec(memory_space=pltpu.SMEM)
+    kept = [a if i < scalars else pltpu.with_memory_space_constraint(a, pltpu.VMEM) for i, a in enumerate(args)]
+    return pl.pallas_call(
+        kernel,
+        out_shape=tuple(pltpu.VMEM(o.shape, o.dtype) for o in outs),
+        in_specs=[smem] * scalars + [vmem] * (len(args) - scalars),
+        out_specs=(vmem,) * len(outs),
+        scratch_shapes=list(scratch),
+        compiler_params=pltpu.CompilerParams(vmem_limit_bytes=VMEM_BYTES),
+        name=name,
+    )(*kept)
+
+
 def swap(x, axis, offset):
     n = lax.axis_size(axis)
     return lax.ppermute(x, axis, [(i, i ^ offset) for i in range(n)])
@@ -359,8 +375,6 @@
     )
     cols = block_cols.T
 
-    vmem = pl.BlockSpec(memory_space=pltpu.VMEM)
-    smem = pl.BlockSpec(memory_space=pltpu.SMEM)
     vector = jax.ShapeDtypeStruct((1, nobs), jnp.float32)
     number = jax.ShapeDtypeStruct((1, LANES), jnp.float32)
     moved_shape = jax.ShapeDtypeStruct((ncol, bands, ncols), jnp.bfloat16)
@@ -369,41 +383,33 @@
         count = len(seen)
         outs = (moved_shape, vector) + ((number, number, vector, vector, number) if count else ())
         extra = (list(before) if before is not None else []) + list(seen)
-        return pl.pallas_call(
+        return local_call(
             functools.partial(adjoint_kernel, seen=count, first=before is None),
-            out_shape=outs,
-            in_specs=[smem] + [vmem] * (6 + len(extra)),
-            out_specs=(vmem,) * len(outs),
-            scratch_shapes=[
-                pltpu.VMEM((rows, wide), jnp.float32),
-                pltpu.VMEM((levels, ncols), jnp.float32),
+            outs,
+            [starts, keys, weight, precision, errors, pert, vertical, *extra],
+            "adjoint",
+            [pltpu.VMEM((rows, wide), jnp.float32), pltpu.VMEM((levels, ncols), jnp.float32)],
+        )
+
+    def middle(moved):
+        return local_call(
+            horizontal_kernel,
+            (jax.ShapeDtypeStruct((bands, nodes), jnp.float32), moved_shape),
+            [cols, moved, mats],
+            "horizontal",
+            [
+                pltpu.VMEM((2 * pairs, bands, LANES), jnp.float32),
+                pltpu.VMEM((2, pairs, bands, LANES), jnp.float32),
+                pltpu.VMEM((2, pairs, bands, LANES), jnp.float32),
+                pltpu.VMEM((2, pairs, bands, LANES), jnp.bfloat16),
             ],
-            name="adjoint",
-        )(starts, keys, weight, precision, errors, pert, vertical, *extra)
-
-    middle = pl.pallas_call(
-        horizontal_kernel,
-        out_shape=(jax.ShapeDtypeStruct((bands, nodes), jnp.float32), moved_shape),
-        in_specs=[smem] + [vmem] * 2,
-        out_specs=(vmem, vmem),
-        scratch_shapes=[
-            pltpu.VMEM((2 * pairs, bands, LANES), jnp.float32),
-            pltpu.VMEM((2, pairs, bands, LANES), jnp.float32),
-            pltpu.VMEM((2, pairs, bands, LANES), jnp.float32),
-            pltpu.VMEM((2, pairs, bands, LANES), jnp.bfloat16),
-        ],
-        name="horizontal",
-    )
-    forward = pl.pallas_call(
-        forward_kernel,
-        out_shape=(
-            jax.ShapeDtypeStruct((levels // group, rows, wide), jnp.bfloat16),
-            vector,
-        ),
-        in_specs=[smem] + [vmem] * 5,
-        out_specs=(vmem, vmem),
-        name="forward",
-    )
+        )
+
+    def forward(columns):
+        field = jax.ShapeDtypeStruct((levels // group, rows, wide), jnp.bfloat16)
+        return local_call(
+            forward_kernel, (field, vector), [starts, keys, weight, columns, pert, vertical], "forward"
+        )
 
     errors, seen, before = value, (), None
     alphas, betas, fields, resids = [], [], [], []
@@ -415,9 +421,9 @@
             alphas.append(alpha)
             betas.append(beta)
         moved = lax.all_to_all(sent, "col", 0, 0, tiled=True)
-        resid, mixed = middle(cols, moved, mats)
+        resid, mixed = middle(moved)
         columns = lax.all_to_all(mixed, "col", 0, 0, tiled=True).reshape(levels, ncols)
-        field, partial = forward(starts, keys, weight, columns, pert, vertical)
+        field, partial = forward(columns)
         seen = shares_everywhere(partial)
         resids.append(resid)
         fields.append(field)
@@ -425,16 +431,16 @@
     split = slices % 16 == 0 and group % slices == 0
     field_shape = (2, nmem // 2, slices, ncols) if split else (levels, ncols)
     args = [precision, errors, *before, *seen, *alphas, *betas, *resids, *fields]
-    state, total = pl.pallas_call(
+    state, total = local_call(
         functools.partial(finish_kernel, seen=len(seen), group=group, wide=wide),
-        out_shape=(
+        (
             jax.ShapeDtypeStruct((bands, nodes), jnp.bfloat16),
             jax.ShapeDtypeStruct(field_shape, jnp.bfloat16),
         ),
-        in_specs=[vmem] * len(args),
-        out_specs=(vmem, vmem),
-        name="finish",
-    )(*args)
+        args,
+        "finish",
+        scalars=0,
+    )
     return (state[None], scatter_members(total))
 
 

time: 166 us -> 144 us (0.87)
  Pallas kernels: 54.4 us -> 40.7 us
  blocking collectives: 34.6 us -> 29.8 us
  waiting for transfers between devices: 27.6 us -> 24.7 us
  other arithmetic: 17.9 us -> 15.1 us
  local copies, waits for them, and re-layouts: 3.97 us -> 5.8 us
    pallas_call x7, Pallas kernels: 54.4 us -> 40.7 us  [local_call(): pl.pallas_call(kernel, out_shape=tuple((pltpu.VMEM(o.shape, o.dtype) for...]
    all_to_all x2, blocking collectives: 23.2 us -> 19.6 us  [per_device(): lax.all_to_all(mixed, 'col', 0, 0, tiled=True).reshape(levels, ncols)]
    unnamed x20 -> x15, local copies, waits for them, and re-layouts: 2.01 us -> 4.8 us
  transfers between devices with their start and end apart: 19 -> 19, of which waited for: 15 -> 15; matrix products, arithmetic and copies ran while one was open for 2% -> 4% of each run, Pallas kernels for 0% -> 0%
where the time goes in v4:
time: 144 us; the launch traced here: 143 us
  Pallas kernels  40.7 us (28%)
  blocking collectives  29.8 us (21%)
  starting transfers between devices  25.9 us (18%)
  waiting for transfers between devices  24.7 us (17%)
  other arithmetic  15.1 us (10%)
  local copies, waits for them, and re-layouts  5.8 us (4%)
    pallas_call x7, Pallas kernels, local_call(): pl.pallas_call(kernel, out_shape=tuple((pltpu.VMEM(o.shape, o.dtype) for...  40.7 us
    ppermute x18, waiting for transfers between devices, swap(): return lax.ppermute(x, axis, [(i, i ^ offset) for i in range(n)])  22.2 us
    ppermute x18, starting transfers between devices, swap(): return lax.ppermute(x, axis, [(i, i ^ offset) for i in range(n)])  20.7 us
    all_to_all x2, blocking collectives, per_device(): lax.all_to_all(mixed, 'col', 0, 0, tiled=True).reshape(levels, ncols)  19.6 us
    all_to_all x1, blocking collectives, per_device(): moved = lax.all_to_all(sent, 'col', 0, 0, tiled=True)  10.2 us
    sort x1, other arithmetic, per_device(): lax.sort((order, both, obs_weight, obs_value, obs_precision), num_keys=1,...  6.65 us
    all_to_all x1, starting transfers between devices, per_device(): moved = lax.all_to_all(sent, 'col', 0, 0, tiled=True)  5.19 us
    unnamed x15, local copies, waits for them, and re-layouts  4.8 us
  transfers between devices with their start and end apart: 19, of which 15 were waited for; matrix products, arithmetic and copies ran while one was open for 4% of the time, Pallas kernels for 0%

profile of v4, /device:TPU:0, one launch (start us, length us, event | category | flops | bytes accessed | tf_op | source)
XLA Modules:
  0.0 143.0 jit_solution(910985123846264047)
XLA Ops:
  0.6 1.0 slice_add_fusion
  1.6 0.8 iota_add_fusion
  2.4 1.0 convert_reduce_fusion.refs_0_.starts_ref
  3.4 6.7 %sort.33 = (s32[8192]{0:T(1024)S(1)}, s32[8192]{0:T(1024)S(1)}, f32[8192]{0:T(1024)S(1)}, f32[8192]{0:T(1024)S(1)}, f32[8192]{0:T(1024)S(1)}) sort(s32[8192]{0:T(1024)S(1)} %iota_add_fusion, s32[8192]{0:T(1024)S(1)} %bitcast.56, f32[8192]{0:T(1024)} %param.17, f32[8192]{0:T(1024)} %param.18, f32[8192]{0:T(1024)} %param.19), dimensions={0}, to_apply=%region_0.0 | sort | flops 106496 | bytes 327680 | tf_op jit(solution)/shard_map/sort | solution.py:351
  10.4 1.0 copy-done.2
  11.4 0.8 copy-done.4
  12.1 7.1 %adjoint.2 = (bf16[4,32,2048]{2,1,0:T(8,128)(2,1)}, f32[1,8192]{1,0:T(1,128)S(1)}) custom-call(s32[5]{0:T(128)S(1)} %convert_reduce_fusion.refs_0_.starts_ref, f32[4,8192]{1,0:T(4,128)S(1)} %add_convert_fusion.refs_1_.keys_ref, f32[1,8192]{1,0:T(1,128)S(1)} %bitcast.44, f32[1,8192]{1,0:T(1,128)S(1)} %bitcast.48, f32[1,8192]{1,0:T(1,128)S(1)} %bitcast.51, ...), custom_call_target="tpu_custom_call" | custom-call | tf_op jit(solution)/shard_map/adjoint/pallas_call | solution.py:280
  19.2 5.2 %all-to-all-start = ((bf16[4,32,2048]{2,1,0:T(8,128)(2,1)}), bf16[4,32,2048]{2,1,0:T(8,128)(2,1)S(1)}, u32[]{:S(2)}, u32[]{:S(2)}) async-start(bf16[4,32,2048]{2,1,0:T(8,128)(2,1)} %get-tuple-element.32), calls=%async_computation | async-start | bytes 1048576 | tf_op jit(solution)/shard_map/all_to_all | solution.py:423
  24.4 0.7 broadcast_in_dim.16
  25.2 2.2 %multiply_convert_fusion = bf16[128,64,128]{2,1,0:T(8,128)(2,1)S(1)} fusion(bf16[128,64,128]{2,1,0:T(8,128)(2,1)} %param.12, f32[128,128]{1,0:T(8,128)S(1)} %copy.16), kind=kLoop, calls=%fused_computation.5 | loop fusion | flops 3145728 | bytes 4259840 | tf_op jit(solution)/shard_map/convert_element_type | solution.py:366
  27.7 2.3 %fusion.2.mats_ref = bf16[64,128,256]{2,1,0:T(8,128)(2,1)} fusion(bf16[64,64,128]{2,1,0:T(8,128)(2,1)S(1)} %get-tuple-element.51, bf16[64,64,128]{2,1,0:T(8,128)(2,1)S(1)} %get-tuple-element.50), kind=kLoop, calls=%fused_computation.4 | loop fusion | flops 16777216 | bytes 6291456 | tf_op jit(solution)/shard_map/concatenate | solution.py:369
  29.9 2.5 %all-to-all-done.moved_ref = bf16[4,32,2048]{2,1,0:T(8,128)(2,1)S(1)} async-done(((bf16[4,32,2048]{2,1,0:T(8,128)(2,1)}), bf16[4,32,2048]{2,1,0:T(8,128)(2,1)S(1)}, u32[]{:S(2)}, u32[]{:S(2)}) %all-to-all-start) | async-done | bytes 524320 | tf_op jit(solution)/shard_map/all_to_all | solution.py:423
  32.5 2.2 %copy-done = bf16[64,128,256]{2,1,0:T(8,128)(2,1)S(1)} copy-done((bf16[64,128,256]{2,1,0:T(8,128)(2,1)S(1)}, bf16[64,128,256]{2,1,0:T(8,128)(2,1)}, u32[]{:S(2)}) %copy-start) | copy-done | bytes 4194328
  34.6 7.0 %horizontal.2 = (f32[32,8192]{1,0:T(8,128)S(1)}, bf16[4,32,2048]{2,1,0:T(8,128)(2,1)S(1)}) custom-call(s32[2,128]{1,0:T(2,128)S(1)} %bitcast.52, bf16[4,32,2048]{2,1,0:T(8,128)(2,1)S(1)} %all-to-all-done.moved_ref, bf16[64,128,256]{2,1,0:T(8,128)(2,1)S(1)} %copy-done), custom_call_target="tpu_custom_call" | custom-call | tf_op jit(solution)/shard_map/horizontal/pallas_call | solution.py:280
  41.6 10.1 %all_to_all.20 = bf16[4,32,2048]{2,1,0:T(8,128)(2,1)S(1)} all-to-all(bf16[4,32,2048]{2,1,0:T(8,128)(2,1)S(1)} %get-tuple-element.33), channel_id=1, replica_groups=mesh['mem'=8,'col'=4] {'col'}, dimensions={0} | all-to-all | bytes 1048576 | tf_op jit(solution)/shard_map/all_to_all | solution.py:425
  51.8 6.1 %forward.2 = (bf16[4,256,256]{2,1,0:T(8,128)(2,1)S(1)}, f32[1,8192]{1,0:T(1,128)S(1)}) custom-call(s32[5]{0:T(128)S(1)} %convert_reduce_fusion.refs_0_.starts_ref, f32[4,8192]{1,0:T(4,128)S(1)} %add_convert_fusion.refs_1_.keys_ref, f32[1,8192]{1,0:T(1,128)S(1)} %bitcast.45, bf16[128,2048]{1,0:T(8,128)(2,1)S(1)} %bitcast.43, bf16[128,2048]{1,0:T(8,128)(2,1)S(1)} %bitcast.39, ...), custom_call_target="tpu_custom_call" | custom-call | tf_op jit(solution)/shard_map/forward/pallas_call | solution.py:280
  57.9 1.2 collective-permute-done
  59.2 1.0 collective-permute-start.1
  60.2 0.6 collective-permute-start.2
  60.7 2.0 %collective-permute-start.3 = (f32[1,8192]{1,0:T(1,128)S(1)}, f32[1,8192]{1,0:T(1,128)S(1)}, u32[]{:S(2)}, u32[]{:S(2)}) collective-permute-start(f32[1,8192]{1,0:T(1,128)S(1)} %add.111), channel_id=1, source_target_pairs={{0,3},{1,2},{2,1},{3,0},{4,7},{5,6},{6,5},{7,4},{8,11},{9,10},{10,... | collective-permute-start | bytes 98312 | tf_op jit(solution)/shard_map/ppermute | solution.py:293
  63.2 1.3 collective-permute-done.2
  64.4 1.1 collective-permute-done.3
  65.6 1.6 %collective-permute-start.4 = (f32[1,8192]{1,0:T(1,128)S(1)}, f32[1,8192]{1,0:T(1,128)S(1)}, u32[]{:S(2)}, u32[]{:S(2)}) collective-permute-start(f32[1,8192]{1,0:T(1,128)S(1)} %add_add_fusion.1.refs_7_), channel_id=1, source_target_pairs={{0,8},{4,12},{8,0},{12,4},{16,24},{20,28},{24,16},{28,20},{1,9},{5... | collective-permute-start | bytes 98312 | tf_op jit(solution)/shard_map/ppermute | solution.py:293
  67.3 2.6 %collective-permute-start.5 = (f32[1,8192]{1,0:T(1,128)S(1)}, f32[1,8192]{1,0:T(1,128)S(1)}, u32[]{:S(2)}, u32[]{:S(2)}) collective-permute-start(f32[1,8192]{1,0:T(1,128)S(1)} %add_add_fusion.1.refs_7_), channel_id=1, source_target_pairs={{0,16},{4,20},{8,24},{12,28},{16,0},{20,4},{24,8},{28,12},{1,17},{... | collective-permute-start | bytes 98312 | tf_op jit(solution)/shard_map/ppermute | solution.py:293
  70.1 2.6 %collective-permute-done.5.refs_9_ = f32[1,8192]{1,0:T(1,128)S(1)} collective-permute-done((f32[1,8192]{1,0:T(1,128)S(1)}, f32[1,8192]{1,0:T(1,128)S(1)}, u32[]{:S(2)}, u32[]{:S(2)}) %collective-permute-start.5) | collective-permute-done | bytes 32800 | tf_op jit(solution)/shard_map/ppermute | solution.py:293
  72.7 2.9 %collective-permute-done.6.refs_10_ = f32[1,8192]{1,0:T(1,128)S(1)} collective-permute-done((f32[1,8192]{1,0:T(1,128)S(1)}, f32[1,8192]{1,0:T(1,128)S(1)}, u32[]{:S(2)}, u32[]{:S(2)}) %collective-permute-start.6) | collective-permute-done | bytes 32800 | tf_op jit(solution)/shard_map/ppermute | solution.py:293
  75.5 6.5 %adjoint.3 = (bf16[4,32,2048]{2,1,0:T(8,128)(2,1)S(1)}, f32[1,8192]{1,0:T(1,128)S(1)}, f32[1,128]{1,0:T(1,128)S(1)}, f32[1,128]{1,0:T(1,128)S(1)}, f32[1,8192]{1...) custom-call(s32[5]{0:T(128)S(1)} %convert_reduce_fusion.refs_0_.starts_ref, ...), custom_call_target="tpu_custom_call" | custom-call | tf_op jit(solution)/shard_map/adjoint/pallas_call | solution.py:280
  82.1 10.2 %all_to_all.21.moved_ref = bf16[4,32,2048]{2,1,0:T(8,128)(2,1)S(1)} all-to-all(bf16[4,32,2048]{2,1,0:T(8,128)(2,1)S(1)} %get-tuple-element.39), channel_id=1, replica_groups=mesh['mem'=8,'col'=4] {'col'}, dimensions={0} | all-to-all | bytes 1048576 | tf_op jit(solution)/shard_map/all_to_all | solution.py:423
  92.3 7.0 %horizontal.3 = (f32[32,8192]{1,0:T(8,128)S(1)}, bf16[4,32,2048]{2,1,0:T(8,128)(2,1)S(1)}) custom-call(s32[2,128]{1,0:T(2,128)S(1)} %bitcast.53, bf16[4,32,2048]{2,1,0:T(8,128)(2,1)S(1)} %all_to_all.21.moved_ref, bf16[64,128,256]{2,1,0:T(8,128)(2,1)S(1)} %copy-done.1), custom_call_target="tpu_custom_call" | custom-call | tf_op jit(solution)/shard_map/horizontal/pallas_call | solution.py:280
  99.3 9.5 %all_to_all.22 = bf16[4,32,2048]{2,1,0:T(8,128)(2,1)S(1)} all-to-all(bf16[4,32,2048]{2,1,0:T(8,128)(2,1)S(1)} %get-tuple-element.40), channel_id=1, replica_groups=mesh['mem'=8,'col'=4] {'col'}, dimensions={0} | all-to-all | bytes 1048576 | tf_op jit(solution)/shard_map/all_to_all | solution.py:425
  108.8 6.1 %forward.3 = (bf16[4,256,256]{2,1,0:T(8,128)(2,1)S(1)}, f32[1,8192]{1,0:T(1,128)S(1)}) custom-call(s32[5]{0:T(128)S(1)} %convert_reduce_fusion.refs_0_.starts_ref, f32[4,8192]{1,0:T(4,128)S(1)} %add_convert_fusion.refs_1_.keys_ref, f32[1,8192]{1,0:T(1,128)S(1)} %bitcast.47, bf16[128,2048]{1,0:T(8,128)(2,1)S(1)} %bitcast.42, bf16[128,2048]{1,0:T(8,128)(2,1)S(1)} %bitcast.41, ...), custom_call_target="tpu_custom_call" | custom-call | tf_op jit(solution)/shard_map/forward/pallas_call | solution.py:280
  115.0 1.2 collective-permute-done.7
  116.2 1.0 collective-permute-start.10
  117.2 1.5 %collective-permute-start.8 = (f32[1,8192]{1,0:T(1,128)S(1)}, f32[1,8192]{1,0:T(1,128)S(1)}, u32[]{:S(2)}, u32[]{:S(2)}) collective-permute-start(f32[1,8192]{1,0:T(1,128)S(1)} %add.115), channel_id=1, source_target_pairs={{0,1},{1,0},{2,3},{3,2},{4,5},{5,4},{6,7},{7,6},{8,9},{9,8},{10,11... | collective-permute-start | bytes 98312 | tf_op jit(solution)/shard_map/ppermute | solution.py:293
  118.7 1.1 collective-permute-start.9
  119.8 1.6 %collective-permute-done.10 = f32[1,8192]{1,0:T(1,128)S(1)} collective-permute-done((f32[1,8192]{1,0:T(1,128)S(1)}, f32[1,8192]{1,0:T(1,128)S(1)}, u32[]{:S(2)}, u32[]{:S(2)}) %collective-permute-start.10) | collective-permute-done | bytes 32800 | tf_op jit(solution)/shard_map/ppermute | solution.py:293
  121.4 1.2 collective-permute-done.9
  122.8 0.9 collective-permute-start.12
  123.6 3.5 %collective-permute-start.13 = (f32[1,8192]{1,0:T(1,128)S(1)}, f32[1,8192]{1,0:T(1,128)S(1)}, u32[]{:S(2)}, u32[]{:S(2)}) collective-permute-start(f32[1,8192]{1,0:T(1,128)S(1)} %add_add_fusion.refs_5_), channel_id=1, source_target_pairs={{0,24},{4,28},{8,16},{12,20},{16,8},{20,12},{24,0},{28,4},{1,25},{... | collective-permute-start | bytes 98312 | tf_op jit(solution)/shard_map/ppermute | solution.py:293
  127.1 0.5 collective-permute-done.12.refs_7_
  127.6 1.7 %collective-permute-done.13.refs_8_ = f32[1,8192]{1,0:T(1,128)S(1)} collective-permute-done((f32[1,8192]{1,0:T(1,128)S(1)}, f32[1,8192]{1,0:T(1,128)S(1)}, u32[]{:S(2)}, u32[]{:S(2)}) %collective-permute-start.13) | collective-permute-done | bytes 32800 | tf_op jit(solution)/shard_map/ppermute | solution.py:293
  129.4 0.9 finish.1
  130.4 1.5 %collective-permute-done.14 = bf16[4,16,2048]{2,1,0:T(8,128)(2,1)S(1)} collective-permute-done((bf16[4,16,2048]{2,1,0:T(8,128)(2,1)S(1)}, bf16[4,16,2048]{2,1,0:T(8,128)(2,1)S(1)}, u32[]{:S(2)}, u32[]{:S(2)}) %collective-permute-start.14) | collective-permute-done | bytes 262176 | tf_op jit(solution)/shard_map/ppermute | solution.py:293
  132.3 3.8 %collective-permute-start.16 = (bf16[16,2048]{1,0:T(8,128)(2,1)S(1)}, bf16[16,2048]{1,0:T(8,128)(2,1)S(1)}, u32[]{:S(2)}, u32[]{:S(2)}) collective-permute-start(bf16[16,2048]{1,0:T(8,128)(2,1)S(1)} %get-tuple-element.54), channel_id=1, source_target_pairs={{0,16},{4,20},{8,24},{12,28},{16,0},{20,4},{24,8},{28,12},{1,17},{... | collective-permute-start | bytes 196616 | tf_op jit(solution)/shard_map/ppermute | solution.py:293
  136.5 0.8 copy.21
  137.3 2.9 %collective-permute-done.16 = bf16[16,2048]{1,0:T(8,128)(2,1)S(1)} collective-permute-done((bf16[16,2048]{1,0:T(8,128)(2,1)S(1)}, bf16[16,2048]{1,0:T(8,128)(2,1)S(1)}, u32[]{:S(2)}, u32[]{:S(2)}) %collective-permute-start.16) | collective-permute-done | bytes 65568 | tf_op jit(solution)/shard_map/ppermute | solution.py:293
  140.1 2.1 %collective-permute-done.17 = bf16[16,2048]{1,0:T(8,128)(2,1)S(1)} collective-permute-done((bf16[16,2048]{1,0:T(8,128)(2,1)S(1)}, bf16[16,2048]{1,0:T(8,128)(2,1)S(1)}, u32[]{:S(2)}, u32[]{:S(2)}) %collective-permute-start.17) | collective-permute-done | bytes 65568 | tf_op jit(solution)/shard_map/ppermute | solution.py:293
  142.3 0.7 fusion.5
  (35 shorter events, 2.5 us)
Async XLA Ops:
  10.3 1.0 copy-start.2
  11.4 0.8 copy-start.4
  19.2 13.2 %all-to-all-start = ((bf16[4,32,2048]{2,1,0:T(8,128)(2,1)}), bf16[4,32,2048]{2,1,0:T(8,128)(2,1)S(1)}, u32[]{:S(2)}, u32[]{:S(2)}) async-start(bf16[4,32,2048]{2,1,0:T(8,128)(2,1)} %get-tuple-element.32), calls=%async_computation | async-start | bytes 1048576 | tf_op jit(solution)/shard_map/all_to_all | solution.py:423
  27.6 4.8 %copy-start.6 = (s32[128,2]{0,1:T(2,128)S(1)}, s32[128,2]{0,1:T(2,128)}, u32[]{:S(2)}) copy-start(s32[128,2]{0,1:T(2,128)} %param.14) | copy-start | bytes 3076
  27.6 24.1 %copy-start.3 = (bf16[1,128,2048]{2,1,0:T(8,128)(2,1)S(1)}, bf16[1,128,2048]{2,1,0:T(8,128)(2,1)}, u32[]{:S(2)}) copy-start(bf16[1,128,2048]{2,1,0:T(8,128)(2,1)} %param.10) | copy-start | bytes 1572868
  27.6 24.1 %copy-start.5 = (bf16[128,128]{1,0:T(8,128)(2,1)S(1)}, bf16[128,128]{1,0:T(8,128)(2,1)}, u32[]{:S(2)}) copy-start(bf16[128,128]{1,0:T(8,128)(2,1)} %vert_ref.3) | copy-start | bytes 98308
  32.5 2.2 %copy-start = (bf16[64,128,256]{2,1,0:T(8,128)(2,1)S(1)}, bf16[64,128,256]{2,1,0:T(8,128)(2,1)}, u32[]{:S(2)}) copy-start(bf16[64,128,256]{2,1,0:T(8,128)(2,1)} %fusion.2.mats_ref) | copy-start | bytes 12582916
  34.6 57.6 %copy-start.1 = (bf16[64,128,256]{2,1,0:T(8,128)(2,1)S(1)}, bf16[64,128,256]{2,1,0:T(8,128)(2,1)}, u32[]{:S(2)}) copy-start(bf16[64,128,256]{2,1,0:T(8,128)(2,1)} %fusion.2.mats_ref) | copy-start | bytes 12582916
  57.9 1.3 collective-permute-start
  59.2 4.0 %collective-permute-start.1 = (f32[1,8192]{1,0:T(1,128)S(1)}, f32[1,8192]{1,0:T(1,128)S(1)}, u32[]{:S(2)}, u32[]{:S(2)}) collective-permute-start(f32[1,8192]{1,0:T(1,128)S(1)} %add.111), channel_id=1, source_target_pairs={{0,1},{1,0},{2,3},{3,2},{4,5},{5,4},{6,7},{7,6},{8,9},{9,8},{10,11... | collective-permute-start | bytes 98312 | tf_op jit(solution)/shard_map/ppermute | solution.py:293
  60.2 4.3 %collective-permute-start.2 = (f32[1,8192]{1,0:T(1,128)S(1)}, f32[1,8192]{1,0:T(1,128)S(1)}, u32[]{:S(2)}, u32[]{:S(2)}) collective-permute-start(f32[1,8192]{1,0:T(1,128)S(1)} %add.111), channel_id=1, source_target_pairs={{0,2},{1,3},{2,0},{3,1},{4,6},{5,7},{6,4},{7,5},{8,10},{9,11},{10,... | collective-permute-start | bytes 98312 | tf_op jit(solution)/shard_map/ppermute | solution.py:293
  60.7 4.8 %collective-permute-start.3 = (f32[1,8192]{1,0:T(1,128)S(1)}, f32[1,8192]{1,0:T(1,128)S(1)}, u32[]{:S(2)}, u32[]{:S(2)}) collective-permute-start(f32[1,8192]{1,0:T(1,128)S(1)} %add.111), channel_id=1, source_target_pairs={{0,3},{1,2},{2,1},{3,0},{4,7},{5,6},{6,5},{7,4},{8,11},{9,10},{10,... | collective-permute-start | bytes 98312 | tf_op jit(solution)/shard_map/ppermute | solution.py:293
  65.6 4.5 %collective-permute-start.4 = (f32[1,8192]{1,0:T(1,128)S(1)}, f32[1,8192]{1,0:T(1,128)S(1)}, u32[]{:S(2)}, u32[]{:S(2)}) collective-permute-start(f32[1,8192]{1,0:T(1,128)S(1)} %add_add_fusion.1.refs_7_), channel_id=1, source_target_pairs={{0,8},{4,12},{8,0},{12,4},{16,24},{20,28},{24,16},{28,20},{1,9},{5... | collective-permute-start | bytes 98312 | tf_op jit(solution)/shard_map/ppermute | solution.py:293
  67.3 5.4 %collective-permute-start.5 = (f32[1,8192]{1,0:T(1,128)S(1)}, f32[1,8192]{1,0:T(1,128)S(1)}, u32[]{:S(2)}, u32[]{:S(2)}) collective-permute-start(f32[1,8192]{1,0:T(1,128)S(1)} %add_add_fusion.1.refs_7_), channel_id=1, source_target_pairs={{0,16},{4,20},{8,24},{12,28},{16,0},{20,4},{24,8},{28,12},{1,17},{... | collective-permute-start | bytes 98312 | tf_op jit(solution)/shard_map/ppermute | solution.py:293
  69.8 5.7 %collective-permute-start.6 = (f32[1,8192]{1,0:T(1,128)S(1)}, f32[1,8192]{1,0:T(1,128)S(1)}, u32[]{:S(2)}, u32[]{:S(2)}) collective-permute-start(f32[1,8192]{1,0:T(1,128)S(1)} %add_add_fusion.1.refs_7_), channel_id=1, source_target_pairs={{0,24},{4,28},{8,16},{12,20},{16,8},{20,12},{24,0},{28,4},{1,25},{... | collective-permute-start | bytes 98312 | tf_op jit(solution)/shard_map/ppermute | solution.py:293
  114.9 1.3 collective-permute-start.7
  116.2 5.2 %collective-permute-start.10 = (f32[1,8192]{1,0:T(1,128)S(1)}, f32[1,8192]{1,0:T(1,128)S(1)}, u32[]{:S(2)}, u32[]{:S(2)}) collective-permute-start(f32[1,8192]{1,0:T(1,128)S(1)} %add.115), channel_id=1, source_target_pairs={{0,3},{1,2},{2,1},{3,0},{4,7},{5,6},{6,5},{7,4},{8,11},{9,10},{10,... | collective-permute-start | bytes 98312 | tf_op jit(solution)/shard_map/ppermute | solution.py:293
  117.2 4.2 %collective-permute-start.8 = (f32[1,8192]{1,0:T(1,128)S(1)}, f32[1,8192]{1,0:T(1,128)S(1)}, u32[]{:S(2)}, u32[]{:S(2)}) collective-permute-start(f32[1,8192]{1,0:T(1,128)S(1)} %add.115), channel_id=1, source_target_pairs={{0,1},{1,0},{2,3},{3,2},{4,5},{5,4},{6,7},{7,6},{8,9},{9,8},{10,11... | collective-permute-start | bytes 98312 | tf_op jit(solution)/shard_map/ppermute | solution.py:293
  118.7 3.9 %collective-permute-start.9 = (f32[1,8192]{1,0:T(1,128)S(1)}, f32[1,8192]{1,0:T(1,128)S(1)}, u32[]{:S(2)}, u32[]{:S(2)}) collective-permute-start(f32[1,8192]{1,0:T(1,128)S(1)} %add.115), channel_id=1, source_target_pairs={{0,2},{1,3},{2,0},{3,1},{4,6},{5,7},{6,4},{7,5},{8,10},{9,11},{10,... | collective-permute-start | bytes 98312 | tf_op jit(solution)/shard_map/ppermute | solution.py:293
  122.7 4.5 %collective-permute-start.11 = (f32[1,8192]{1,0:T(1,128)S(1)}, f32[1,8192]{1,0:T(1,128)S(1)}, u32[]{:S(2)}, u32[]{:S(2)}) collective-permute-start(f32[1,8192]{1,0:T(1,128)S(1)} %add_add_fusion.refs_5_), channel_id=1, source_target_pairs={{0,8},{4,12},{8,0},{12,4},{16,24},{20,28},{24,16},{28,20},{1,9},{5... | collective-permute-start | bytes 98312 | tf_op jit(solution)/shard_map/ppermute | solution.py:293
  122.8 4.9 %collective-permute-start.12 = (f32[1,8192]{1,0:T(1,128)S(1)}, f32[1,8192]{1,0:T(1,128)S(1)}, u32[]{:S(2)}, u32[]{:S(2)}) collective-permute-start(f32[1,8192]{1,0:T(1,128)S(1)} %add_add_fusion.refs_5_), channel_id=1, source_target_pairs={{0,16},{4,20},{8,24},{12,28},{16,0},{20,4},{24,8},{28,12},{1,17},{... | collective-permute-start | bytes 98312 | tf_op jit(solution)/shard_map/ppermute | solution.py:293
  123.6 5.7 %collective-permute-start.13 = (f32[1,8192]{1,0:T(1,128)S(1)}, f32[1,8192]{1,0:T(1,128)S(1)}, u32[]{:S(2)}, u32[]{:S(2)}) collective-permute-start(f32[1,8192]{1,0:T(1,128)S(1)} %add_add_fusion.refs_5_), channel_id=1, source_target_pairs={{0,24},{4,28},{8,16},{12,20},{16,8},{20,12},{24,0},{28,4},{1,25},{... | collective-permute-start | bytes 98312 | tf_op jit(solution)/shard_map/ppermute | solution.py:293
  130.3 1.6 %collective-permute-start.14 = (bf16[4,16,2048]{2,1,0:T(8,128)(2,1)S(1)}, bf16[4,16,2048]{2,1,0:T(8,128)(2,1)S(1)}, u32[]{:S(2)}, u32[]{:S(2)}) collective-permute-start(bf16[4,16,2048]{2,1,0:T(8,128)(2,1)S(1)} %slice_bitcast_fusion.2), channel_id=1, source_target_pairs={{0,4},{4,0},{8,12},{12,8},{16,20},{20,16},{24,28},{28,24},{1,5},{5... | collective-permute-start | bytes 786440 | tf_op jit(solution)/shard_map/ppermute | solution.py:293
  132.0 5.2 %collective-permute-start.15 = (bf16[16,2048]{1,0:T(8,128)(2,1)S(1)}, bf16[16,2048]{1,0:T(8,128)(2,1)S(1)}, u32[]{:S(2)}, u32[]{:S(2)}) collective-permute-start(bf16[16,2048]{1,0:T(8,128)(2,1)S(1)} %get-tuple-element.52), channel_id=1, source_target_pairs={{0,8},{4,12},{8,0},{12,4},{16,24},{20,28},{24,16},{28,20},{1,9},{5... | collective-permute-start | bytes 196616 | tf_op jit(solution)/shard_map/ppermute | solution.py:293
  132.3 7.8 %collective-permute-start.16 = (bf16[16,2048]{1,0:T(8,128)(2,1)S(1)}, bf16[16,2048]{1,0:T(8,128)(2,1)S(1)}, u32[]{:S(2)}, u32[]{:S(2)}) collective-permute-start(bf16[16,2048]{1,0:T(8,128)(2,1)S(1)} %get-tuple-element.54), channel_id=1, source_target_pairs={{0,16},{4,20},{8,24},{12,28},{16,0},{20,4},{24,8},{28,12},{1,17},{... | collective-permute-start | bytes 196616 | tf_op jit(solution)/shard_map/ppermute | solution.py:293
  136.1 6.2 %collective-permute-start.17 = (bf16[16,2048]{1,0:T(8,128)(2,1)S(1)}, bf16[16,2048]{1,0:T(8,128)(2,1)S(1)}, u32[]{:S(2)}, u32[]{:S(2)}) collective-permute-start(bf16[16,2048]{1,0:T(8,128)(2,1)S(1)} %get-tuple-element.53), channel_id=1, source_target_pairs={{0,24},{4,28},{8,16},{12,20},{16,8},{20,12},{24,0},{28,4},{1,25},{... | collective-permute-start | bytes 196616 | tf_op jit(solution)/shard_map/ppermute | solution.py:293

commit v5 on v4

--- a/solution.py
+++ b/solution.py
@@ -10,10 +10,12 @@
 
 ITERS = 2
 LANES = 128
+SUBLANES = 16
 WIDE = 256
 ROWS = 256
-CHUNK = 1024
-UNROLL = 8
+FIRST = 768
+SECOND = 256
+TILES = 8
 VMEM_BYTES = 24 << 20
 
 
@@ -34,8 +36,34 @@
     return lax.broadcasted_iota(jnp.int32, (rows, n), 0).astype(jnp.float32).astype(jnp.bfloat16)
 
 
-def span_of(c):
-    return pl.ds(pl.multiple_of(c * CHUNK, CHUNK), CHUNK)
+def runs_of(starts_ref, g, mine, ncol):
+    runs = [(0, starts_ref[(g * ncol + mine) * ncol], starts_ref[(g * ncol + mine + 1) * ncol])]
+    for other in range(ncol):
+        at = (g * ncol + other) * ncol + mine
+        runs.append((1, starts_ref[at], starts_ref[at + 1]))
+    return runs
+
+
+def width_of(which):
+    return SECOND if which else FIRST
+
+
+def trips_of(runs):
+    trips = jnp.int32(0)
+    for which, low, end in runs:
+        need = (end - (low // LANES) * LANES + width_of(which) - 1) // width_of(which)
+        trips = jnp.maximum(trips, jnp.where(end > low, need, 0))
+    return trips
+
+
+def window_of(run, trip, nobs):
+    which, low, end = run
+    width = width_of(which)
+    first = (low // LANES) * LANES + trip * width
+    base = pl.multiple_of(jnp.minimum(first, nobs - width), LANES)
+    place = base + lax.broadcasted_iota(jnp.int32, (1, width), 1)
+    valid = (place >= jnp.maximum(low, first)) & (place < jnp.minimum(end, first + width))
+    return pl.ds(base, width), valid
 
 
 def total_of(x):
@@ -58,9 +86,16 @@
 
 
 def adjoint_kernel(*refs, seen, first):
-    starts_ref, keys_ref, weight_ref, precision_ref, err_ref, pert_ref, vert_ref = refs[:7]
-    refs = refs[7:]
+    starts_ref, pert_hbm, vert_hbm, keys_ref, weight_ref, precision_ref, err_ref = refs[:7]
+    pert_ref, vert_ref, sems = refs[-3:]
+    refs = refs[7:-3]
     levels, ncols = pert_ref.shape
+    copies = [
+        pltpu.make_async_copy(pert_hbm, pert_ref, sems.at[0]),
+        pltpu.make_async_copy(vert_hbm, vert_ref, sems.at[1]),
+    ]
+    for copy in copies:
+        copy.start()
     members = lax.axis_size("mem")
     wide, chunks, group = grouping(levels, ncols)
     rows = chunks * group
@@ -81,23 +116,26 @@
         out_ref, new_ref, total, field = refs
         new_ref[...] = precision_ref[...] * err_ref[...]
     bands = out_ref.shape[1]
-    numbers = row_numbers(rows, CHUNK)
-    places = row_numbers(wide, CHUNK)
-    ones = jnp.ones((1, CHUNK), jnp.bfloat16)
+    nobs = weight_ref.shape[1]
+    ncol = lax.axis_size("col")
+    mine = lax.axis_index("col")
 
     def collect(g, carry):
         total[...] = jnp.zeros_like(total)
-        base = (g * rows).astype(jnp.float32)
-
-        def step(c, carry):
-            span = span_of(c)
-            weight = weight_ref[:, span]
-            err = new_ref[:, span]
+        runs = runs_of(starts_ref, g, mine, ncol)
+
+        def step(trip, carry):
             above, beside = [], []
-            for which, w in ((0, weight), (1, 1.0 - weight)):
-                row = keys_ref[2 * which : 2 * which + 1, span] - base
-                above.append(one_hot(row, numbers, (w * err).astype(jnp.bfloat16)))
-                beside.append(one_hot(keys_ref[2 * which + 1 : 2 * which + 2, span], places, ones))
+            for run in runs:
+                which = run[0]
+                span, valid = window_of(run, trip, nobs)
+                weight = weight_ref[:, span]
+                weight = 1.0 - weight if which else weight
+                row = jnp.where(valid, keys_ref[2 * which : 2 * which + 1, span], -1.0)
+                lane = keys_ref[2 * which + 1 : 2 * which + 2, span]
+                width = width_of(which)
+                above.append(one_hot(row, row_numbers(rows, width), (weight * new_ref[:, span]).astype(jnp.bfloat16)))
+                beside.append(one_hot(lane, row_numbers(wide, width), jnp.ones((1, width), jnp.bfloat16)))
             total[...] += lax.dot_general(
                 jnp.concatenate(above, axis=1),
                 jnp.concatenate(beside, axis=1),
@@ -106,7 +144,7 @@
             )
             return carry
 
-        lax.fori_loop(starts_ref[g] // CHUNK, (starts_ref[g + 1] + CHUNK - 1) // CHUNK, step, 0)
+        lax.fori_loop(0, trips_of(runs), step, 0)
         here = pl.ds(pl.multiple_of(g * group, group), group)
         for c in range(chunks):
             field[here, c * wide : (c + 1) * wide] = total[c * group : (c + 1) * group, :]
@@ -114,6 +152,8 @@
 
     lax.fori_loop(0, levels // group, collect, 0)
 
+    for copy in copies:
+        copy.wait()
     scale_inv = 1.0 / math.sqrt(members)
     for c in range(chunks):
         part = slice(c * wide, (c + 1) * wide)
@@ -125,69 +165,94 @@
             out_ref[b, :, part] = turned[b * bands : (b + 1) * bands, :].astype(jnp.bfloat16)
 
 
-def horizontal_kernel(cols_ref, moved_ref, mats_ref, resid_ref, mixed_ref, terms, first, second, picked):
+def horizontal_kernel(
+    spots_ref, moved_ref, mats_ref, resid_ref, mixed_ref, terms, first, second, picked
+):
     parts, bands, ncols = moved_ref.shape
     pairs = mats_ref.shape[0]
     per_part = ncols // LANES
+    group = terms.shape[1] // 2
     half = LANES // 2
     lane = lax.broadcasted_iota(jnp.int32, (bands, LANES), 1)
     low = lane < half
     low16 = lane.astype(jnp.float32).astype(jnp.bfloat16) < half
     sums = (first, second)
+
     for s in sums:
         s[...] = jnp.zeros_like(s)
 
-    def tile_of(p):
-        at = pl.multiple_of((p % per_part) * LANES, LANES)
-        return p // per_part, pl.ds(at, LANES)
-
-    def product(p, carry):
-        part, lanes = tile_of(p)
-        both = jnp.dot(moved_ref[part, :, lanes], mats_ref[p], preferred_element_type=jnp.float32)
-        terms[2 * p] = both[:, :LANES]
-        terms[2 * p + 1] = both[:, LANES:]
-        return carry
-
-    lax.fori_loop(0, pairs, product, 0, unroll=UNROLL)
-
-    def scatter(i, carry):
-        term = terms[i]
-        for k in range(2):
-            col = cols_ref[k, i]
-            sums[k][(col & 1) ^ k, col >> 1] += term
-        return carry
-
-    lax.fori_loop(0, 2 * pairs, scatter, 0, unroll=UNROLL)
-
-    def join(p, carry):
-        part, lanes = tile_of(p)
-        here = jnp.where(low, first[0, p], second[0, p])
-        there = jnp.where(low, first[1, p], second[1, p])
-        resid = moved_ref[part, :, lanes].astype(jnp.float32) + here + pltpu.roll(there, half, 1)
-        resid_ref[:, pl.ds(pl.multiple_of(p * LANES, LANES), LANES)] = resid
-        picked[0, p] = resid.astype(jnp.bfloat16)
-        picked[1, p] = pltpu.roll(resid, half, 1).astype(jnp.bfloat16)
-        return carry
-
-    lax.fori_loop(0, pairs, join, 0, unroll=UNROLL)
-
-    def gather(p, carry):
-        part, lanes = tile_of(p)
-        sources = []
-        for q in range(2):
-            one = cols_ref[0, 2 * p + q]
-            two = cols_ref[1, 2 * p + q]
-            sources.append(jnp.where(low16, picked[one & 1, one >> 1], picked[(two & 1) ^ 1, two >> 1]))
-        both = lax.dot_general(
-            jnp.concatenate(sources, axis=1),
-            mats_ref[p],
-            (((1,), (1,)), ((), ())),
-            preferred_element_type=jnp.float32,
-        )
-        mixed_ref[part, :, lanes] = (picked[0, p].astype(jnp.float32) + both).astype(jnp.bfloat16)
-        return carry
-
-    lax.fori_loop(0, pairs, gather, 0, unroll=UNROLL)
+    def tiles(part, at, body):
+        for u in range(group):
+            lanes = pl.ds(pl.multiple_of((at + u) * LANES, LANES), LANES)
+            body(u, part * per_part + at + u, lanes)
+
+    def over(part, function):
+        lax.fori_loop(0, per_part // group, lambda n, c: function(part, n * group, n % 2) or c, 0)
+
+    def products(part, at, slot):
+        def one(u, p, lanes):
+            tile = moved_ref[part, :, lanes]
+            none = jnp.zeros_like(tile)
+            tall = jnp.concatenate([jnp.where(low16, tile, none), jnp.where(low16, none, tile)], axis=0)
+            both = jnp.dot(tall, mats_ref[p], preferred_element_type=jnp.float32)
+            terms[slot, 2 * u] = both[:bands]
+            terms[slot, 2 * u + 1] = both[bands:]
+
+        tiles(part, at, one)
+
+    def scatter(base, slot):
+        for n in range(2 * group):
+            term = terms[slot, n]
+            for k in range(2):
+                sums[k][spots_ref[2 * base + 2 * n + k]] += term
+
+    for part in range(parts):
+        products(part, 0, 0)
+
+        def step(n, carry):
+            scatter(2 * (part * per_part + (n - 1) * group), (n - 1) % 2)
+            products(part, n * group, n % 2)
+            return carry
+
+        steps = per_part // group
+        lax.fori_loop(1, steps, step, 0)
+        scatter(2 * (part * per_part + (steps - 1) * group), (steps - 1) % 2)
+
+    def join(part, at, slot):
+        def one(u, p, lanes):
+            here = jnp.where(low, first[p], second[p])
+            there = jnp.where(low, first[pairs + p], second[pairs + p])
+            resid = moved_ref[part, :, lanes].astype(jnp.float32) + here + pltpu.roll(there, half, 1)
+            resid_ref[:, pl.ds(pl.multiple_of(p * LANES, LANES), LANES)] = resid
+            picked[p] = resid.astype(jnp.bfloat16)
+            picked[pairs + p] = pltpu.roll(resid, half, 1).astype(jnp.bfloat16)
+
+        tiles(part, at, one)
+
+    for part in range(parts):
+        over(part, join)
+
+    def gather(part, at, slot):
+        base = 4 * (part * per_part + at)
+
+        def one(u, p, lanes):
+            sources = []
+            for q in range(2):
+                spot = base + 4 * u + 2 * q
+                sources.append(jnp.where(low16, picked[spots_ref[spot]], picked[spots_ref[spot + 1]]))
+            both = lax.dot_general(
+                jnp.concatenate(sources, axis=0),
+                mats_ref[p],
+                (((1,), (1,)), ((), ())),
+                preferred_element_type=jnp.float32,
+            )
+            both = jnp.where(low, both[:bands], both[bands:])
+            mixed_ref[part, :, lanes] = (picked[p].astype(jnp.float32) + both).astype(jnp.bfloat16)
+
+        tiles(part, at, one)
+
+    for part in range(parts):
+        over(part, gather)
 
 
 def forward_kernel(starts_ref, keys_ref, weight_ref, mixed_ref, pert_ref, vert_ref, field_ref, obs_ref):
@@ -207,26 +272,39 @@
             field_ref[g, c * group : (c + 1) * group, :] = field[g * group : (g + 1) * group, :]
 
     obs_ref[...] = jnp.zeros_like(obs_ref)
-    places = row_numbers(wide, CHUNK)
-    ones = jnp.ones((1, CHUNK), jnp.bfloat16)
-    numbers = lax.broadcasted_iota(jnp.int32, (rows, CHUNK), 0).astype(jnp.float32)
+    nobs = weight_ref.shape[1]
+    ncol = lax.axis_size("col")
+    mine = lax.axis_index("col")
+
     def collect(g, carry):
-        base = (g * rows).astype(jnp.float32)
-
-        def step(c, carry):
-            span = span_of(c)
-            weight = weight_ref[:, span]
-            result = obs_ref[:, span]
-            for which, w in ((0, weight), (1, 1.0 - weight)):
-                row = keys_ref[2 * which : 2 * which + 1, span] - base
-                hot = one_hot(keys_ref[2 * which + 1 : 2 * which + 2, span], places, ones)
-                lines = jnp.dot(field_ref[g], hot, preferred_element_type=jnp.float32)
-                kept = jnp.where(numbers == row, lines, 0.0)
-                result = result + w * jnp.sum(kept, axis=0, keepdims=True)
-            obs_ref[:, span] = result
+        runs = runs_of(starts_ref, g, mine, ncol)
+
+        def step(trip, carry):
+            spans, rights, hots, rows_of = [], [], [], []
+            for run in runs:
+                which = run[0]
+                span, valid = window_of(run, trip, nobs)
+                width = width_of(which)
+                lane = keys_ref[2 * which + 1 : 2 * which + 2, span]
+                hots.append(one_hot(lane, row_numbers(wide, width), jnp.ones((1, width), jnp.bfloat16)))
+                rows_of.append(jnp.where(valid, keys_ref[2 * which : 2 * which + 1, span], -1.0))
+                weight = weight_ref[:, span]
+                rights.append(1.0 - weight if which else weight)
+                spans.append(span)
+            hot = jnp.concatenate(hots, axis=1)
+            lines = jnp.dot(field_ref[g], hot, preferred_element_type=jnp.float32).astype(jnp.bfloat16)
+            at = 0
+            for span, right, row in zip(spans, rights, rows_of):
+                width = row.shape[1]
+                kept = one_hot(row, row_numbers(rows, width), lines[:, at : at + width])
+                found = kept[:SUBLANES]
+                for r in range(SUBLANES, rows, SUBLANES):
+                    found = found + kept[r : r + SUBLANES]
+                obs_ref[:, span] += right * jnp.sum(found.astype(jnp.float32), axis=0, keepdims=True)
+                at += width
             return carry
 
-        lax.fori_loop(starts_ref[g] // CHUNK, (starts_ref[g + 1] + CHUNK - 1) // CHUNK, step, 0)
+        lax.fori_loop(0, trips_of(runs), step, 0)
         return carry
 
     lax.fori_loop(0, levels // group, collect, 0)
@@ -273,15 +351,17 @@
                     ]
 
 
-def local_call(kernel, outs, args, name, scratch=(), scalars=1):
-    vmem = pl.BlockSpec(memory_space=pltpu.VMEM)
-    smem = pl.BlockSpec(memory_space=pltpu.SMEM)
-    kept = [a if i < scalars else pltpu.with_memory_space_constraint(a, pltpu.VMEM) for i, a in enumerate(args)]
+def local_call(kernel, outs, args, name, scratch=(), scalars=1, remote=0):
+    spaces = [pltpu.SMEM] * scalars + [pltpu.HBM] * remote + [pltpu.VMEM] * (len(args) - scalars - remote)
+    kept = [
+        a if space is pltpu.SMEM else pltpu.with_memory_space_constraint(a, space)
+        for a, space in zip(args, spaces)
+    ]
     return pl.pallas_call(
         kernel,
         out_shape=tuple(pltpu.VMEM(o.shape, o.dtype) for o in outs),
-        in_specs=[smem] * scalars + [vmem] * (len(args) - scalars),
-        out_specs=(vmem,) * len(outs),
+        in_specs=[pl.BlockSpec(memory_space=space) for space in spaces],
+        out_specs=(pl.BlockSpec(memory_space=pltpu.VMEM),) * len(outs),
         scratch_shapes=list(scratch),
         compiler_params=pltpu.CompilerParams(vmem_limit_bytes=VMEM_BYTES),
         name=name,
@@ -346,34 +426,26 @@
     rows = chunks * group
     slices = levels // nmem
 
-    order = obs_level * nobs + jnp.arange(nobs, dtype=jnp.int32)
-    both = obs_nodes[:, 0] * nodes + obs_nodes[:, 1]
-    order, both, weight, value, precision = lax.sort(
-        (order, both, obs_weight, obs_value, obs_precision), num_keys=1, is_stable=False
+    level, node, other = obs_level, obs_nodes[:, 0], obs_nodes[:, 1]
+    kind = ((level // group) * ncol + node // ncols) * ncol + other // ncols
+    bounds = jnp.arange(levels // group * ncol * ncol + 1, dtype=jnp.int32)
+    starts = jnp.sum((kind[None, :] < bounds[:, None]).astype(jnp.int32), axis=1)
+    order = (kind * group + level % group) * ncols + node % ncols
+    order, other, weight, value, precision = lax.sort(
+        (order, other % ncols, obs_weight, obs_value, obs_precision), num_keys=1, is_stable=False
     )
-    level = order // nobs
+    level = (order // ncols) % group
     keys = []
-    for node in (both // nodes, both % nodes):
-        local = node - lax.axis_index("col") * ncols
-        inside = (local >= 0) & (local < ncols)
-        row = (level // group) * rows + (local // wide) * group + level % group
-        keys += [jnp.where(inside, row, -(1 << 20)), jnp.where(inside, local % wide, 0)]
+    for local in (order % ncols, other):
+        keys += [(local // wide) * group + level, local % wide]
     keys = jnp.stack(keys).astype(jnp.float32)
-    bounds = jnp.arange(levels // group + 1, dtype=jnp.int32) * group
-    starts = jnp.sum((obs_level[None, :] < bounds[:, None]).astype(jnp.int32), axis=1)
     weight, value, precision = (a.reshape(1, nobs) for a in (weight, value, precision))
 
-    scaled = (blocks.astype(jnp.float32) * jnp.repeat(block_scale, width, axis=1)[:, None, :]).astype(
-        jnp.bfloat16
-    ).reshape(pairs, 2, width, depth)
-    mats = jnp.concatenate(
-        [
-            jnp.pad(scaled[:, 0], ((0, 0), (0, 0), (0, depth))),
-            jnp.pad(scaled[:, 1], ((0, 0), (0, 0), (depth, 0))),
-        ],
-        axis=1,
-    )
-    cols = block_cols.T
+    tiles = min(TILES, ncols // LANES)
+    scales = jnp.repeat(block_scale, width, axis=1)[:, None, :]
+    mats = (blocks.astype(jnp.float32) * scales).astype(jnp.bfloat16).reshape(pairs, LANES, depth)
+    which = jnp.arange(block_cols.shape[1], dtype=jnp.int32)[None, :]
+    spots = (((block_cols & 1) ^ which) * pairs + (block_cols >> 1)).reshape(-1)
 
     vector = jax.ShapeDtypeStruct((1, nobs), jnp.float32)
     number = jax.ShapeDtypeStruct((1, LANES), jnp.float32)
@@ -386,23 +458,40 @@
         return local_call(
             functools.partial(adjoint_kernel, seen=count, first=before is None),
             outs,
-            [starts, keys, weight, precision, errors, pert, vertical, *extra],
+            [starts, pert, vertical, keys, weight, precision, errors, *extra],
             "adjoint",
-            [pltpu.VMEM((rows, wide), jnp.float32), pltpu.VMEM((levels, ncols), jnp.float32)],
+            [
+                pltpu.VMEM((rows, wide), jnp.float32),
+                pltpu.VMEM((levels, ncols), jnp.float32),
+                pltpu.VMEM((levels, ncols), jnp.bfloat16),
+                pltpu.VMEM((levels, levels), jnp.bfloat16),
+                pltpu.SemaphoreType.DMA((2,)),
+            ],
+            remote=2,
         )
 
     def middle(moved):
-        return local_call(
+        vmem = pl.BlockSpec(memory_space=pltpu.VMEM)
+        return pl.pallas_call(
             horizontal_kernel,
-            (jax.ShapeDtypeStruct((bands, nodes), jnp.float32), moved_shape),
-            [cols, moved, mats],
-            "horizontal",
-            [
+            out_shape=(
+                pltpu.VMEM((bands, nodes), jnp.float32),
+                pltpu.VMEM(moved_shape.shape, moved_shape.dtype),
+            ),
+            in_specs=[pl.BlockSpec(memory_space=pltpu.SMEM), vmem, vmem],
+            out_specs=(vmem, vmem),
+            scratch_shapes=[
+                pltpu.VMEM((2, 2 * tiles, bands, LANES), jnp.float32),
                 pltpu.VMEM((2 * pairs, bands, LANES), jnp.float32),
-                pltpu.VMEM((2, pairs, bands, LANES), jnp.float32),
-                pltpu.VMEM((2, pairs, bands, LANES), jnp.float32),
-                pltpu.VMEM((2, pairs, bands, LANES), jnp.bfloat16),
+                pltpu.VMEM((2 * pairs, bands, LANES), jnp.float32),
+                pltpu.VMEM((2 * pairs, bands, LANES), jnp.bfloat16),
             ],
+            compiler_params=pltpu.CompilerParams(vmem_limit_bytes=VMEM_BYTES),
+            name="horizontal",
+        )(
+            spots,
+            pltpu.with_memory_space_constraint(moved, pltpu.VMEM),
+            pltpu.with_memory_space_constraint(mats, pltpu.VMEM),
         )
 
     def forward(columns):

time: 144 us -> 126 us (0.88)
  Pallas kernels: 40.7 us -> 24.9 us
  waiting for transfers between devices: 24.7 us -> 28.9 us
  other arithmetic: 15.1 us -> 11.3 us
  local copies, waits for them, and re-layouts: 5.8 us -> 2.19 us
    pallas_call x7 -> x5, Pallas kernels: 40.7 us -> 14 us  [local_call(): pl.pallas_call(kernel, out_shape=tuple((pltpu.VMEM(o.shape, o.dtype) for...]
    pallas_call x0 -> x2, Pallas kernels: none -> 10.9 us  [middle(): pl.pallas_call(horizontal_kernel, out_shape=(pltpu.VMEM((bands, nodes), j...]
    unnamed x15 -> x13, local copies, waits for them, and re-layouts: 4.8 us -> 0.82 us
    all_to_all x1, waiting for transfers between devices: 2.51 us -> 6 us  [per_device(): moved = lax.all_to_all(sent, 'col', 0, 0, tiled=True)]
    concatenate x1 -> x0, other arithmetic: 2.29 us -> none  [per_device(): jnp.concatenate([jnp.pad(scaled[:, 0], ((0, 0), (0, 0), (0, depth))), jnp...]
  transfers between devices with their start and end apart: 19 -> 19, of which waited for: 15 -> 16; matrix products, arithmetic and copies ran while one was open for 4% -> 3% of each run, Pallas kernels for 0% -> 0%
where the time goes in v5:
time: 126 us
  blocking collectives  30.8 us (24%)
  waiting for transfers between devices  28.9 us (23%)
  starting transfers between devices  26.8 us (21%)
  Pallas kernels  24.9 us (20%)
  other arithmetic  11.3 us (9%)
  local copies, waits for them, and re-layouts  2.19 us (2%)
    ppermute x18, waiting for transfers between devices, swap(): return lax.ppermute(x, axis, [(i, i ^ offset) for i in range(n)])  22.9 us
    ppermute x18, starting transfers between devices, swap(): return lax.ppermute(x, axis, [(i, i ^ offset) for i in range(n)])  21.2 us
    all_to_all x2, blocking collectives, per_device(): lax.all_to_all(mixed, 'col', 0, 0, tiled=True).reshape(levels, ncols)  20.2 us
    pallas_call x5, Pallas kernels, local_call(): pl.pallas_call(kernel, out_shape=tuple((pltpu.VMEM(o.shape, o.dtype) for...  14 us
    pallas_call x2, Pallas kernels, middle(): pl.pallas_call(horizontal_kernel, out_shape=(pltpu.VMEM((bands, nodes), j...  10.9 us
    all_to_all x1, blocking collectives, per_device(): moved = lax.all_to_all(sent, 'col', 0, 0, tiled=True)  10.7 us
    sort x1, other arithmetic, per_device(): lax.sort((order, other % ncols, obs_weight, obs_value, obs_precision), nu...  6.66 us
    all_to_all x1, waiting for transfers between devices, per_device(): moved = lax.all_to_all(sent, 'col', 0, 0, tiled=True)  6 us
  transfers between devices with their start and end apart: 19, of which 16 were waited for; matrix products, arithmetic and copies ran while one was open for 3% of the time, Pallas kernels for 0%

profile of v5, /device:TPU:0, one launch (start us, length us, event | category | flops | bytes accessed | tf_op | source)
XLA Modules:
  0.0 125.8 jit_solution(15076404261483332281)
XLA Ops:
  0.7 1.0 fusion.28
  1.6 0.9 fusion.9
  2.5 0.3 convert_reduce_fusion.refs_0_.starts_ref
  2.8 6.7 %sort.33 = (s32[8192]{0:T(1024)S(1)}, s32[8192]{0:T(1024)S(1)}, f32[8192]{0:T(1024)S(1)}, f32[8192]{0:T(1024)S(1)}, f32[8192]{0:T(1024)S(1)}) sort(s32[8192]{0:T(1024)S(1)} %get-tuple-element.50, s32[8192]{0:T(1024)S(1)} %get-tuple-element.61, f32[8192]{0:T(1024)} %param.17, f32[8192]{0:T(1024)} %param.18, f32[8192]{0:T(1024)} %param.19), dimensions={0}, to_apply=%region_0.1 | sort | flops 106496 | bytes 327680 | tf_op jit(solution)/shard_map/sort | solution.py:434
  9.7 3.8 %adjoint.2 = (bf16[4,32,2048]{2,1,0:T(8,128)(2,1)}, f32[1,8192]{1,0:T(1,128)S(1)}) custom-call(s32[65]{0:T(128)S(1)} %convert_reduce_fusion.refs_0_.starts_ref, bf16[128,2048]{1,0:T(8,128)(2,1)} %bitcast.32, bf16[128,128]{1,0:T(8,128)(2,1)} %vert_ref.3, f32[4,8192]{1,0:T(4,128)S(1)} %add_convert_fusion.refs_3_.keys_ref, f32[1,8192]{1,0:T(1,128)S(1)} %bitcast.38, ...), custom_call_target="tpu_custom_call" | custom-call | tf_op jit(solution)/shard_map/adjoint/pallas_call | solution.py:360
  13.6 5.7 %all-to-all-start = ((bf16[4,32,2048]{2,1,0:T(8,128)(2,1)}), bf16[4,32,2048]{2,1,0:T(8,128)(2,1)S(1)}, u32[]{:S(2)}, u32[]{:S(2)}) async-start(bf16[4,32,2048]{2,1,0:T(8,128)(2,1)} %get-tuple-element.32), calls=%async_computation | async-start | bytes 1048576 | tf_op jit(solution)/shard_map/all_to_all | solution.py:512
  19.5 0.1 reshape.34.spots_ref
  19.6 2.2 %multiply_convert_fusion = bf16[128,64,128]{2,1,0:T(8,128)(2,1)S(1)} fusion(bf16[128,64,128]{2,1,0:T(8,128)(2,1)} %param.12, f32[128,128]{1,0:T(8,128)S(1)} %copy.16), kind=kLoop, calls=%fused_computation | loop fusion | flops 3145728 | bytes 4259840 | tf_op jit(solution)/shard_map/convert_element_type | solution.py:446
  21.9 6.0 %all-to-all-done.moved_ref = bf16[4,32,2048]{2,1,0:T(8,128)(2,1)S(1)} async-done(((bf16[4,32,2048]{2,1,0:T(8,128)(2,1)}), bf16[4,32,2048]{2,1,0:T(8,128)(2,1)S(1)}, u32[]{:S(2)}, u32[]{:S(2)}) %all-to-all-start) | async-done | bytes 524320 | tf_op jit(solution)/shard_map/all_to_all | solution.py:512
  27.9 5.4 %horizontal.2 = (f32[32,8192]{1,0:T(8,128)S(1)}, bf16[4,32,2048]{2,1,0:T(8,128)(2,1)S(1)}) custom-call(s32[256]{0:T(256)S(1)} %reshape.34.spots_ref, bf16[4,32,2048]{2,1,0:T(8,128)(2,1)S(1)} %all-to-all-done.moved_ref, bf16[64,128,128]{2,1,0:T(8,128)(2,1)S(1)} %bitcast.30), custom_call_target="tpu_custom_call" | custom-call | tf_op jit(solution)/shard_map/horizontal/pallas_call | solution.py:475
  33.4 10.6 %all_to_all.20 = bf16[4,32,2048]{2,1,0:T(8,128)(2,1)S(1)} all-to-all(bf16[4,32,2048]{2,1,0:T(8,128)(2,1)S(1)} %get-tuple-element.33), channel_id=1, replica_groups=mesh['mem'=8,'col'=4] {'col'}, dimensions={0} | all-to-all | bytes 1048576 | tf_op jit(solution)/shard_map/all_to_all | solution.py:514
  44.0 3.0 %forward.2 = (bf16[4,256,256]{2,1,0:T(8,128)(2,1)S(1)}, f32[1,8192]{1,0:T(1,128)S(1)}) custom-call(s32[65]{0:T(128)S(1)} %convert_reduce_fusion.refs_0_.starts_ref, f32[4,8192]{1,0:T(4,128)S(1)} %add_convert_fusion.refs_3_.keys_ref, f32[1,8192]{1,0:T(1,128)S(1)} %bitcast.39, bf16[128,2048]{1,0:T(8,128)(2,1)S(1)} %bitcast.37, bf16[128,2048]{1,0:T(8,128)(2,1)S(1)} %bitcast.34, ...), custom_call_target="tpu_custom_call" | custom-call | tf_op jit(solution)/shard_map/forward/pallas_call | solution.py:360
  47.1 1.2 collective-permute-done
  48.3 2.3 %collective-permute-start.1 = (f32[1,8192]{1,0:T(1,128)S(1)}, f32[1,8192]{1,0:T(1,128)S(1)}, u32[]{:S(2)}, u32[]{:S(2)}) collective-permute-start(f32[1,8192]{1,0:T(1,128)S(1)} %add.121), channel_id=1, source_target_pairs={{0,1},{1,0},{2,3},{3,2},{4,5},{5,4},{6,7},{7,6},{8,9},{9,8},{10,11... | collective-permute-start | bytes 98312 | tf_op jit(solution)/shard_map/ppermute | solution.py:373
  50.6 1.5 %collective-permute-start.3 = (f32[1,8192]{1,0:T(1,128)S(1)}, f32[1,8192]{1,0:T(1,128)S(1)}, u32[]{:S(2)}, u32[]{:S(2)}) collective-permute-start(f32[1,8192]{1,0:T(1,128)S(1)} %add.121), channel_id=1, source_target_pairs={{0,3},{1,2},{2,1},{3,0},{4,7},{5,6},{6,5},{7,4},{8,11},{9,10},{10,... | collective-permute-start | bytes 98312 | tf_op jit(solution)/shard_map/ppermute | solution.py:373
  52.2 0.4 collective-permute-done.1
  52.5 2.2 %collective-permute-done.2 = f32[1,8192]{1,0:T(1,128)S(1)} collective-permute-done((f32[1,8192]{1,0:T(1,128)S(1)}, f32[1,8192]{1,0:T(1,128)S(1)}, u32[]{:S(2)}, u32[]{:S(2)}) %collective-permute-start.2) | collective-permute-done | bytes 32800 | tf_op jit(solution)/shard_map/ppermute | solution.py:373
  54.7 0.7 collective-permute-done.3
  55.5 1.6 %collective-permute-start.4 = (f32[1,8192]{1,0:T(1,128)S(1)}, f32[1,8192]{1,0:T(1,128)S(1)}, u32[]{:S(2)}, u32[]{:S(2)}) collective-permute-start(f32[1,8192]{1,0:T(1,128)S(1)} %add_add_fusion.1.refs_7_), channel_id=1, source_target_pairs={{0,8},{4,12},{8,0},{12,4},{16,24},{20,28},{24,16},{28,20},{1,9},{5... | collective-permute-start | bytes 98312 | tf_op jit(solution)/shard_map/ppermute | solution.py:373
  57.1 2.6 %collective-permute-start.5 = (f32[1,8192]{1,0:T(1,128)S(1)}, f32[1,8192]{1,0:T(1,128)S(1)}, u32[]{:S(2)}, u32[]{:S(2)}) collective-permute-start(f32[1,8192]{1,0:T(1,128)S(1)} %add_add_fusion.1.refs_7_), channel_id=1, source_target_pairs={{0,16},{4,20},{8,24},{12,28},{16,0},{20,4},{24,8},{28,12},{1,17},{... | collective-permute-start | bytes 98312 | tf_op jit(solution)/shard_map/ppermute | solution.py:373
  59.7 0.2 collective-permute-start.6
  59.9 2.2 %collective-permute-done.5.refs_9_ = f32[1,8192]{1,0:T(1,128)S(1)} collective-permute-done((f32[1,8192]{1,0:T(1,128)S(1)}, f32[1,8192]{1,0:T(1,128)S(1)}, u32[]{:S(2)}, u32[]{:S(2)}) %collective-permute-start.5) | collective-permute-done | bytes 32800 | tf_op jit(solution)/shard_map/ppermute | solution.py:373
  62.2 3.2 %collective-permute-done.6.refs_10_ = f32[1,8192]{1,0:T(1,128)S(1)} collective-permute-done((f32[1,8192]{1,0:T(1,128)S(1)}, f32[1,8192]{1,0:T(1,128)S(1)}, u32[]{:S(2)}, u32[]{:S(2)}) %collective-permute-start.6) | collective-permute-done | bytes 32800 | tf_op jit(solution)/shard_map/ppermute | solution.py:373
  65.4 3.3 %adjoint.3 = (bf16[4,32,2048]{2,1,0:T(8,128)(2,1)S(1)}, f32[1,8192]{1,0:T(1,128)S(1)}, f32[1,128]{1,0:T(1,128)S(1)}, f32[1,128]{1,0:T(1,128)S(1)}, f32[1,8192]{1...) custom-call(s32[65]{0:T(128)S(1)} %convert_reduce_fusion.refs_0_.starts_ref, bf16[128,2048]{1,0:T(8,128)(2,1)} %bitcast.33, ...), custom_call_target="tpu_custom_call" | custom-call | tf_op jit(solution)/shard_map/adjoint/pallas_call | solution.py:360
  68.7 10.7 %all_to_all.21.moved_ref = bf16[4,32,2048]{2,1,0:T(8,128)(2,1)S(1)} all-to-all(bf16[4,32,2048]{2,1,0:T(8,128)(2,1)S(1)} %get-tuple-element.39), channel_id=1, replica_groups=mesh['mem'=8,'col'=4] {'col'}, dimensions={0} | all-to-all | bytes 1048576 | tf_op jit(solution)/shard_map/all_to_all | solution.py:512
  79.4 5.5 %horizontal.3 = (f32[32,8192]{1,0:T(8,128)S(1)}, bf16[4,32,2048]{2,1,0:T(8,128)(2,1)S(1)}) custom-call(s32[256]{0:T(256)S(1)} %reshape.34.spots_ref, bf16[4,32,2048]{2,1,0:T(8,128)(2,1)S(1)} %all_to_all.21.moved_ref, bf16[64,128,128]{2,1,0:T(8,128)(2,1)S(1)} %bitcast.31), custom_call_target="tpu_custom_call" | custom-call | tf_op jit(solution)/shard_map/horizontal/pallas_call | solution.py:475
  84.9 9.5 %all_to_all.22 = bf16[4,32,2048]{2,1,0:T(8,128)(2,1)S(1)} all-to-all(bf16[4,32,2048]{2,1,0:T(8,128)(2,1)S(1)} %get-tuple-element.40), channel_id=1, replica_groups=mesh['mem'=8,'col'=4] {'col'}, dimensions={0} | all-to-all | bytes 1048576 | tf_op jit(solution)/shard_map/all_to_all | solution.py:514
  94.4 3.0 %forward.3 = (bf16[4,256,256]{2,1,0:T(8,128)(2,1)S(1)}, f32[1,8192]{1,0:T(1,128)S(1)}) custom-call(s32[65]{0:T(128)S(1)} %convert_reduce_fusion.refs_0_.starts_ref, f32[4,8192]{1,0:T(4,128)S(1)} %add_convert_fusion.refs_3_.keys_ref, f32[1,8192]{1,0:T(1,128)S(1)} %bitcast.41, bf16[128,2048]{1,0:T(8,128)(2,1)S(1)} %bitcast.36, bf16[128,2048]{1,0:T(8,128)(2,1)S(1)} %bitcast.35, ...), custom_call_target="tpu_custom_call" | custom-call | tf_op jit(solution)/shard_map/forward/pallas_call | solution.py:360
  97.4 1.2 collective-permute-done.7
  98.7 1.2 collective-permute-start.10
  99.9 1.7 %collective-permute-start.8 = (f32[1,8192]{1,0:T(1,128)S(1)}, f32[1,8192]{1,0:T(1,128)S(1)}, u32[]{:S(2)}, u32[]{:S(2)}) collective-permute-start(f32[1,8192]{1,0:T(1,128)S(1)} %add.125), channel_id=1, source_target_pairs={{0,1},{1,0},{2,3},{3,2},{4,5},{5,4},{6,7},{7,6},{8,9},{9,8},{10,11... | collective-permute-start | bytes 98312 | tf_op jit(solution)/shard_map/ppermute | solution.py:373
  101.6 0.9 collective-permute-start.9
  102.4 1.1 collective-permute-done.10
  103.6 0.2 collective-permute-done.8
  103.8 1.7 %collective-permute-done.9 = f32[1,8192]{1,0:T(1,128)S(1)} collective-permute-done((f32[1,8192]{1,0:T(1,128)S(1)}, f32[1,8192]{1,0:T(1,128)S(1)}, u32[]{:S(2)}, u32[]{:S(2)}) %collective-permute-start.9) | collective-permute-done | bytes 32800 | tf_op jit(solution)/shard_map/ppermute | solution.py:373
  105.6 0.9 collective-permute-start.12
  106.5 3.5 %collective-permute-start.13 = (f32[1,8192]{1,0:T(1,128)S(1)}, f32[1,8192]{1,0:T(1,128)S(1)}, u32[]{:S(2)}, u32[]{:S(2)}) collective-permute-start(f32[1,8192]{1,0:T(1,128)S(1)} %add_add_fusion.refs_5_), channel_id=1, source_target_pairs={{0,24},{4,28},{8,16},{12,20},{16,8},{20,12},{24,0},{28,4},{1,25},{... | collective-permute-start | bytes 98312 | tf_op jit(solution)/shard_map/ppermute | solution.py:373
  110.0 0.5 collective-permute-done.12.refs_7_
  110.5 1.7 %collective-permute-done.13.refs_8_ = f32[1,8192]{1,0:T(1,128)S(1)} collective-permute-done((f32[1,8192]{1,0:T(1,128)S(1)}, f32[1,8192]{1,0:T(1,128)S(1)}, u32[]{:S(2)}, u32[]{:S(2)}) %collective-permute-start.13) | collective-permute-done | bytes 32800 | tf_op jit(solution)/shard_map/ppermute | solution.py:373
  112.2 0.9 finish.1
  113.3 1.5 %collective-permute-done.14 = bf16[4,16,2048]{2,1,0:T(8,128)(2,1)S(1)} collective-permute-done((bf16[4,16,2048]{2,1,0:T(8,128)(2,1)S(1)}, bf16[4,16,2048]{2,1,0:T(8,128)(2,1)S(1)}, u32[]{:S(2)}, u32[]{:S(2)}) %collective-permute-start.14) | collective-permute-done | bytes 262176 | tf_op jit(solution)/shard_map/ppermute | solution.py:373
  114.9 0.3 collective-permute-start.15
  115.2 3.8 %collective-permute-start.16 = (bf16[16,2048]{1,0:T(8,128)(2,1)S(1)}, bf16[16,2048]{1,0:T(8,128)(2,1)S(1)}, u32[]{:S(2)}, u32[]{:S(2)}) collective-permute-start(bf16[16,2048]{1,0:T(8,128)(2,1)S(1)} %get-tuple-element.54), channel_id=1, source_target_pairs={{0,16},{4,20},{8,24},{12,28},{16,0},{20,4},{24,8},{28,12},{1,17},{... | collective-permute-start | bytes 196616 | tf_op jit(solution)/shard_map/ppermute | solution.py:373
  119.0 0.4 collective-permute-start.17
  119.3 0.8 copy.17
  120.1 2.9 %collective-permute-done.16 = bf16[16,2048]{1,0:T(8,128)(2,1)S(1)} collective-permute-done((bf16[16,2048]{1,0:T(8,128)(2,1)S(1)}, bf16[16,2048]{1,0:T(8,128)(2,1)S(1)}, u32[]{:S(2)}, u32[]{:S(2)}) %collective-permute-start.16) | collective-permute-done | bytes 65568 | tf_op jit(solution)/shard_map/ppermute | solution.py:373
  123.0 2.1 %collective-permute-done.17 = bf16[16,2048]{1,0:T(8,128)(2,1)S(1)} collective-permute-done((bf16[16,2048]{1,0:T(8,128)(2,1)S(1)}, bf16[16,2048]{1,0:T(8,128)(2,1)S(1)}, u32[]{:S(2)}, u32[]{:S(2)}) %collective-permute-start.17) | collective-permute-done | bytes 65568 | tf_op jit(solution)/shard_map/ppermute | solution.py:373
  125.1 0.7 fusion.2
  (33 shorter events, 1.1 us)
Async XLA Ops:
  0.6 18.6 %copy-start.5 = (s32[128,2]{0,1:T(2,128)S(1)}, s32[128,2]{0,1:T(2,128)}, u32[]{:S(2)}) copy-start(s32[128,2]{0,1:T(2,128)} %param.14) | copy-start | bytes 3076
  0.6 18.6 %copy-start.4 = (f32[128,2]{0,1:T(2,128)S(1)}, f32[128,2]{0,1:T(2,128)}, u32[]{:S(2)}) copy-start(f32[128,2]{0,1:T(2,128)} %param.13) | copy-start | bytes 3076
  13.6 14.3 %all-to-all-start = ((bf16[4,32,2048]{2,1,0:T(8,128)(2,1)}), bf16[4,32,2048]{2,1,0:T(8,128)(2,1)S(1)}, u32[]{:S(2)}, u32[]{:S(2)}) async-start(bf16[4,32,2048]{2,1,0:T(8,128)(2,1)} %get-tuple-element.32), calls=%async_computation | async-start | bytes 1048576 | tf_op jit(solution)/shard_map/all_to_all | solution.py:512
  21.9 22.1 %copy-start = (bf16[1,128,2048]{2,1,0:T(8,128)(2,1)S(1)}, bf16[1,128,2048]{2,1,0:T(8,128)(2,1)}, u32[]{:S(2)}) copy-start(bf16[1,128,2048]{2,1,0:T(8,128)(2,1)} %param.10) | copy-start | bytes 1572868
  21.9 22.1 %copy-start.2 = (bf16[128,128]{1,0:T(8,128)(2,1)S(1)}, bf16[128,128]{1,0:T(8,128)(2,1)}, u32[]{:S(2)}) copy-start(bf16[128,128]{1,0:T(8,128)(2,1)} %vert_ref.3) | copy-start | bytes 98308
  47.0 1.3 %collective-permute-start = (f32[1,8192]{1,0:T(1,128)S(1)}, f32[1,8192]{1,0:T(1,128)S(1)}, u32[]{:S(2)}, u32[]{:S(2)}) collective-permute-start(f32[1,8192]{1,0:T(1,128)S(1)} %get-tuple-element.34), channel_id=1, source_target_pairs={{0,4},{4,0},{8,12},{12,8},{16,20},{20,16},{24,28},{28,24},{1,5},{5... | collective-permute-start | bytes 98312 | tf_op jit(solution)/shard_map/ppermute | solution.py:373
  48.3 4.2 %collective-permute-start.1 = (f32[1,8192]{1,0:T(1,128)S(1)}, f32[1,8192]{1,0:T(1,128)S(1)}, u32[]{:S(2)}, u32[]{:S(2)}) collective-permute-start(f32[1,8192]{1,0:T(1,128)S(1)} %add.121), channel_id=1, source_target_pairs={{0,1},{1,0},{2,3},{3,2},{4,5},{5,4},{6,7},{7,6},{8,9},{9,8},{10,11... | collective-permute-start | bytes 98312 | tf_op jit(solution)/shard_map/ppermute | solution.py:373
  50.6 4.1 %collective-permute-start.2 = (f32[1,8192]{1,0:T(1,128)S(1)}, f32[1,8192]{1,0:T(1,128)S(1)}, u32[]{:S(2)}, u32[]{:S(2)}) collective-permute-start(f32[1,8192]{1,0:T(1,128)S(1)} %add.121), channel_id=1, source_target_pairs={{0,2},{1,3},{2,0},{3,1},{4,6},{5,7},{6,4},{7,5},{8,10},{9,11},{10,... | collective-permute-start | bytes 98312 | tf_op jit(solution)/shard_map/ppermute | solution.py:373
  50.6 4.8 %collective-permute-start.3 = (f32[1,8192]{1,0:T(1,128)S(1)}, f32[1,8192]{1,0:T(1,128)S(1)}, u32[]{:S(2)}, u32[]{:S(2)}) collective-permute-start(f32[1,8192]{1,0:T(1,128)S(1)} %add.121), channel_id=1, source_target_pairs={{0,3},{1,2},{2,1},{3,0},{4,7},{5,6},{6,5},{7,4},{8,11},{9,10},{10,... | collective-permute-start | bytes 98312 | tf_op jit(solution)/shard_map/ppermute | solution.py:373
  55.5 4.5 %collective-permute-start.4 = (f32[1,8192]{1,0:T(1,128)S(1)}, f32[1,8192]{1,0:T(1,128)S(1)}, u32[]{:S(2)}, u32[]{:S(2)}) collective-permute-start(f32[1,8192]{1,0:T(1,128)S(1)} %add_add_fusion.1.refs_7_), channel_id=1, source_target_pairs={{0,8},{4,12},{8,0},{12,4},{16,24},{20,28},{24,16},{28,20},{1,9},{5... | collective-permute-start | bytes 98312 | tf_op jit(solution)/shard_map/ppermute | solution.py:373
  57.1 5.0 %collective-permute-start.5 = (f32[1,8192]{1,0:T(1,128)S(1)}, f32[1,8192]{1,0:T(1,128)S(1)}, u32[]{:S(2)}, u32[]{:S(2)}) collective-permute-start(f32[1,8192]{1,0:T(1,128)S(1)} %add_add_fusion.1.refs_7_), channel_id=1, source_target_pairs={{0,16},{4,20},{8,24},{12,28},{16,0},{20,4},{24,8},{28,12},{1,17},{... | collective-permute-start | bytes 98312 | tf_op jit(solution)/shard_map/ppermute | solution.py:373
  59.7 5.7 %collective-permute-start.6 = (f32[1,8192]{1,0:T(1,128)S(1)}, f32[1,8192]{1,0:T(1,128)S(1)}, u32[]{:S(2)}, u32[]{:S(2)}) collective-permute-start(f32[1,8192]{1,0:T(1,128)S(1)} %add_add_fusion.1.refs_7_), channel_id=1, source_target_pairs={{0,24},{4,28},{8,16},{12,20},{16,8},{20,12},{24,0},{28,4},{1,25},{... | collective-permute-start | bytes 98312 | tf_op jit(solution)/shard_map/ppermute | solution.py:373
  79.4 15.0 %copy-start.1 = (bf16[1,128,2048]{2,1,0:T(8,128)(2,1)S(1)}, bf16[1,128,2048]{2,1,0:T(8,128)(2,1)}, u32[]{:S(2)}) copy-start(bf16[1,128,2048]{2,1,0:T(8,128)(2,1)} %param.10) | copy-start | bytes 1572868
  79.4 15.0 %copy-start.3 = (bf16[128,128]{1,0:T(8,128)(2,1)S(1)}, bf16[128,128]{1,0:T(8,128)(2,1)}, u32[]{:S(2)}) copy-start(bf16[128,128]{1,0:T(8,128)(2,1)} %vert_ref.3) | copy-start | bytes 98308
  97.4 1.3 %collective-permute-start.7 = (f32[1,8192]{1,0:T(1,128)S(1)}, f32[1,8192]{1,0:T(1,128)S(1)}, u32[]{:S(2)}, u32[]{:S(2)}) collective-permute-start(f32[1,8192]{1,0:T(1,128)S(1)} %get-tuple-element.41), channel_id=1, source_target_pairs={{0,4},{4,0},{8,12},{12,8},{16,20},{20,16},{24,28},{28,24},{1,5},{5... | collective-permute-start | bytes 98312 | tf_op jit(solution)/shard_map/ppermute | solution.py:373
  98.7 4.9 %collective-permute-start.10 = (f32[1,8192]{1,0:T(1,128)S(1)}, f32[1,8192]{1,0:T(1,128)S(1)}, u32[]{:S(2)}, u32[]{:S(2)}) collective-permute-start(f32[1,8192]{1,0:T(1,128)S(1)} %add.125), channel_id=1, source_target_pairs={{0,3},{1,2},{2,1},{3,0},{4,7},{5,6},{6,5},{7,4},{8,11},{9,10},{10,... | collective-permute-start | bytes 98312 | tf_op jit(solution)/shard_map/ppermute | solution.py:373
  99.9 3.9 %collective-permute-start.8 = (f32[1,8192]{1,0:T(1,128)S(1)}, f32[1,8192]{1,0:T(1,128)S(1)}, u32[]{:S(2)}, u32[]{:S(2)}) collective-permute-start(f32[1,8192]{1,0:T(1,128)S(1)} %add.125), channel_id=1, source_target_pairs={{0,1},{1,0},{2,3},{3,2},{4,5},{5,4},{6,7},{7,6},{8,9},{9,8},{10,11... | collective-permute-start | bytes 98312 | tf_op jit(solution)/shard_map/ppermute | solution.py:373
  101.6 3.9 %collective-permute-start.9 = (f32[1,8192]{1,0:T(1,128)S(1)}, f32[1,8192]{1,0:T(1,128)S(1)}, u32[]{:S(2)}, u32[]{:S(2)}) collective-permute-start(f32[1,8192]{1,0:T(1,128)S(1)} %add.125), channel_id=1, source_target_pairs={{0,2},{1,3},{2,0},{3,1},{4,6},{5,7},{6,4},{7,5},{8,10},{9,11},{10,... | collective-permute-start | bytes 98312 | tf_op jit(solution)/shard_map/ppermute | solution.py:373
  105.5 4.5 %collective-permute-start.11 = (f32[1,8192]{1,0:T(1,128)S(1)}, f32[1,8192]{1,0:T(1,128)S(1)}, u32[]{:S(2)}, u32[]{:S(2)}) collective-permute-start(f32[1,8192]{1,0:T(1,128)S(1)} %add_add_fusion.refs_5_), channel_id=1, source_target_pairs={{0,8},{4,12},{8,0},{12,4},{16,24},{20,28},{24,16},{28,20},{1,9},{5... | collective-permute-start | bytes 98312 | tf_op jit(solution)/shard_map/ppermute | solution.py:373
  105.6 4.9 %collective-permute-start.12 = (f32[1,8192]{1,0:T(1,128)S(1)}, f32[1,8192]{1,0:T(1,128)S(1)}, u32[]{:S(2)}, u32[]{:S(2)}) collective-permute-start(f32[1,8192]{1,0:T(1,128)S(1)} %add_add_fusion.refs_5_), channel_id=1, source_target_pairs={{0,16},{4,20},{8,24},{12,28},{16,0},{20,4},{24,8},{28,12},{1,17},{... | collective-permute-start | bytes 98312 | tf_op jit(solution)/shard_map/ppermute | solution.py:373
  106.5 5.7 %collective-permute-start.13 = (f32[1,8192]{1,0:T(1,128)S(1)}, f32[1,8192]{1,0:T(1,128)S(1)}, u32[]{:S(2)}, u32[]{:S(2)}) collective-permute-start(f32[1,8192]{1,0:T(1,128)S(1)} %add_add_fusion.refs_5_), channel_id=1, source_target_pairs={{0,24},{4,28},{8,16},{12,20},{16,8},{20,12},{24,0},{28,4},{1,25},{... | collective-permute-start | bytes 98312 | tf_op jit(solution)/shard_map/ppermute | solution.py:373
  113.2 1.6 %collective-permute-start.14 = (bf16[4,16,2048]{2,1,0:T(8,128)(2,1)S(1)}, bf16[4,16,2048]{2,1,0:T(8,128)(2,1)S(1)}, u32[]{:S(2)}, u32[]{:S(2)}) collective-permute-start(bf16[4,16,2048]{2,1,0:T(8,128)(2,1)S(1)} %slice_bitcast_fusion), channel_id=1, source_target_pairs={{0,4},{4,0},{8,12},{12,8},{16,20},{20,16},{24,28},{28,24},{1,5},{5... | collective-permute-start | bytes 786440 | tf_op jit(solution)/shard_map/ppermute | solution.py:373
  114.9 5.2 %collective-permute-start.15 = (bf16[16,2048]{1,0:T(8,128)(2,1)S(1)}, bf16[16,2048]{1,0:T(8,128)(2,1)S(1)}, u32[]{:S(2)}, u32[]{:S(2)}) collective-permute-start(bf16[16,2048]{1,0:T(8,128)(2,1)S(1)} %get-tuple-element.52), channel_id=1, source_target_pairs={{0,8},{4,12},{8,0},{12,4},{16,24},{20,28},{24,16},{28,20},{1,9},{5... | collective-permute-start | bytes 196616 | tf_op jit(solution)/shard_map/ppermute | solution.py:373
  115.2 7.8 %collective-permute-start.16 = (bf16[16,2048]{1,0:T(8,128)(2,1)S(1)}, bf16[16,2048]{1,0:T(8,128)(2,1)S(1)}, u32[]{:S(2)}, u32[]{:S(2)}) collective-permute-start(bf16[16,2048]{1,0:T(8,128)(2,1)S(1)} %get-tuple-element.54), channel_id=1, source_target_pairs={{0,16},{4,20},{8,24},{12,28},{16,0},{20,4},{24,8},{28,12},{1,17},{... | collective-permute-start | bytes 196616 | tf_op jit(solution)/shard_map/ppermute | solution.py:373
  119.0 6.2 %collective-permute-start.17 = (bf16[16,2048]{1,0:T(8,128)(2,1)S(1)}, bf16[16,2048]{1,0:T(8,128)(2,1)S(1)}, u32[]{:S(2)}, u32[]{:S(2)}) collective-permute-start(bf16[16,2048]{1,0:T(8,128)(2,1)S(1)} %get-tuple-element.53), channel_id=1, source_target_pairs={{0,24},{4,28},{8,16},{12,20},{16,8},{20,12},{24,0},{28,4},{1,25},{... | collective-permute-start | bytes 196616 | tf_op jit(solution)/shard_map/ppermute | solution.py:373

commit v6 on v5

--- a/solution.py
+++ b/solution.py
@@ -14,7 +14,7 @@
 WIDE = 256
 ROWS = 256
 FIRST = 768
-SECOND = 256
+SECOND = 384
 TILES = 8
 VMEM_BYTES = 24 << 20
 
@@ -166,7 +166,7 @@
 
 
 def horizontal_kernel(
-    spots_ref, moved_ref, mats_ref, resid_ref, mixed_ref, terms, first, second, picked
+    spots_ref, scale_ref, moved_ref, mats_ref, resid_ref, mixed_ref, terms, first, second, picked
 ):
     parts, bands, ncols = moved_ref.shape
     pairs = mats_ref.shape[0]
@@ -195,8 +195,9 @@
             none = jnp.zeros_like(tile)
             tall = jnp.concatenate([jnp.where(low16, tile, none), jnp.where(low16, none, tile)], axis=0)
             both = jnp.dot(tall, mats_ref[p], preferred_element_type=jnp.float32)
-            terms[slot, 2 * u] = both[:bands]
-            terms[slot, 2 * u + 1] = both[bands:]
+            for q in range(2):
+                scale = jnp.where(low[:1], scale_ref[0, 2 * p + q], scale_ref[1, 2 * p + q])
+                terms[slot, 2 * u + q] = both[q * bands : (q + 1) * bands] * scale
 
         tiles(part, at, one)
 
@@ -239,14 +240,21 @@
             sources = []
             for q in range(2):
                 spot = base + 4 * u + 2 * q
-                sources.append(jnp.where(low16, picked[spots_ref[spot]], picked[spots_ref[spot + 1]]))
-            both = lax.dot_general(
+                one, two = picked[spots_ref[spot]], picked[spots_ref[spot + 1]]
+                none = jnp.zeros_like(one)
+                sources += [jnp.where(low16, one, none), jnp.where(low16, none, two)]
+            each = lax.dot_general(
                 jnp.concatenate(sources, axis=0),
                 mats_ref[p],
                 (((1,), (1,)), ((), ())),
                 preferred_element_type=jnp.float32,
             )
-            both = jnp.where(low, both[:bands], both[bands:])
+            halves = [
+                scale_ref[0, 2 * p + q] * each[2 * q * bands : (2 * q + 1) * bands]
+                + scale_ref[1, 2 * p + q] * each[(2 * q + 1) * bands : (2 * q + 2) * bands]
+                for q in range(2)
+            ]
+            both = jnp.where(low, halves[0], halves[1])
             mixed_ref[part, :, lanes] = (picked[p].astype(jnp.float32) + both).astype(jnp.bfloat16)
 
         tiles(part, at, one)
@@ -378,9 +386,11 @@
 
 
 def shares_everywhere(x):
+    shape = x.shape
+    x = x.reshape(-1, LANES)
     x = total_over(x, "mem", (1,))
-    x = total_over(x, "col", range(1, lax.axis_size("col")))
-    return [x] + [swap(x, "mem", k) for k in range(2, lax.axis_size("mem"), 2)]
+    x = total_over(x, "mem", range(2, lax.axis_size("mem"), 2))
+    return [y.reshape(shape) for y in [x] + [swap(x, "col", k) for k in range(1, lax.axis_size("col"))]]
 
 
 def scatter_members(field):
@@ -442,8 +452,7 @@
     weight, value, precision = (a.reshape(1, nobs) for a in (weight, value, precision))
 
     tiles = min(TILES, ncols // LANES)
-    scales = jnp.repeat(block_scale, width, axis=1)[:, None, :]
-    mats = (blocks.astype(jnp.float32) * scales).astype(jnp.bfloat16).reshape(pairs, LANES, depth)
+    mats = blocks.reshape(pairs, LANES, depth)
     which = jnp.arange(block_cols.shape[1], dtype=jnp.int32)[None, :]
     spots = (((block_cols & 1) ^ which) * pairs + (block_cols >> 1)).reshape(-1)
 
@@ -472,13 +481,14 @@
 
     def middle(moved):
         vmem = pl.BlockSpec(memory_space=pltpu.VMEM)
+        smem = pl.BlockSpec(memory_space=pltpu.SMEM)
         return pl.pallas_call(
             horizontal_kernel,
             out_shape=(
                 pltpu.VMEM((bands, nodes), jnp.float32),
                 pltpu.VMEM(moved_shape.shape, moved_shape.dtype),
             ),
-            in_specs=[pl.BlockSpec(memory_space=pltpu.SMEM), vmem, vmem],
+            in_specs=[smem, smem, vmem, vmem],
             out_specs=(vmem, vmem),
             scratch_shapes=[
                 pltpu.VMEM((2, 2 * tiles, bands, LANES), jnp.float32),
@@ -490,6 +500,7 @@
             name="horizontal",
         )(
             spots,
+            block_scale.T,
             pltpu.with_memory_space_constraint(moved, pltpu.VMEM),
             pltpu.with_memory_space_constraint(mats, pltpu.VMEM),
         )

time: 126 us -> 123 us (0.976)
  other arithmetic: 11.3 us -> 8.87 us
  Pallas kernels: 24.9 us -> 26.4 us
    convert_element_type x1 -> x0, other arithmetic: 2.25 us -> none  [per_device(): (blocks.astype(jnp.float32) * scales).astype(jnp.bfloat16)]
    ppermute x18, waiting for transfers between devices: 22.9 us -> 20.8 us  [swap(): return lax.ppermute(x, axis, [(i, i ^ offset) for i in range(n)])]
    all_to_all x1, waiting for transfers between devices: 6 us -> 7.73 us  [per_device(): moved = lax.all_to_all(sent, 'col', 0, 0, tiled=True)]
  transfers between devices with their start and end apart: 19 -> 19, of which waited for: 16 -> 16; matrix products, arithmetic and copies ran while one was open for 3% -> 1% of each run, Pallas kernels for 0% -> 0%
where the time goes in v6:
time: 123 us; the launch traced here: 122 us
  blocking collectives  29.8 us (24%)
  waiting for transfers between devices  28.6 us (23%)
  Pallas kernels  26.4 us (21%)
  starting transfers between devices  25.8 us (21%)
  other arithmetic  8.87 us (7%)
  local copies, waits for them, and re-layouts  2.19 us (2%)
    ppermute x18, waiting for transfers between devices, swap(): return lax.ppermute(x, axis, [(i, i ^ offset) for i in range(n)])  20.8 us
    ppermute x18, starting transfers between devices, swap(): return lax.ppermute(x, axis, [(i, i ^ offset) for i in range(n)])  20.5 us
    all_to_all x2, blocking collectives, per_device(): lax.all_to_all(mixed, 'col', 0, 0, tiled=True).reshape(levels, ncols)  19.6 us
    pallas_call x5, Pallas kernels, local_call(): pl.pallas_call(kernel, out_shape=tuple((pltpu.VMEM(o.shape, o.dtype) for...  15.2 us
    pallas_call x2, Pallas kernels, middle(): pl.pallas_call(horizontal_kernel, out_shape=(pltpu.VMEM((bands, nodes), j...  11.2 us
    all_to_all x1, blocking collectives, per_device(): moved = lax.all_to_all(sent, 'col', 0, 0, tiled=True)  10.2 us
    all_to_all x1, waiting for transfers between devices, per_device(): moved = lax.all_to_all(sent, 'col', 0, 0, tiled=True)  7.73 us
    sort x1, other arithmetic, per_device(): lax.sort((order, other % ncols, obs_weight, obs_value, obs_precision), nu...  6.66 us
  transfers between devices with their start and end apart: 19, of which 16 were waited for; matrix products, arithmetic and copies ran while one was open for 1% of the time, Pallas kernels for 0%

profile of v6, /device:TPU:0, one launch (start us, length us, event | category | flops | bytes accessed | tf_op | source)
XLA Modules:
  0.0 122.5 jit_solution(2946350473788937724)
XLA Ops:
  0.7 1.1 fusion.28
  1.7 0.9 fusion.9
  2.6 0.3 convert_reduce_fusion.refs_0_.starts_ref
  2.9 6.7 %sort.33 = (s32[8192]{0:T(1024)S(1)}, s32[8192]{0:T(1024)S(1)}, f32[8192]{0:T(1024)S(1)}, f32[8192]{0:T(1024)S(1)}, f32[8192]{0:T(1024)S(1)}) sort(s32[8192]{0:T(1024)S(1)} %get-tuple-element.50, s32[8192]{0:T(1024)S(1)} %get-tuple-element.61, f32[8192]{0:T(1024)} %param.17, f32[8192]{0:T(1024)} %param.18, f32[8192]{0:T(1024)} %param.19), dimensions={0}, to_apply=%region_0.1 | sort | flops 106496 | bytes 327680 | tf_op jit(solution)/shard_map/sort | solution.py:444
  9.8 4.2 %adjoint.2 = (bf16[4,32,2048]{2,1,0:T(8,128)(2,1)}, f32[1,8192]{1,0:T(1,128)S(1)}) custom-call(s32[65]{0:T(128)S(1)} %convert_reduce_fusion.refs_0_.starts_ref, bf16[128,2048]{1,0:T(8,128)(2,1)} %bitcast.42, bf16[128,128]{1,0:T(8,128)(2,1)} %vert_ref.3, f32[4,8192]{1,0:T(4,128)S(1)} %add_convert_fusion.refs_3_.keys_ref, f32[1,8192]{1,0:T(1,128)S(1)} %bitcast.48, ...), custom_call_target="tpu_custom_call" | custom-call | tf_op jit(solution)/shard_map/adjoint/pallas_call | solution.py:368
  14.0 5.2 %all-to-all-start = ((bf16[4,32,2048]{2,1,0:T(8,128)(2,1)}), bf16[4,32,2048]{2,1,0:T(8,128)(2,1)S(1)}, u32[]{:S(2)}, u32[]{:S(2)}) async-start(bf16[4,32,2048]{2,1,0:T(8,128)(2,1)} %get-tuple-element.32), calls=%async_computation | async-start | bytes 1048576 | tf_op jit(solution)/shard_map/all_to_all | solution.py:523
  19.4 0.1 reshape.63.spots_ref
  19.5 7.7 %all-to-all-done.moved_ref = bf16[4,32,2048]{2,1,0:T(8,128)(2,1)S(1)} async-done(((bf16[4,32,2048]{2,1,0:T(8,128)(2,1)}), bf16[4,32,2048]{2,1,0:T(8,128)(2,1)S(1)}, u32[]{:S(2)}, u32[]{:S(2)}) %all-to-all-start) | async-done | bytes 524320 | tf_op jit(solution)/shard_map/all_to_all | solution.py:523
  27.2 5.6 %horizontal.2 = (f32[32,8192]{1,0:T(8,128)S(1)}, bf16[4,32,2048]{2,1,0:T(8,128)(2,1)S(1)}) custom-call(s32[256]{0:T(256)S(1)} %reshape.63.spots_ref, f32[2,128]{1,0:T(2,128)S(1)} %bitcast.68, bf16[4,32,2048]{2,1,0:T(8,128)(2,1)S(1)} %all-to-all-done.moved_ref, bf16[64,128,128]{2,1,0:T(8,128)(2,1)S(1)} %bitcast.40), custom_call_target="tpu_custom_call" | custom-call | tf_op jit(solution)/shard_map/horizontal/pallas_call | solution.py:485
  32.8 10.1 %all_to_all.20 = bf16[4,32,2048]{2,1,0:T(8,128)(2,1)S(1)} all-to-all(bf16[4,32,2048]{2,1,0:T(8,128)(2,1)S(1)} %get-tuple-element.33), channel_id=1, replica_groups=mesh['mem'=8,'col'=4] {'col'}, dimensions={0} | all-to-all | bytes 1048576 | tf_op jit(solution)/shard_map/all_to_all | solution.py:525
  43.0 3.3 %forward.2 = (bf16[4,256,256]{2,1,0:T(8,128)(2,1)S(1)}, f32[1,8192]{1,0:T(1,128)S(1)}) custom-call(s32[65]{0:T(128)S(1)} %convert_reduce_fusion.refs_0_.starts_ref, f32[4,8192]{1,0:T(4,128)S(1)} %add_convert_fusion.refs_3_.keys_ref, f32[1,8192]{1,0:T(1,128)S(1)} %bitcast.49, bf16[128,2048]{1,0:T(8,128)(2,1)S(1)} %bitcast.47, bf16[128,2048]{1,0:T(8,128)(2,1)S(1)} %bitcast.44, ...), custom_call_target="tpu_custom_call" | custom-call | tf_op jit(solution)/shard_map/forward/pallas_call | solution.py:368
  46.3 1.2 collective-permute-done
  47.5 1.6 %collective-permute-start.1 = (f32[64,128]{1,0:T(8,128)S(1)}, f32[64,128]{1,0:T(8,128)S(1)}, u32[]{:S(2)}, u32[]{:S(2)}) collective-permute-start(f32[64,128]{1,0:T(8,128)S(1)} %add.121), channel_id=1, source_target_pairs={{0,8},{4,12},{8,0},{12,4},{16,24},{20,28},{24,16},{28,20},{1,9},{5... | collective-permute-start | bytes 98312 | tf_op jit(solution)/shard_map/ppermute | solution.py:381
  49.1 2.6 %collective-permute-start.2 = (f32[64,128]{1,0:T(8,128)S(1)}, f32[64,128]{1,0:T(8,128)S(1)}, u32[]{:S(2)}, u32[]{:S(2)}) collective-permute-start(f32[64,128]{1,0:T(8,128)S(1)} %add.121), channel_id=1, source_target_pairs={{0,16},{4,20},{8,24},{12,28},{16,0},{20,4},{24,8},{28,12},{1,17},{... | collective-permute-start | bytes 98312 | tf_op jit(solution)/shard_map/ppermute | solution.py:381
  51.7 0.2 collective-permute-start.3
  51.9 2.6 %collective-permute-done.2 = f32[64,128]{1,0:T(8,128)S(1)} collective-permute-done((f32[64,128]{1,0:T(8,128)S(1)}, f32[64,128]{1,0:T(8,128)S(1)}, u32[]{:S(2)}, u32[]{:S(2)}) %collective-permute-start.2) | collective-permute-done | bytes 32800 | tf_op jit(solution)/shard_map/ppermute | solution.py:381
  54.5 2.9 %collective-permute-done.3 = f32[64,128]{1,0:T(8,128)S(1)} collective-permute-done((f32[64,128]{1,0:T(8,128)S(1)}, f32[64,128]{1,0:T(8,128)S(1)}, u32[]{:S(2)}, u32[]{:S(2)}) %collective-permute-start.3) | collective-permute-done | bytes 32800 | tf_op jit(solution)/shard_map/ppermute | solution.py:381
  57.4 1.0 collective-permute-start.4
  58.4 0.6 collective-permute-start.5
  59.0 2.0 %collective-permute-start.6 = (f32[64,128]{1,0:T(8,128)S(1)}, f32[64,128]{1,0:T(8,128)S(1)}, u32[]{:S(2)}, u32[]{:S(2)}) collective-permute-start(f32[64,128]{1,0:T(8,128)S(1)} %add_add_fusion.1), channel_id=1, source_target_pairs={{0,3},{1,2},{2,1},{3,0},{4,7},{5,6},{6,5},{7,4},{8,11},{9,10},{10,... | collective-permute-start | bytes 98312 | tf_op jit(solution)/shard_map/ppermute | solution.py:381
  61.0 0.4 collective-permute-done.4
  61.4 0.9 collective-permute-done.5
  62.3 1.5 %collective-permute-done.6 = f32[64,128]{1,0:T(8,128)S(1)} collective-permute-done((f32[64,128]{1,0:T(8,128)S(1)}, f32[64,128]{1,0:T(8,128)S(1)}, u32[]{:S(2)}, u32[]{:S(2)}) %collective-permute-start.6) | collective-permute-done | bytes 32800 | tf_op jit(solution)/shard_map/ppermute | solution.py:381
  63.8 3.6 %adjoint.3 = (bf16[4,32,2048]{2,1,0:T(8,128)(2,1)S(1)}, f32[1,8192]{1,0:T(1,128)S(1)}, f32[1,128]{1,0:T(1,128)S(1)}, f32[1,128]{1,0:T(1,128)S(1)}, f32[1,8192]{1...) custom-call(s32[65]{0:T(128)S(1)} %convert_reduce_fusion.refs_0_.starts_ref, bf16[128,2048]{1,0:T(8,128)(2,1)} %bitcast.43, ...), custom_call_target="tpu_custom_call" | custom-call | tf_op jit(solution)/shard_map/adjoint/pallas_call | solution.py:368
  67.4 10.2 %all_to_all.21.moved_ref = bf16[4,32,2048]{2,1,0:T(8,128)(2,1)S(1)} all-to-all(bf16[4,32,2048]{2,1,0:T(8,128)(2,1)S(1)} %get-tuple-element.39), channel_id=1, replica_groups=mesh['mem'=8,'col'=4] {'col'}, dimensions={0} | all-to-all | bytes 1048576 | tf_op jit(solution)/shard_map/all_to_all | solution.py:523
  77.6 5.6 %horizontal.3 = (f32[32,8192]{1,0:T(8,128)S(1)}, bf16[4,32,2048]{2,1,0:T(8,128)(2,1)S(1)}) custom-call(s32[256]{0:T(256)S(1)} %reshape.63.spots_ref, f32[2,128]{1,0:T(2,128)S(1)} %bitcast.69, bf16[4,32,2048]{2,1,0:T(8,128)(2,1)S(1)} %all_to_all.21.moved_ref, bf16[64,128,128]{2,1,0:T(8,128)(2,1)S(1)} %bitcast.41), custom_call_target="tpu_custom_call" | custom-call | tf_op jit(solution)/shard_map/horizontal/pallas_call | solution.py:485
  83.2 9.5 %all_to_all.22 = bf16[4,32,2048]{2,1,0:T(8,128)(2,1)S(1)} all-to-all(bf16[4,32,2048]{2,1,0:T(8,128)(2,1)S(1)} %get-tuple-element.40), channel_id=1, replica_groups=mesh['mem'=8,'col'=4] {'col'}, dimensions={0} | all-to-all | bytes 1048576 | tf_op jit(solution)/shard_map/all_to_all | solution.py:525
  92.7 3.3 %forward.3 = (bf16[4,256,256]{2,1,0:T(8,128)(2,1)S(1)}, f32[1,8192]{1,0:T(1,128)S(1)}) custom-call(s32[65]{0:T(128)S(1)} %convert_reduce_fusion.refs_0_.starts_ref, f32[4,8192]{1,0:T(4,128)S(1)} %add_convert_fusion.refs_3_.keys_ref, f32[1,8192]{1,0:T(1,128)S(1)} %bitcast.51, bf16[128,2048]{1,0:T(8,128)(2,1)S(1)} %bitcast.46, bf16[128,2048]{1,0:T(8,128)(2,1)S(1)} %bitcast.45, ...), custom_call_target="tpu_custom_call" | custom-call | tf_op jit(solution)/shard_map/forward/pallas_call | solution.py:368
  96.1 1.2 collective-permute-done.7
  97.3 0.4 collective-permute-start.10
  97.6 4.0 %collective-permute-start.9 = (f32[64,128]{1,0:T(8,128)S(1)}, f32[64,128]{1,0:T(8,128)S(1)}, u32[]{:S(2)}, u32[]{:S(2)}) collective-permute-start(f32[64,128]{1,0:T(8,128)S(1)} %add.125), channel_id=1, source_target_pairs={{0,16},{4,20},{8,24},{12,28},{16,0},{20,4},{24,8},{28,12},{1,17},{... | collective-permute-start | bytes 98312 | tf_op jit(solution)/shard_map/ppermute | solution.py:381
  101.7 1.6 %collective-permute-done.10 = f32[64,128]{1,0:T(8,128)S(1)} collective-permute-done((f32[64,128]{1,0:T(8,128)S(1)}, f32[64,128]{1,0:T(8,128)S(1)}, u32[]{:S(2)}, u32[]{:S(2)}) %collective-permute-start.10) | collective-permute-done | bytes 32800 | tf_op jit(solution)/shard_map/ppermute | solution.py:381
  103.2 0.3 collective-permute-done.9
  103.6 1.0 collective-permute-start.11
  104.6 0.4 collective-permute-start.12
  104.9 2.2 %collective-permute-start.13 = (f32[64,128]{1,0:T(8,128)S(1)}, f32[64,128]{1,0:T(8,128)S(1)}, u32[]{:S(2)}, u32[]{:S(2)}) collective-permute-start(f32[64,128]{1,0:T(8,128)S(1)} %add_add_fusion), channel_id=1, source_target_pairs={{0,3},{1,2},{2,1},{3,0},{4,7},{5,6},{6,5},{7,4},{8,11},{9,10},{10,... | collective-permute-start | bytes 98312 | tf_op jit(solution)/shard_map/ppermute | solution.py:381
  107.1 0.4 collective-permute-done.11
  107.6 0.9 collective-permute-done.12
  108.5 1.3 %collective-permute-done.13 = f32[64,128]{1,0:T(8,128)S(1)} collective-permute-done((f32[64,128]{1,0:T(8,128)S(1)}, f32[64,128]{1,0:T(8,128)S(1)}, u32[]{:S(2)}, u32[]{:S(2)}) %collective-permute-start.13) | collective-permute-done | bytes 32800 | tf_op jit(solution)/shard_map/ppermute | solution.py:381
  109.8 0.9 finish.1
  110.8 1.5 %collective-permute-done.14 = bf16[4,16,2048]{2,1,0:T(8,128)(2,1)S(1)} collective-permute-done((bf16[4,16,2048]{2,1,0:T(8,128)(2,1)S(1)}, bf16[4,16,2048]{2,1,0:T(8,128)(2,1)S(1)}, u32[]{:S(2)}, u32[]{:S(2)}) %collective-permute-start.14) | collective-permute-done | bytes 262176 | tf_op jit(solution)/shard_map/ppermute | solution.py:381
  112.4 1.0 collective-permute-start.15
  113.4 2.3 %collective-permute-start.16 = (bf16[16,2048]{1,0:T(8,128)(2,1)S(1)}, bf16[16,2048]{1,0:T(8,128)(2,1)S(1)}, u32[]{:S(2)}, u32[]{:S(2)}) collective-permute-start(bf16[16,2048]{1,0:T(8,128)(2,1)S(1)} %get-tuple-element.54), channel_id=1, source_target_pairs={{0,16},{4,20},{8,24},{12,28},{16,0},{20,4},{24,8},{28,12},{1,17},{... | collective-permute-start | bytes 196616 | tf_op jit(solution)/shard_map/ppermute | solution.py:381
  115.7 1.1 collective-permute-start.17
  116.9 0.8 copy.14
  117.7 1.3 %collective-permute-done.16 = bf16[16,2048]{1,0:T(8,128)(2,1)S(1)} collective-permute-done((bf16[16,2048]{1,0:T(8,128)(2,1)S(1)}, bf16[16,2048]{1,0:T(8,128)(2,1)S(1)}, u32[]{:S(2)}, u32[]{:S(2)}) %collective-permute-start.16) | collective-permute-done | bytes 65568 | tf_op jit(solution)/shard_map/ppermute | solution.py:381
  119.0 2.8 %collective-permute-done.17 = bf16[16,2048]{1,0:T(8,128)(2,1)S(1)} collective-permute-done((bf16[16,2048]{1,0:T(8,128)(2,1)S(1)}, bf16[16,2048]{1,0:T(8,128)(2,1)S(1)}, u32[]{:S(2)}, u32[]{:S(2)}) %collective-permute-start.17) | collective-permute-done | bytes 65568 | tf_op jit(solution)/shard_map/ppermute | solution.py:381
  121.8 0.7 fusion.2
  (32 shorter events, 0.7 us)
Async XLA Ops:
  0.6 18.6 %copy-start.6 = (s32[128,2]{0,1:T(2,128)S(1)}, s32[128,2]{0,1:T(2,128)}, u32[]{:S(2)}) copy-start(s32[128,2]{0,1:T(2,128)} %param.14) | copy-start | bytes 3076
  0.6 26.6 %copy-start.5 = (f32[128,2]{0,1:T(2,128)S(1)}, f32[128,2]{0,1:T(2,128)}, u32[]{:S(2)}) copy-start(f32[128,2]{0,1:T(2,128)} %param.13) | copy-start | bytes 3076
  0.7 26.6 %copy-start = (bf16[128,64,128]{2,1,0:T(8,128)(2,1)S(1)}, bf16[128,64,128]{2,1,0:T(8,128)(2,1)}, u32[]{:S(2)}) copy-start(bf16[128,64,128]{2,1,0:T(8,128)(2,1)} %param.12) | copy-start | bytes 6291460
  14.0 13.2 %all-to-all-start = ((bf16[4,32,2048]{2,1,0:T(8,128)(2,1)}), bf16[4,32,2048]{2,1,0:T(8,128)(2,1)S(1)}, u32[]{:S(2)}, u32[]{:S(2)}) async-start(bf16[4,32,2048]{2,1,0:T(8,128)(2,1)} %get-tuple-element.32), calls=%async_computation | async-start | bytes 1048576 | tf_op jit(solution)/shard_map/all_to_all | solution.py:523
  19.2 23.7 %copy-start.1 = (bf16[1,128,2048]{2,1,0:T(8,128)(2,1)S(1)}, bf16[1,128,2048]{2,1,0:T(8,128)(2,1)}, u32[]{:S(2)}) copy-start(bf16[1,128,2048]{2,1,0:T(8,128)(2,1)} %param.10) | copy-start | bytes 1572868
  19.2 23.7 %copy-start.3 = (bf16[128,128]{1,0:T(8,128)(2,1)S(1)}, bf16[128,128]{1,0:T(8,128)(2,1)}, u32[]{:S(2)}) copy-start(bf16[128,128]{1,0:T(8,128)(2,1)} %vert_ref.3) | copy-start | bytes 98308
  46.2 1.3 %collective-permute-start = (f32[64,128]{1,0:T(8,128)S(1)}, f32[64,128]{1,0:T(8,128)S(1)}, u32[]{:S(2)}, u32[]{:S(2)}) collective-permute-start(f32[64,128]{1,0:T(8,128)S(1)} %bitcast.65), channel_id=1, source_target_pairs={{0,4},{4,0},{8,12},{12,8},{16,20},{20,16},{24,28},{28,24},{1,5},{5... | collective-permute-start | bytes 98312 | tf_op jit(solution)/shard_map/ppermute | solution.py:381
  47.5 4.4 %collective-permute-start.1 = (f32[64,128]{1,0:T(8,128)S(1)}, f32[64,128]{1,0:T(8,128)S(1)}, u32[]{:S(2)}, u32[]{:S(2)}) collective-permute-start(f32[64,128]{1,0:T(8,128)S(1)} %add.121), channel_id=1, source_target_pairs={{0,8},{4,12},{8,0},{12,4},{16,24},{20,28},{24,16},{28,20},{1,9},{5... | collective-permute-start | bytes 98312 | tf_op jit(solution)/shard_map/ppermute | solution.py:381
  49.1 5.4 %collective-permute-start.2 = (f32[64,128]{1,0:T(8,128)S(1)}, f32[64,128]{1,0:T(8,128)S(1)}, u32[]{:S(2)}, u32[]{:S(2)}) collective-permute-start(f32[64,128]{1,0:T(8,128)S(1)} %add.121), channel_id=1, source_target_pairs={{0,16},{4,20},{8,24},{12,28},{16,0},{20,4},{24,8},{28,12},{1,17},{... | collective-permute-start | bytes 98312 | tf_op jit(solution)/shard_map/ppermute | solution.py:381
  51.7 5.7 %collective-permute-start.3 = (f32[64,128]{1,0:T(8,128)S(1)}, f32[64,128]{1,0:T(8,128)S(1)}, u32[]{:S(2)}, u32[]{:S(2)}) collective-permute-start(f32[64,128]{1,0:T(8,128)S(1)} %add.121), channel_id=1, source_target_pairs={{0,24},{4,28},{8,16},{12,20},{16,8},{20,12},{24,0},{28,4},{1,25},{... | collective-permute-start | bytes 98312 | tf_op jit(solution)/shard_map/ppermute | solution.py:381
  57.4 4.0 %collective-permute-start.4 = (f32[64,128]{1,0:T(8,128)S(1)}, f32[64,128]{1,0:T(8,128)S(1)}, u32[]{:S(2)}, u32[]{:S(2)}) collective-permute-start(f32[64,128]{1,0:T(8,128)S(1)} %add_add_fusion.1), channel_id=1, source_target_pairs={{0,1},{1,0},{2,3},{3,2},{4,5},{5,4},{6,7},{7,6},{8,9},{9,8},{10,11... | collective-permute-start | bytes 98312 | tf_op jit(solution)/shard_map/ppermute | solution.py:381
  58.4 3.9 %collective-permute-start.5 = (f32[64,128]{1,0:T(8,128)S(1)}, f32[64,128]{1,0:T(8,128)S(1)}, u32[]{:S(2)}, u32[]{:S(2)}) collective-permute-start(f32[64,128]{1,0:T(8,128)S(1)} %add_add_fusion.1), channel_id=1, source_target_pairs={{0,2},{1,3},{2,0},{3,1},{4,6},{5,7},{6,4},{7,5},{8,10},{9,11},{10,... | collective-permute-start | bytes 98312 | tf_op jit(solution)/shard_map/ppermute | solution.py:381
  59.0 4.8 %collective-permute-start.6 = (f32[64,128]{1,0:T(8,128)S(1)}, f32[64,128]{1,0:T(8,128)S(1)}, u32[]{:S(2)}, u32[]{:S(2)}) collective-permute-start(f32[64,128]{1,0:T(8,128)S(1)} %add_add_fusion.1), channel_id=1, source_target_pairs={{0,3},{1,2},{2,1},{3,0},{4,7},{5,6},{6,5},{7,4},{8,11},{9,10},{10,... | collective-permute-start | bytes 98312 | tf_op jit(solution)/shard_map/ppermute | solution.py:381
  77.6 15.1 %copy-start.2 = (bf16[1,128,2048]{2,1,0:T(8,128)(2,1)S(1)}, bf16[1,128,2048]{2,1,0:T(8,128)(2,1)}, u32[]{:S(2)}) copy-start(bf16[1,128,2048]{2,1,0:T(8,128)(2,1)} %param.10) | copy-start | bytes 1572868
  77.6 15.1 %copy-start.4 = (bf16[128,128]{1,0:T(8,128)(2,1)S(1)}, bf16[128,128]{1,0:T(8,128)(2,1)}, u32[]{:S(2)}) copy-start(bf16[128,128]{1,0:T(8,128)(2,1)} %vert_ref.3) | copy-start | bytes 98308
  96.0 1.3 %collective-permute-start.7 = (f32[64,128]{1,0:T(8,128)S(1)}, f32[64,128]{1,0:T(8,128)S(1)}, u32[]{:S(2)}, u32[]{:S(2)}) collective-permute-start(f32[64,128]{1,0:T(8,128)S(1)} %bitcast.63), channel_id=1, source_target_pairs={{0,4},{4,0},{8,12},{12,8},{16,20},{20,16},{24,28},{28,24},{1,5},{5... | collective-permute-start | bytes 98312 | tf_op jit(solution)/shard_map/ppermute | solution.py:381
  97.3 6.0 %collective-permute-start.10 = (f32[64,128]{1,0:T(8,128)S(1)}, f32[64,128]{1,0:T(8,128)S(1)}, u32[]{:S(2)}, u32[]{:S(2)}) collective-permute-start(f32[64,128]{1,0:T(8,128)S(1)} %add.125), channel_id=1, source_target_pairs={{0,24},{4,28},{8,16},{12,20},{16,8},{20,12},{24,0},{28,4},{1,25},{... | collective-permute-start | bytes 98312 | tf_op jit(solution)/shard_map/ppermute | solution.py:381
  97.6 5.6 %collective-permute-start.8 = (f32[64,128]{1,0:T(8,128)S(1)}, f32[64,128]{1,0:T(8,128)S(1)}, u32[]{:S(2)}, u32[]{:S(2)}) collective-permute-start(f32[64,128]{1,0:T(8,128)S(1)} %add.125), channel_id=1, source_target_pairs={{0,8},{4,12},{8,0},{12,4},{16,24},{20,28},{24,16},{28,20},{1,9},{5... | collective-permute-start | bytes 98312 | tf_op jit(solution)/shard_map/ppermute | solution.py:381
  97.6 6.0 %collective-permute-start.9 = (f32[64,128]{1,0:T(8,128)S(1)}, f32[64,128]{1,0:T(8,128)S(1)}, u32[]{:S(2)}, u32[]{:S(2)}) collective-permute-start(f32[64,128]{1,0:T(8,128)S(1)} %add.125), channel_id=1, source_target_pairs={{0,16},{4,20},{8,24},{12,28},{16,0},{20,4},{24,8},{28,12},{1,17},{... | collective-permute-start | bytes 98312 | tf_op jit(solution)/shard_map/ppermute | solution.py:381
  103.6 4.0 %collective-permute-start.11 = (f32[64,128]{1,0:T(8,128)S(1)}, f32[64,128]{1,0:T(8,128)S(1)}, u32[]{:S(2)}, u32[]{:S(2)}) collective-permute-start(f32[64,128]{1,0:T(8,128)S(1)} %add_add_fusion), channel_id=1, source_target_pairs={{0,1},{1,0},{2,3},{3,2},{4,5},{5,4},{6,7},{7,6},{8,9},{9,8},{10,11... | collective-permute-start | bytes 98312 | tf_op jit(solution)/shard_map/ppermute | solution.py:381
  104.6 3.9 %collective-permute-start.12 = (f32[64,128]{1,0:T(8,128)S(1)}, f32[64,128]{1,0:T(8,128)S(1)}, u32[]{:S(2)}, u32[]{:S(2)}) collective-permute-start(f32[64,128]{1,0:T(8,128)S(1)} %add_add_fusion), channel_id=1, source_target_pairs={{0,2},{1,3},{2,0},{3,1},{4,6},{5,7},{6,4},{7,5},{8,10},{9,11},{10,... | collective-permute-start | bytes 98312 | tf_op jit(solution)/shard_map/ppermute | solution.py:381
  104.9 4.8 %collective-permute-start.13 = (f32[64,128]{1,0:T(8,128)S(1)}, f32[64,128]{1,0:T(8,128)S(1)}, u32[]{:S(2)}, u32[]{:S(2)}) collective-permute-start(f32[64,128]{1,0:T(8,128)S(1)} %add_add_fusion), channel_id=1, source_target_pairs={{0,3},{1,2},{2,1},{3,0},{4,7},{5,6},{6,5},{7,4},{8,11},{9,10},{10,... | collective-permute-start | bytes 98312 | tf_op jit(solution)/shard_map/ppermute | solution.py:381
  110.7 1.6 %collective-permute-start.14 = (bf16[4,16,2048]{2,1,0:T(8,128)(2,1)S(1)}, bf16[4,16,2048]{2,1,0:T(8,128)(2,1)S(1)}, u32[]{:S(2)}, u32[]{:S(2)}) collective-permute-start(bf16[4,16,2048]{2,1,0:T(8,128)(2,1)S(1)} %slice_bitcast_fusion), channel_id=1, source_target_pairs={{0,4},{4,0},{8,12},{12,8},{16,20},{20,16},{24,28},{28,24},{1,5},{5... | collective-permute-start | bytes 786440 | tf_op jit(solution)/shard_map/ppermute | solution.py:381
  112.4 5.2 %collective-permute-start.15 = (bf16[16,2048]{1,0:T(8,128)(2,1)S(1)}, bf16[16,2048]{1,0:T(8,128)(2,1)S(1)}, u32[]{:S(2)}, u32[]{:S(2)}) collective-permute-start(bf16[16,2048]{1,0:T(8,128)(2,1)S(1)} %get-tuple-element.52), channel_id=1, source_target_pairs={{0,8},{4,12},{8,0},{12,4},{16,24},{20,28},{24,16},{28,20},{1,9},{5... | collective-permute-start | bytes 196616 | tf_op jit(solution)/shard_map/ppermute | solution.py:381
  113.4 5.6 %collective-permute-start.16 = (bf16[16,2048]{1,0:T(8,128)(2,1)S(1)}, bf16[16,2048]{1,0:T(8,128)(2,1)S(1)}, u32[]{:S(2)}, u32[]{:S(2)}) collective-permute-start(bf16[16,2048]{1,0:T(8,128)(2,1)S(1)} %get-tuple-element.54), channel_id=1, source_target_pairs={{0,16},{4,20},{8,24},{12,28},{16,0},{20,4},{24,8},{28,12},{1,17},{... | collective-permute-start | bytes 196616 | tf_op jit(solution)/shard_map/ppermute | solution.py:381
  115.7 6.1 %collective-permute-start.17 = (bf16[16,2048]{1,0:T(8,128)(2,1)S(1)}, bf16[16,2048]{1,0:T(8,128)(2,1)S(1)}, u32[]{:S(2)}, u32[]{:S(2)}) collective-permute-start(bf16[16,2048]{1,0:T(8,128)(2,1)S(1)} %get-tuple-element.53), channel_id=1, source_target_pairs={{0,24},{4,28},{8,16},{12,20},{16,8},{20,12},{24,0},{28,4},{1,25},{... | collective-permute-start | bytes 196616 | tf_op jit(solution)/shard_map/ppermute | solution.py:381

commit v7 on v6

--- a/solution.py
+++ b/solution.py
@@ -15,7 +15,7 @@
 ROWS = 256
 FIRST = 768
 SECOND = 384
-TILES = 8
+TILES = 16
 VMEM_BYTES = 24 << 20
 
 
@@ -71,9 +71,9 @@
 
 
 def advance(seen_refs, precision, errors, previous):
-    seen = seen_refs[0][...]
+    seen = seen_refs[0][...].astype(jnp.float32)
     for ref in seen_refs[1:]:
-        seen = seen + ref[...]
+        seen = seen + ref[...].astype(jnp.float32)
     norm = total_of(errors * seen)
     if previous is None:
         beta = jnp.zeros_like(norm)
@@ -102,7 +102,7 @@
     if seen:
         before, refs = (None, refs) if first else ([r[...] for r in refs[:3]], refs[3:])
         seen_refs, refs = refs[:seen], refs[seen:]
-        out_ref, new_ref, alpha_ref, beta_ref, guide_ref, image_ref, norm_ref, total, field = refs
+        out_ref, new_ref, alpha_ref, beta_ref, guide_ref, image_ref, norm_ref, field = refs
         if before is not None:
             before[2] = before[2][:, :1]
         errors, precision = err_ref[...], precision_ref[...]
@@ -113,45 +113,49 @@
         for ref, value in ((alpha_ref, alpha), (beta_ref, beta), (norm_ref, norm)):
             ref[...] = jnp.broadcast_to(value, ref.shape)
     else:
-        out_ref, new_ref, total, field = refs
+        out_ref, new_ref, field = refs
         new_ref[...] = precision_ref[...] * err_ref[...]
     bands = out_ref.shape[1]
     nobs = weight_ref.shape[1]
     ncol = lax.axis_size("col")
     mine = lax.axis_index("col")
 
+    def product(g, trip):
+        above, beside = [], []
+        for run in runs_of(starts_ref, g, mine, ncol):
+            which = run[0]
+            span, valid = window_of(run, trip, nobs)
+            weight = weight_ref[:, span]
+            weight = 1.0 - weight if which else weight
+            row = jnp.where(valid, keys_ref[2 * which : 2 * which + 1, span], -1.0)
+            lane = keys_ref[2 * which + 1 : 2 * which + 2, span]
+            width = width_of(which)
+            above.append(one_hot(row, row_numbers(rows, width), (weight * new_ref[:, span]).astype(jnp.bfloat16)))
+            beside.append(one_hot(lane, row_numbers(wide, width), jnp.ones((1, width), jnp.bfloat16)))
+        return lax.dot_general(
+            jnp.concatenate(above, axis=1),
+            jnp.concatenate(beside, axis=1),
+            (((1,), (1,)), ((), ())),
+            preferred_element_type=jnp.float32,
+        )
+
+    for g in range(levels // group):
+        result = product(g, 0)
+        for c in range(chunks):
+            field[g * group : (g + 1) * group, c * wide : (c + 1) * wide] = result[c * group : (c + 1) * group]
+
     def collect(g, carry):
-        total[...] = jnp.zeros_like(total)
-        runs = runs_of(starts_ref, g, mine, ncol)
+        here = pl.ds(pl.multiple_of(g * group, group), group)
 
         def step(trip, carry):
-            above, beside = [], []
-            for run in runs:
-                which = run[0]
-                span, valid = window_of(run, trip, nobs)
-                weight = weight_ref[:, span]
-                weight = 1.0 - weight if which else weight
-                row = jnp.where(valid, keys_ref[2 * which : 2 * which + 1, span], -1.0)
-                lane = keys_ref[2 * which + 1 : 2 * which + 2, span]
-                width = width_of(which)
-                above.append(one_hot(row, row_numbers(rows, width), (weight * new_ref[:, span]).astype(jnp.bfloat16)))
-                beside.append(one_hot(lane, row_numbers(wide, width), jnp.ones((1, width), jnp.bfloat16)))
-            total[...] += lax.dot_general(
-                jnp.concatenate(above, axis=1),
-                jnp.concatenate(beside, axis=1),
-                (((1,), (1,)), ((), ())),
-                preferred_element_type=jnp.float32,
-            )
+            result = product(g, trip)
+            for c in range(chunks):
+                field[here, c * wide : (c + 1) * wide] += result[c * group : (c + 1) * group]
             return carry
 
-        lax.fori_loop(0, trips_of(runs), step, 0)
-        here = pl.ds(pl.multiple_of(g * group, group), group)
-        for c in range(chunks):
-            field[here, c * wide : (c + 1) * wide] = total[c * group : (c + 1) * group, :]
-        return carry
+        return lax.fori_loop(1, trips_of(runs_of(starts_ref, g, mine, ncol)), step, carry)
 
     lax.fori_loop(0, levels // group, collect, 0)
-
     for copy in copies:
         copy.wait()
     scale_inv = 1.0 / math.sqrt(members)
@@ -187,7 +191,10 @@
             body(u, part * per_part + at + u, lanes)
 
     def over(part, function):
-        lax.fori_loop(0, per_part // group, lambda n, c: function(part, n * group, n % 2) or c, 0)
+        if per_part == group:
+            function(part, 0, 0)
+        else:
+            lax.fori_loop(0, per_part // group, lambda n, c: function(part, n * group, n % 2) or c, 0)
 
     def products(part, at, slot):
         def one(u, p, lanes):
@@ -207,7 +214,13 @@
             for k in range(2):
                 sums[k][spots_ref[2 * base + 2 * n + k]] += term
 
+    steps = per_part // group
     for part in range(parts):
+        if steps == 1:
+            products(part, 0, part % 2)
+            if part > 0:
+                scatter(2 * (part - 1) * per_part, (part - 1) % 2)
+            continue
         products(part, 0, 0)
 
         def step(n, carry):
@@ -215,9 +228,10 @@
             products(part, n * group, n % 2)
             return carry
 
-        steps = per_part // group
         lax.fori_loop(1, steps, step, 0)
         scatter(2 * (part * per_part + (steps - 1) * group), (steps - 1) % 2)
+    if steps == 1:
+        scatter(2 * (parts - 1) * per_part, (parts - 1) % 2)
 
     def join(part, at, slot):
         def one(u, p, lanes):
@@ -284,36 +298,40 @@
     ncol = lax.axis_size("col")
     mine = lax.axis_index("col")
 
+    def gathered(g, trip):
+        runs = runs_of(starts_ref, g, mine, ncol)
+        spans, rights, hots, rows_of = [], [], [], []
+        for run in runs:
+            which = run[0]
+            span, valid = window_of(run, trip, nobs)
+            width = width_of(which)
+            lane = keys_ref[2 * which + 1 : 2 * which + 2, span]
+            hots.append(one_hot(lane, row_numbers(wide, width), jnp.ones((1, width), jnp.bfloat16)))
+            rows_of.append(jnp.where(valid, keys_ref[2 * which : 2 * which + 1, span], -1.0))
+            weight = weight_ref[:, span]
+            rights.append(1.0 - weight if which else weight)
+            spans.append(span)
+        hot = jnp.concatenate(hots, axis=1)
+        lines = jnp.dot(field_ref[g], hot, preferred_element_type=jnp.float32).astype(jnp.bfloat16)
+        at = 0
+        for span, right, row in zip(spans, rights, rows_of):
+            width = row.shape[1]
+            kept = one_hot(row, row_numbers(rows, width), lines[:, at : at + width])
+            found = kept[:SUBLANES]
+            for r in range(SUBLANES, rows, SUBLANES):
+                found = found + kept[r : r + SUBLANES]
+            obs_ref[:, span] += right * jnp.sum(found.astype(jnp.float32), axis=0, keepdims=True)
+            at += width
+
+    for g in range(levels // group):
+        gathered(g, 0)
+
     def collect(g, carry):
-        runs = runs_of(starts_ref, g, mine, ncol)
-
         def step(trip, carry):
-            spans, rights, hots, rows_of = [], [], [], []
-            for run in runs:
-                which = run[0]
-                span, valid = window_of(run, trip, nobs)
-                width = width_of(which)
-                lane = keys_ref[2 * which + 1 : 2 * which + 2, span]
-                hots.append(one_hot(lane, row_numbers(wide, width), jnp.ones((1, width), jnp.bfloat16)))
-                rows_of.append(jnp.where(valid, keys_ref[2 * which : 2 * which + 1, span], -1.0))
-                weight = weight_ref[:, span]
-                rights.append(1.0 - weight if which else weight)
-                spans.append(span)
-            hot = jnp.concatenate(hots, axis=1)
-            lines = jnp.dot(field_ref[g], hot, preferred_element_type=jnp.float32).astype(jnp.bfloat16)
-            at = 0
-            for span, right, row in zip(spans, rights, rows_of):
-                width = row.shape[1]
-                kept = one_hot(row, row_numbers(rows, width), lines[:, at : at + width])
-                found = kept[:SUBLANES]
-                for r in range(SUBLANES, rows, SUBLANES):
-                    found = found + kept[r : r + SUBLANES]
-                obs_ref[:, span] += right * jnp.sum(found.astype(jnp.float32), axis=0, keepdims=True)
-                at += width
+            gathered(g, trip)
             return carry
 
-        lax.fori_loop(0, trips_of(runs), step, 0)
-        return carry
+        return lax.fori_loop(1, trips_of(runs_of(starts_ref, g, mine, ncol)), step, carry)
 
     lax.fori_loop(0, levels // group, collect, 0)
 
@@ -382,14 +400,14 @@
 
 
 def total_over(x, axis, offsets):
-    return sum([swap(x, axis, k) for k in offsets], x)
+    return sum([swap(x, axis, k).astype(jnp.float32) for k in offsets], x.astype(jnp.float32))
 
 
 def shares_everywhere(x):
     shape = x.shape
     x = x.reshape(-1, LANES)
-    x = total_over(x, "mem", (1,))
-    x = total_over(x, "mem", range(2, lax.axis_size("mem"), 2))
+    x = total_over(x, "mem", (1,)).astype(jnp.bfloat16)
+    x = total_over(x, "mem", range(2, lax.axis_size("mem"), 2)).astype(jnp.bfloat16)
     return [y.reshape(shape) for y in [x] + [swap(x, "col", k) for k in range(1, lax.axis_size("col"))]]
 
 
@@ -470,7 +488,6 @@
             [starts, pert, vertical, keys, weight, precision, errors, *extra],
             "adjoint",
             [
-                pltpu.VMEM((rows, wide), jnp.float32),
                 pltpu.VMEM((levels, ncols), jnp.float32),
                 pltpu.VMEM((levels, ncols), jnp.bfloat16),
                 pltpu.VMEM((levels, levels), jnp.bfloat16),

time: 123 us -> 117 us (0.951)
  Pallas kernels: 26.4 us -> 20.9 us
    pallas_call x2, Pallas kernels: 11.2 us -> 7.6 us  [middle(): pl.pallas_call(horizontal_kernel, out_shape=(pltpu.VMEM((bands, nodes), j...]
    pallas_call x5, Pallas kernels: 15.2 us -> 13.3 us  [local_call(): pl.pallas_call(kernel, out_shape=tuple((pltpu.VMEM(o.shape, o.dtype) for...]
where the time goes in v7:
time: 117 us; the launch traced here: 116 us
  blocking collectives  29.3 us (25%)
  waiting for transfers between devices  27.8 us (24%)
  starting transfers between devices  25.9 us (22%)
  Pallas kernels  20.9 us (18%)
  other arithmetic  8.88 us (8%)
  local copies, waits for them, and re-layouts  2.4 us (2%)
    ppermute x18, starting transfers between devices, swap(): return lax.ppermute(x, axis, [(i, i ^ offset) for i in range(n)])  20.7 us
    ppermute x18, waiting for transfers between devices, swap(): return lax.ppermute(x, axis, [(i, i ^ offset) for i in range(n)])  20.1 us
    all_to_all x2, blocking collectives, per_device(): lax.all_to_all(mixed, 'col', 0, 0, tiled=True).reshape(levels, ncols)  19.6 us
    pallas_call x5, Pallas kernels, local_call(): pl.pallas_call(kernel, out_shape=tuple((pltpu.VMEM(o.shape, o.dtype) for...  13.3 us
    all_to_all x1, blocking collectives, per_device(): moved = lax.all_to_all(sent, 'col', 0, 0, tiled=True)  9.66 us
    all_to_all x1, waiting for transfers between devices, per_device(): moved = lax.all_to_all(sent, 'col', 0, 0, tiled=True)  7.73 us
    pallas_call x2, Pallas kernels, middle(): pl.pallas_call(horizontal_kernel, out_shape=(pltpu.VMEM((bands, nodes), j...  7.6 us
    sort x1, other arithmetic, per_device(): lax.sort((order, other % ncols, obs_weight, obs_value, obs_precision), nu...  6.66 us
  transfers between devices with their start and end apart: 19, of which 16 were waited for; matrix products, arithmetic and copies ran while one was open for 1% of the time, Pallas kernels for 0%

profile of v7, /device:TPU:0, one launch (start us, length us, event | category | flops | bytes accessed | tf_op | source)
XLA Modules:
  0.0 116.1 jit_solution(10720394036812113959)
XLA Ops:
  0.7 1.1 fusion.28
  1.7 0.9 fusion.9
  2.6 0.3 convert_reduce_fusion.refs_0_.starts_ref
  2.9 6.7 %sort.33 = (s32[8192]{0:T(1024)S(1)}, s32[8192]{0:T(1024)S(1)}, f32[8192]{0:T(1024)S(1)}, f32[8192]{0:T(1024)S(1)}, f32[8192]{0:T(1024)S(1)}) sort(s32[8192]{0:T(1024)S(1)} %get-tuple-element.50, s32[8192]{0:T(1024)S(1)} %get-tuple-element.61, f32[8192]{0:T(1024)} %param.17, f32[8192]{0:T(1024)} %param.18, f32[8192]{0:T(1024)} %param.19), dimensions={0}, to_apply=%region_0.1 | sort | flops 106496 | bytes 327680 | tf_op jit(solution)/shard_map/sort | solution.py:462
  9.8 3.9 %adjoint.2 = (bf16[4,32,2048]{2,1,0:T(8,128)(2,1)}, f32[1,8192]{1,0:T(1,128)S(1)}) custom-call(s32[65]{0:T(128)S(1)} %convert_reduce_fusion.refs_0_.starts_ref, bf16[128,2048]{1,0:T(8,128)(2,1)} %bitcast.74, bf16[128,128]{1,0:T(8,128)(2,1)} %vert_ref.3, f32[4,8192]{1,0:T(4,128)S(1)} %add_convert_fusion.refs_3_.keys_ref, f32[1,8192]{1,0:T(1,128)S(1)} %bitcast.80, ...), custom_call_target="tpu_custom_call" | custom-call | tf_op jit(solution)/shard_map/adjoint/pallas_call | solution.py:386
  13.8 5.2 %all-to-all-start = ((bf16[4,32,2048]{2,1,0:T(8,128)(2,1)}), bf16[4,32,2048]{2,1,0:T(8,128)(2,1)S(1)}, u32[]{:S(2)}, u32[]{:S(2)}) async-start(bf16[4,32,2048]{2,1,0:T(8,128)(2,1)} %get-tuple-element.32), calls=%async_computation | async-start | bytes 1048576 | tf_op jit(solution)/shard_map/all_to_all | solution.py:540
  19.1 0.1 reshape.63.spots_ref
  19.3 7.7 %all-to-all-done.moved_ref = bf16[4,32,2048]{2,1,0:T(8,128)(2,1)S(1)} async-done(((bf16[4,32,2048]{2,1,0:T(8,128)(2,1)}), bf16[4,32,2048]{2,1,0:T(8,128)(2,1)S(1)}, u32[]{:S(2)}, u32[]{:S(2)}) %all-to-all-start) | async-done | bytes 524320 | tf_op jit(solution)/shard_map/all_to_all | solution.py:540
  27.0 3.8 %horizontal.2 = (f32[32,8192]{1,0:T(8,128)S(1)}, bf16[4,32,2048]{2,1,0:T(8,128)(2,1)S(1)}) custom-call(s32[256]{0:T(256)S(1)} %reshape.63.spots_ref, f32[2,128]{1,0:T(2,128)S(1)} %bitcast.100, bf16[4,32,2048]{2,1,0:T(8,128)(2,1)S(1)} %all-to-all-done.moved_ref, bf16[64,128,128]{2,1,0:T(8,128)(2,1)S(1)} %bitcast.72), custom_call_target="tpu_custom_call" | custom-call | tf_op jit(solution)/shard_map/horizontal/pallas_call | solution.py:502
  30.8 10.1 %all_to_all.20 = bf16[4,32,2048]{2,1,0:T(8,128)(2,1)S(1)} all-to-all(bf16[4,32,2048]{2,1,0:T(8,128)(2,1)S(1)} %get-tuple-element.33), channel_id=1, replica_groups=mesh['mem'=8,'col'=4] {'col'}, dimensions={0} | all-to-all | bytes 1048576 | tf_op jit(solution)/shard_map/all_to_all | solution.py:542
  40.9 2.6 %forward.2 = (bf16[4,256,256]{2,1,0:T(8,128)(2,1)S(1)}, f32[1,8192]{1,0:T(1,128)S(1)}) custom-call(s32[65]{0:T(128)S(1)} %convert_reduce_fusion.refs_0_.starts_ref, f32[4,8192]{1,0:T(4,128)S(1)} %add_convert_fusion.refs_3_.keys_ref, f32[1,8192]{1,0:T(1,128)S(1)} %bitcast.81, bf16[128,2048]{1,0:T(8,128)(2,1)S(1)} %bitcast.79, bf16[128,2048]{1,0:T(8,128)(2,1)S(1)} %bitcast.76, ...), custom_call_target="tpu_custom_call" | custom-call | tf_op jit(solution)/shard_map/forward/pallas_call | solution.py:386
  43.6 1.2 %collective-permute-done = f32[64,128]{1,0:T(8,128)S(1)} collective-permute-done((f32[64,128]{1,0:T(8,128)S(1)}, f32[64,128]{1,0:T(8,128)S(1)}, u32[]{:S(2)}, u32[]{:S(2)}) %collective-permute-start) | collective-permute-done | bytes 32800 | tf_op jit(solution)/shard_map/ppermute | solution.py:399
  44.8 1.7 %collective-permute-start.1 = (bf16[64,128]{1,0:T(8,128)(2,1)S(1)}, bf16[64,128]{1,0:T(8,128)(2,1)S(1)}, u32[]{:S(2)}, u32[]{:S(2)}) collective-permute-start(bf16[64,128]{1,0:T(8,128)(2,1)S(1)} %add_convert_fusion.4), channel_id=1, source_target_pairs={{0,8},{4,12},{8,0},{12,4},{16,24},{20,28},{24,16},{28,20},{1,9},{5... | collective-permute-start | bytes 49160 | tf_op jit(solution)/shard_map/ppermute | solution.py:399
  46.4 2.6 %collective-permute-start.2 = (bf16[64,128]{1,0:T(8,128)(2,1)S(1)}, bf16[64,128]{1,0:T(8,128)(2,1)S(1)}, u32[]{:S(2)}, u32[]{:S(2)}) collective-permute-start(bf16[64,128]{1,0:T(8,128)(2,1)S(1)} %add_convert_fusion.4), channel_id=1, source_target_pairs={{0,16},{4,20},{8,24},{12,28},{16,0},{20,4},{24,8},{28,12},{1,17},{... | collective-permute-start | bytes 49160 | tf_op jit(solution)/shard_map/ppermute | solution.py:399
  49.0 0.2 collective-permute-start.3
  49.2 1.9 %collective-permute-done.2 = bf16[64,128]{1,0:T(8,128)(2,1)S(1)} collective-permute-done((bf16[64,128]{1,0:T(8,128)(2,1)S(1)}, bf16[64,128]{1,0:T(8,128)(2,1)S(1)}, u32[]{:S(2)}, u32[]{:S(2)}) %collective-permute-start.2) | collective-permute-done | bytes 16416 | tf_op jit(solution)/shard_map/ppermute | solution.py:399
  51.2 3.4 %collective-permute-done.3 = bf16[64,128]{1,0:T(8,128)(2,1)S(1)} collective-permute-done((bf16[64,128]{1,0:T(8,128)(2,1)S(1)}, bf16[64,128]{1,0:T(8,128)(2,1)S(1)}, u32[]{:S(2)}, u32[]{:S(2)}) %collective-permute-start.3) | collective-permute-done | bytes 16416 | tf_op jit(solution)/shard_map/ppermute | solution.py:399
  54.6 1.0 collective-permute-start.6
  55.5 1.5 %collective-permute-start.5 = (bf16[64,128]{1,0:T(8,128)(2,1)S(1)}, bf16[64,128]{1,0:T(8,128)(2,1)S(1)}, u32[]{:S(2)}, u32[]{:S(2)}) collective-permute-start(bf16[64,128]{1,0:T(8,128)(2,1)S(1)} %add_convert_fusion.3), channel_id=1, source_target_pairs={{0,2},{1,3},{2,0},{3,1},{4,6},{5,7},{6,4},{7,5},{8,10},{9,11},{10,... | collective-permute-start | bytes 49160 | tf_op jit(solution)/shard_map/ppermute | solution.py:399
  57.0 1.1 collective-permute-start.4
  58.2 1.1 collective-permute-done.6
  59.3 0.1 collective-permute-done.5
  59.5 1.3 %collective-permute-done.4 = bf16[64,128]{1,0:T(8,128)(2,1)S(1)} collective-permute-done((bf16[64,128]{1,0:T(8,128)(2,1)S(1)}, bf16[64,128]{1,0:T(8,128)(2,1)S(1)}, u32[]{:S(2)}, u32[]{:S(2)}) %collective-permute-start.4) | collective-permute-done | bytes 16416 | tf_op jit(solution)/shard_map/ppermute | solution.py:399
  60.8 3.4 %adjoint.3 = (bf16[4,32,2048]{2,1,0:T(8,128)(2,1)S(1)}, f32[1,8192]{1,0:T(1,128)S(1)}, f32[1,128]{1,0:T(1,128)S(1)}, f32[1,128]{1,0:T(1,128)S(1)}, f32[1,8192]{1...) custom-call(s32[65]{0:T(128)S(1)} %convert_reduce_fusion.refs_0_.starts_ref, bf16[128,2048]{1,0:T(8,128)(2,1)} %bitcast.75, ...), custom_call_target="tpu_custom_call" | custom-call | tf_op jit(solution)/shard_map/adjoint/pallas_call | solution.py:386
  64.1 9.7 %all_to_all.21.moved_ref = bf16[4,32,2048]{2,1,0:T(8,128)(2,1)S(1)} all-to-all(bf16[4,32,2048]{2,1,0:T(8,128)(2,1)S(1)} %get-tuple-element.39), channel_id=1, replica_groups=mesh['mem'=8,'col'=4] {'col'}, dimensions={0} | all-to-all | bytes 1048576 | tf_op jit(solution)/shard_map/all_to_all | solution.py:540
  73.8 3.8 %horizontal.3 = (f32[32,8192]{1,0:T(8,128)S(1)}, bf16[4,32,2048]{2,1,0:T(8,128)(2,1)S(1)}) custom-call(s32[256]{0:T(256)S(1)} %reshape.63.spots_ref, f32[2,128]{1,0:T(2,128)S(1)} %bitcast.101, bf16[4,32,2048]{2,1,0:T(8,128)(2,1)S(1)} %all_to_all.21.moved_ref, bf16[64,128,128]{2,1,0:T(8,128)(2,1)S(1)} %bitcast.73), custom_call_target="tpu_custom_call" | custom-call | tf_op jit(solution)/shard_map/horizontal/pallas_call | solution.py:502
  77.6 9.5 %all_to_all.22 = bf16[4,32,2048]{2,1,0:T(8,128)(2,1)S(1)} all-to-all(bf16[4,32,2048]{2,1,0:T(8,128)(2,1)S(1)} %get-tuple-element.40), channel_id=1, replica_groups=mesh['mem'=8,'col'=4] {'col'}, dimensions={0} | all-to-all | bytes 1048576 | tf_op jit(solution)/shard_map/all_to_all | solution.py:542
  87.1 2.6 %forward.3 = (bf16[4,256,256]{2,1,0:T(8,128)(2,1)S(1)}, f32[1,8192]{1,0:T(1,128)S(1)}) custom-call(s32[65]{0:T(128)S(1)} %convert_reduce_fusion.refs_0_.starts_ref, f32[4,8192]{1,0:T(4,128)S(1)} %add_convert_fusion.refs_3_.keys_ref, f32[1,8192]{1,0:T(1,128)S(1)} %bitcast.83, bf16[128,2048]{1,0:T(8,128)(2,1)S(1)} %bitcast.78, bf16[128,2048]{1,0:T(8,128)(2,1)S(1)} %bitcast.77, ...), custom_call_target="tpu_custom_call" | custom-call | tf_op jit(solution)/shard_map/forward/pallas_call | solution.py:386
  89.8 1.2 %collective-permute-done.7 = f32[64,128]{1,0:T(8,128)S(1)} collective-permute-done((f32[64,128]{1,0:T(8,128)S(1)}, f32[64,128]{1,0:T(8,128)S(1)}, u32[]{:S(2)}, u32[]{:S(2)}) %collective-permute-start.7) | collective-permute-done | bytes 32800 | tf_op jit(solution)/shard_map/ppermute | solution.py:399
  91.0 0.3 collective-permute-start.10
  91.3 4.2 %collective-permute-start.9 = (bf16[64,128]{1,0:T(8,128)(2,1)S(1)}, bf16[64,128]{1,0:T(8,128)(2,1)S(1)}, u32[]{:S(2)}, u32[]{:S(2)}) collective-permute-start(bf16[64,128]{1,0:T(8,128)(2,1)S(1)} %add_convert_fusion.2), channel_id=1, source_target_pairs={{0,16},{4,20},{8,24},{12,28},{16,0},{20,4},{24,8},{28,12},{1,17},{... | collective-permute-start | bytes 49160 | tf_op jit(solution)/shard_map/ppermute | solution.py:399
  95.5 1.1 collective-permute-done.10
  96.6 0.6 collective-permute-done.9
  97.2 1.0 collective-permute-start.13
  98.2 1.5 %collective-permute-start.12 = (bf16[64,128]{1,0:T(8,128)(2,1)S(1)}, bf16[64,128]{1,0:T(8,128)(2,1)S(1)}, u32[]{:S(2)}, u32[]{:S(2)}) collective-permute-start(bf16[64,128]{1,0:T(8,128)(2,1)S(1)} %add_convert_fusion.1), channel_id=1, source_target_pairs={{0,2},{1,3},{2,0},{3,1},{4,6},{5,7},{6,4},{7,5},{8,10},{9,11},{10,... | collective-permute-start | bytes 49160 | tf_op jit(solution)/shard_map/ppermute | solution.py:399
  99.6 1.1 collective-permute-start.11
  100.8 1.1 collective-permute-done.13
  101.9 0.1 collective-permute-done.12
  102.1 1.3 %collective-permute-done.11 = bf16[64,128]{1,0:T(8,128)(2,1)S(1)} collective-permute-done((bf16[64,128]{1,0:T(8,128)(2,1)S(1)}, bf16[64,128]{1,0:T(8,128)(2,1)S(1)}, u32[]{:S(2)}, u32[]{:S(2)}) %collective-permute-start.11) | collective-permute-done | bytes 16416 | tf_op jit(solution)/shard_map/ppermute | solution.py:399
  103.4 0.9 finish.1
  104.5 1.5 %collective-permute-done.14 = bf16[4,16,2048]{2,1,0:T(8,128)(2,1)S(1)} collective-permute-done((bf16[4,16,2048]{2,1,0:T(8,128)(2,1)S(1)}, bf16[4,16,2048]{2,1,0:T(8,128)(2,1)S(1)}, u32[]{:S(2)}, u32[]{:S(2)}) %collective-permute-start.14) | collective-permute-done | bytes 262176 | tf_op jit(solution)/shard_map/ppermute | solution.py:399
  106.1 0.8 collective-permute-start.15
  106.9 2.3 %collective-permute-start.16 = (bf16[16,2048]{1,0:T(8,128)(2,1)S(1)}, bf16[16,2048]{1,0:T(8,128)(2,1)S(1)}, u32[]{:S(2)}, u32[]{:S(2)}) collective-permute-start(bf16[16,2048]{1,0:T(8,128)(2,1)S(1)} %get-tuple-element.54), channel_id=1, source_target_pairs={{0,16},{4,20},{8,24},{12,28},{16,0},{20,4},{24,8},{28,12},{1,17},{... | collective-permute-start | bytes 196616 | tf_op jit(solution)/shard_map/ppermute | solution.py:399
  109.2 1.3 %collective-permute-start.17 = (bf16[16,2048]{1,0:T(8,128)(2,1)S(1)}, bf16[16,2048]{1,0:T(8,128)(2,1)S(1)}, u32[]{:S(2)}, u32[]{:S(2)}) collective-permute-start(bf16[16,2048]{1,0:T(8,128)(2,1)S(1)} %get-tuple-element.53), channel_id=1, source_target_pairs={{0,24},{4,28},{8,16},{12,20},{16,8},{20,12},{24,0},{28,4},{1,25},{... | collective-permute-start | bytes 196616 | tf_op jit(solution)/shard_map/ppermute | solution.py:399
  110.5 0.8 copy.38
  111.3 1.0 collective-permute-done.16
  112.3 3.1 %collective-permute-done.17 = bf16[16,2048]{1,0:T(8,128)(2,1)S(1)} collective-permute-done((bf16[16,2048]{1,0:T(8,128)(2,1)S(1)}, bf16[16,2048]{1,0:T(8,128)(2,1)S(1)}, u32[]{:S(2)}, u32[]{:S(2)}) %collective-permute-start.17) | collective-permute-done | bytes 65568 | tf_op jit(solution)/shard_map/ppermute | solution.py:399
  115.4 0.7 fusion.2
  (40 shorter events, 1.0 us)
Async XLA Ops:
  0.6 18.3 %copy-start.6 = (s32[128,2]{0,1:T(2,128)S(1)}, s32[128,2]{0,1:T(2,128)}, u32[]{:S(2)}) copy-start(s32[128,2]{0,1:T(2,128)} %param.14) | copy-start | bytes 3076
  0.6 26.4 %copy-start.5 = (f32[128,2]{0,1:T(2,128)S(1)}, f32[128,2]{0,1:T(2,128)}, u32[]{:S(2)}) copy-start(f32[128,2]{0,1:T(2,128)} %param.13) | copy-start | bytes 3076
  0.7 26.3 %copy-start = (bf16[128,64,128]{2,1,0:T(8,128)(2,1)S(1)}, bf16[128,64,128]{2,1,0:T(8,128)(2,1)}, u32[]{:S(2)}) copy-start(bf16[128,64,128]{2,1,0:T(8,128)(2,1)} %param.12) | copy-start | bytes 6291460
  13.8 13.2 %all-to-all-start = ((bf16[4,32,2048]{2,1,0:T(8,128)(2,1)}), bf16[4,32,2048]{2,1,0:T(8,128)(2,1)S(1)}, u32[]{:S(2)}, u32[]{:S(2)}) async-start(bf16[4,32,2048]{2,1,0:T(8,128)(2,1)} %get-tuple-element.32), calls=%async_computation | async-start | bytes 1048576 | tf_op jit(solution)/shard_map/all_to_all | solution.py:540
  19.0 21.9 %copy-start.1 = (bf16[1,128,2048]{2,1,0:T(8,128)(2,1)S(1)}, bf16[1,128,2048]{2,1,0:T(8,128)(2,1)}, u32[]{:S(2)}) copy-start(bf16[1,128,2048]{2,1,0:T(8,128)(2,1)} %param.10) | copy-start | bytes 1572868
  19.0 21.9 %copy-start.3 = (bf16[128,128]{1,0:T(8,128)(2,1)S(1)}, bf16[128,128]{1,0:T(8,128)(2,1)}, u32[]{:S(2)}) copy-start(bf16[128,128]{1,0:T(8,128)(2,1)} %vert_ref.3) | copy-start | bytes 98308
  43.5 1.3 %collective-permute-start = (f32[64,128]{1,0:T(8,128)S(1)}, f32[64,128]{1,0:T(8,128)S(1)}, u32[]{:S(2)}, u32[]{:S(2)}) collective-permute-start(f32[64,128]{1,0:T(8,128)S(1)} %bitcast.97), channel_id=1, source_target_pairs={{0,4},{4,0},{8,12},{12,8},{16,20},{20,16},{24,28},{28,24},{1,5},{5... | collective-permute-start | bytes 98312 | tf_op jit(solution)/shard_map/ppermute | solution.py:399
  44.8 4.5 %collective-permute-start.1 = (bf16[64,128]{1,0:T(8,128)(2,1)S(1)}, bf16[64,128]{1,0:T(8,128)(2,1)S(1)}, u32[]{:S(2)}, u32[]{:S(2)}) collective-permute-start(bf16[64,128]{1,0:T(8,128)(2,1)S(1)} %add_convert_fusion.4), channel_id=1, source_target_pairs={{0,8},{4,12},{8,0},{12,4},{16,24},{20,28},{24,16},{28,20},{1,9},{5... | collective-permute-start | bytes 49160 | tf_op jit(solution)/shard_map/ppermute | solution.py:399
  46.4 4.7 %collective-permute-start.2 = (bf16[64,128]{1,0:T(8,128)(2,1)S(1)}, bf16[64,128]{1,0:T(8,128)(2,1)S(1)}, u32[]{:S(2)}, u32[]{:S(2)}) collective-permute-start(bf16[64,128]{1,0:T(8,128)(2,1)S(1)} %add_convert_fusion.4), channel_id=1, source_target_pairs={{0,16},{4,20},{8,24},{12,28},{16,0},{20,4},{24,8},{28,12},{1,17},{... | collective-permute-start | bytes 49160 | tf_op jit(solution)/shard_map/ppermute | solution.py:399
  49.0 5.5 %collective-permute-start.3 = (bf16[64,128]{1,0:T(8,128)(2,1)S(1)}, bf16[64,128]{1,0:T(8,128)(2,1)S(1)}, u32[]{:S(2)}, u32[]{:S(2)}) collective-permute-start(bf16[64,128]{1,0:T(8,128)(2,1)S(1)} %add_convert_fusion.4), channel_id=1, source_target_pairs={{0,24},{4,28},{8,16},{12,20},{16,8},{20,12},{24,0},{28,4},{1,25},{... | collective-permute-start | bytes 49160 | tf_op jit(solution)/shard_map/ppermute | solution.py:399
  54.6 4.7 %collective-permute-start.6 = (bf16[64,128]{1,0:T(8,128)(2,1)S(1)}, bf16[64,128]{1,0:T(8,128)(2,1)S(1)}, u32[]{:S(2)}, u32[]{:S(2)}) collective-permute-start(bf16[64,128]{1,0:T(8,128)(2,1)S(1)} %add_convert_fusion.3), channel_id=1, source_target_pairs={{0,3},{1,2},{2,1},{3,0},{4,7},{5,6},{6,5},{7,4},{8,11},{9,10},{10,... | collective-permute-start | bytes 49160 | tf_op jit(solution)/shard_map/ppermute | solution.py:399
  55.5 3.9 %collective-permute-start.5 = (bf16[64,128]{1,0:T(8,128)(2,1)S(1)}, bf16[64,128]{1,0:T(8,128)(2,1)S(1)}, u32[]{:S(2)}, u32[]{:S(2)}) collective-permute-start(bf16[64,128]{1,0:T(8,128)(2,1)S(1)} %add_convert_fusion.3), channel_id=1, source_target_pairs={{0,2},{1,3},{2,0},{3,1},{4,6},{5,7},{6,4},{7,5},{8,10},{9,11},{10,... | collective-permute-start | bytes 49160 | tf_op jit(solution)/shard_map/ppermute | solution.py:399
  57.0 3.7 %collective-permute-start.4 = (bf16[64,128]{1,0:T(8,128)(2,1)S(1)}, bf16[64,128]{1,0:T(8,128)(2,1)S(1)}, u32[]{:S(2)}, u32[]{:S(2)}) collective-permute-start(bf16[64,128]{1,0:T(8,128)(2,1)S(1)} %add_convert_fusion.3), channel_id=1, source_target_pairs={{0,1},{1,0},{2,3},{3,2},{4,5},{5,4},{6,7},{7,6},{8,9},{9,8},{10,11... | collective-permute-start | bytes 49160 | tf_op jit(solution)/shard_map/ppermute | solution.py:399
  73.8 13.3 %copy-start.2 = (bf16[1,128,2048]{2,1,0:T(8,128)(2,1)S(1)}, bf16[1,128,2048]{2,1,0:T(8,128)(2,1)}, u32[]{:S(2)}) copy-start(bf16[1,128,2048]{2,1,0:T(8,128)(2,1)} %param.10) | copy-start | bytes 1572868
  73.8 13.3 %copy-start.4 = (bf16[128,128]{1,0:T(8,128)(2,1)S(1)}, bf16[128,128]{1,0:T(8,128)(2,1)}, u32[]{:S(2)}) copy-start(bf16[128,128]{1,0:T(8,128)(2,1)} %vert_ref.3) | copy-start | bytes 98308
  89.7 1.3 %collective-permute-start.7 = (f32[64,128]{1,0:T(8,128)S(1)}, f32[64,128]{1,0:T(8,128)S(1)}, u32[]{:S(2)}, u32[]{:S(2)}) collective-permute-start(f32[64,128]{1,0:T(8,128)S(1)} %bitcast.95), channel_id=1, source_target_pairs={{0,4},{4,0},{8,12},{12,8},{16,20},{20,16},{24,28},{28,24},{1,5},{5... | collective-permute-start | bytes 98312 | tf_op jit(solution)/shard_map/ppermute | solution.py:399
  91.0 5.6 %collective-permute-start.10 = (bf16[64,128]{1,0:T(8,128)(2,1)S(1)}, bf16[64,128]{1,0:T(8,128)(2,1)S(1)}, u32[]{:S(2)}, u32[]{:S(2)}) collective-permute-start(bf16[64,128]{1,0:T(8,128)(2,1)S(1)} %add_convert_fusion.2), channel_id=1, source_target_pairs={{0,24},{4,28},{8,16},{12,20},{16,8},{20,12},{24,0},{28,4},{1,25},{... | collective-permute-start | bytes 49160 | tf_op jit(solution)/shard_map/ppermute | solution.py:399
  91.3 5.3 %collective-permute-start.8 = (bf16[64,128]{1,0:T(8,128)(2,1)S(1)}, bf16[64,128]{1,0:T(8,128)(2,1)S(1)}, u32[]{:S(2)}, u32[]{:S(2)}) collective-permute-start(bf16[64,128]{1,0:T(8,128)(2,1)S(1)} %add_convert_fusion.2), channel_id=1, source_target_pairs={{0,8},{4,12},{8,0},{12,4},{16,24},{20,28},{24,16},{28,20},{1,9},{5... | collective-permute-start | bytes 49160 | tf_op jit(solution)/shard_map/ppermute | solution.py:399
  91.3 5.9 %collective-permute-start.9 = (bf16[64,128]{1,0:T(8,128)(2,1)S(1)}, bf16[64,128]{1,0:T(8,128)(2,1)S(1)}, u32[]{:S(2)}, u32[]{:S(2)}) collective-permute-start(bf16[64,128]{1,0:T(8,128)(2,1)S(1)} %add_convert_fusion.2), channel_id=1, source_target_pairs={{0,16},{4,20},{8,24},{12,28},{16,0},{20,4},{24,8},{28,12},{1,17},{... | collective-permute-start | bytes 49160 | tf_op jit(solution)/shard_map/ppermute | solution.py:399
  97.2 4.7 %collective-permute-start.13 = (bf16[64,128]{1,0:T(8,128)(2,1)S(1)}, bf16[64,128]{1,0:T(8,128)(2,1)S(1)}, u32[]{:S(2)}, u32[]{:S(2)}) collective-permute-start(bf16[64,128]{1,0:T(8,128)(2,1)S(1)} %add_convert_fusion.1), channel_id=1, source_target_pairs={{0,3},{1,2},{2,1},{3,0},{4,7},{5,6},{6,5},{7,4},{8,11},{9,10},{10,... | collective-permute-start | bytes 49160 | tf_op jit(solution)/shard_map/ppermute | solution.py:399
  98.2 3.9 %collective-permute-start.12 = (bf16[64,128]{1,0:T(8,128)(2,1)S(1)}, bf16[64,128]{1,0:T(8,128)(2,1)S(1)}, u32[]{:S(2)}, u32[]{:S(2)}) collective-permute-start(bf16[64,128]{1,0:T(8,128)(2,1)S(1)} %add_convert_fusion.1), channel_id=1, source_target_pairs={{0,2},{1,3},{2,0},{3,1},{4,6},{5,7},{6,4},{7,5},{8,10},{9,11},{10,... | collective-permute-start | bytes 49160 | tf_op jit(solution)/shard_map/ppermute | solution.py:399
  99.6 3.7 %collective-permute-start.11 = (bf16[64,128]{1,0:T(8,128)(2,1)S(1)}, bf16[64,128]{1,0:T(8,128)(2,1)S(1)}, u32[]{:S(2)}, u32[]{:S(2)}) collective-permute-start(bf16[64,128]{1,0:T(8,128)(2,1)S(1)} %add_convert_fusion.1), channel_id=1, source_target_pairs={{0,1},{1,0},{2,3},{3,2},{4,5},{5,4},{6,7},{7,6},{8,9},{9,8},{10,11... | collective-permute-start | bytes 49160 | tf_op jit(solution)/shard_map/ppermute | solution.py:399
  104.4 1.6 %collective-permute-start.14 = (bf16[4,16,2048]{2,1,0:T(8,128)(2,1)S(1)}, bf16[4,16,2048]{2,1,0:T(8,128)(2,1)S(1)}, u32[]{:S(2)}, u32[]{:S(2)}) collective-permute-start(bf16[4,16,2048]{2,1,0:T(8,128)(2,1)S(1)} %slice_bitcast_fusion), channel_id=1, source_target_pairs={{0,4},{4,0},{8,12},{12,8},{16,20},{20,16},{24,28},{28,24},{1,5},{5... | collective-permute-start | bytes 786440 | tf_op jit(solution)/shard_map/ppermute | solution.py:399
  106.1 5.2 %collective-permute-start.15 = (bf16[16,2048]{1,0:T(8,128)(2,1)S(1)}, bf16[16,2048]{1,0:T(8,128)(2,1)S(1)}, u32[]{:S(2)}, u32[]{:S(2)}) collective-permute-start(bf16[16,2048]{1,0:T(8,128)(2,1)S(1)} %get-tuple-element.52), channel_id=1, source_target_pairs={{0,8},{4,12},{8,0},{12,4},{16,24},{20,28},{24,16},{28,20},{1,9},{5... | collective-permute-start | bytes 196616 | tf_op jit(solution)/shard_map/ppermute | solution.py:399
  106.9 5.4 %collective-permute-start.16 = (bf16[16,2048]{1,0:T(8,128)(2,1)S(1)}, bf16[16,2048]{1,0:T(8,128)(2,1)S(1)}, u32[]{:S(2)}, u32[]{:S(2)}) collective-permute-start(bf16[16,2048]{1,0:T(8,128)(2,1)S(1)} %get-tuple-element.54), channel_id=1, source_target_pairs={{0,16},{4,20},{8,24},{12,28},{16,0},{20,4},{24,8},{28,12},{1,17},{... | collective-permute-start | bytes 196616 | tf_op jit(solution)/shard_map/ppermute | solution.py:399
  109.2 6.2 %collective-permute-start.17 = (bf16[16,2048]{1,0:T(8,128)(2,1)S(1)}, bf16[16,2048]{1,0:T(8,128)(2,1)S(1)}, u32[]{:S(2)}, u32[]{:S(2)}) collective-permute-start(bf16[16,2048]{1,0:T(8,128)(2,1)S(1)} %get-tuple-element.53), channel_id=1, source_target_pairs={{0,24},{4,28},{8,16},{12,20},{16,8},{20,12},{24,0},{28,4},{1,25},{... | collective-permute-start | bytes 196616 | tf_op jit(solution)/shard_map/ppermute | solution.py:399

commit v8 on v7

--- a/solution.py
+++ b/solution.py
@@ -407,8 +407,9 @@
     shape = x.shape
     x = x.reshape(-1, LANES)
     x = total_over(x, "mem", (1,)).astype(jnp.bfloat16)
-    x = total_over(x, "mem", range(2, lax.axis_size("mem"), 2)).astype(jnp.bfloat16)
-    return [y.reshape(shape) for y in [x] + [swap(x, "col", k) for k in range(1, lax.axis_size("col"))]]
+    x = total_over(x, "col", range(1, lax.axis_size("col"))).astype(jnp.bfloat16)
+    ring = range(2, lax.axis_size("mem"), 2)
+    return [y.reshape(shape) for y in [x] + [swap(x, "mem", k) for k in ring]]
 
 
 def scatter_members(field):

time: 117 us -> 116 us (level)
  transfers between devices with their start and end apart: 19 -> 19, of which waited for: 16 -> 15; matrix products, arithmetic and copies ran while one was open for 1% -> 1% of each run, Pallas kernels for 0% -> 0%
where the time goes in v8:
time: 116 us
  blocking collectives  29.8 us (26%)
  waiting for transfers between devices  27.1 us (23%)
  starting transfers between devices  25.9 us (22%)
  Pallas kernels  20.9 us (18%)
  other arithmetic  8.88 us (8%)
  local copies, waits for them, and re-layouts  2.41 us (2%)
    ppermute x18, starting transfers between devices, swap(): return lax.ppermute(x, axis, [(i, i ^ offset) for i in range(n)])  20.7 us
    all_to_all x2, blocking collectives, per_device(): lax.all_to_all(mixed, 'col', 0, 0, tiled=True).reshape(levels, ncols)  19.6 us
    ppermute x18, waiting for transfers between devices, swap(): return lax.ppermute(x, axis, [(i, i ^ offset) for i in range(n)])  19.4 us
    pallas_call x5, Pallas kernels, local_call(): pl.pallas_call(kernel, out_shape=tuple((pltpu.VMEM(o.shape, o.dtype) for...  13.3 us
    all_to_all x1, blocking collectives, per_device(): moved = lax.all_to_all(sent, 'col', 0, 0, tiled=True)  10.2 us
    all_to_all x1, waiting for transfers between devices, per_device(): moved = lax.all_to_all(sent, 'col', 0, 0, tiled=True)  7.73 us
    pallas_call x2, Pallas kernels, middle(): pl.pallas_call(horizontal_kernel, out_shape=(pltpu.VMEM((bands, nodes), j...  7.6 us
    sort x1, other arithmetic, per_device(): lax.sort((order, other % ncols, obs_weight, obs_value, obs_precision), nu...  6.66 us
  transfers between devices with their start and end apart: 19, of which 15 were waited for; matrix products, arithmetic and copies ran while one was open for 1% of the time, Pallas kernels for 0%

profile of v8, /device:TPU:0, one launch (start us, length us, event | category | flops | bytes accessed | tf_op | source)
XLA Modules:
  0.0 116.0 jit_solution(4390912670450631804)
XLA Ops:
  0.7 1.1 fusion.28
  1.7 0.9 fusion.9
  2.6 0.3 convert_reduce_fusion.refs_0_.starts_ref
  2.9 6.7 %sort.33 = (s32[8192]{0:T(1024)S(1)}, s32[8192]{0:T(1024)S(1)}, f32[8192]{0:T(1024)S(1)}, f32[8192]{0:T(1024)S(1)}, f32[8192]{0:T(1024)S(1)}) sort(s32[8192]{0:T(1024)S(1)} %get-tuple-element.50, s32[8192]{0:T(1024)S(1)} %get-tuple-element.61, f32[8192]{0:T(1024)} %param.17, f32[8192]{0:T(1024)} %param.18, f32[8192]{0:T(1024)} %param.19), dimensions={0}, to_apply=%region_0.1 | sort | flops 106496 | bytes 327680 | tf_op jit(solution)/shard_map/sort | solution.py:463
  9.7 0.1 add_convert_fusion.refs_3_.keys_ref
  9.8 3.9 %adjoint.2 = (bf16[4,32,2048]{2,1,0:T(8,128)(2,1)}, f32[1,8192]{1,0:T(1,128)S(1)}) custom-call(s32[65]{0:T(128)S(1)} %convert_reduce_fusion.refs_0_.starts_ref, bf16[128,2048]{1,0:T(8,128)(2,1)} %bitcast.74, bf16[128,128]{1,0:T(8,128)(2,1)} %vert_ref.3, f32[4,8192]{1,0:T(4,128)S(1)} %add_convert_fusion.refs_3_.keys_ref, f32[1,8192]{1,0:T(1,128)S(1)} %bitcast.80, ...), custom_call_target="tpu_custom_call" | custom-call | tf_op jit(solution)/shard_map/adjoint/pallas_call | solution.py:386
  13.8 5.2 %all-to-all-start = ((bf16[4,32,2048]{2,1,0:T(8,128)(2,1)}), bf16[4,32,2048]{2,1,0:T(8,128)(2,1)S(1)}, u32[]{:S(2)}, u32[]{:S(2)}) async-start(bf16[4,32,2048]{2,1,0:T(8,128)(2,1)} %get-tuple-element.32), calls=%async_computation | async-start | bytes 1048576 | tf_op jit(solution)/shard_map/all_to_all | solution.py:541
  19.1 0.1 reshape.63.spots_ref
  19.3 7.7 %all-to-all-done.moved_ref = bf16[4,32,2048]{2,1,0:T(8,128)(2,1)S(1)} async-done(((bf16[4,32,2048]{2,1,0:T(8,128)(2,1)}), bf16[4,32,2048]{2,1,0:T(8,128)(2,1)S(1)}, u32[]{:S(2)}, u32[]{:S(2)}) %all-to-all-start) | async-done | bytes 524320 | tf_op jit(solution)/shard_map/all_to_all | solution.py:541
  27.0 3.8 %horizontal.2 = (f32[32,8192]{1,0:T(8,128)S(1)}, bf16[4,32,2048]{2,1,0:T(8,128)(2,1)S(1)}) custom-call(s32[256]{0:T(256)S(1)} %reshape.63.spots_ref, f32[2,128]{1,0:T(2,128)S(1)} %bitcast.100, bf16[4,32,2048]{2,1,0:T(8,128)(2,1)S(1)} %all-to-all-done.moved_ref, bf16[64,128,128]{2,1,0:T(8,128)(2,1)S(1)} %bitcast.72), custom_call_target="tpu_custom_call" | custom-call | tf_op jit(solution)/shard_map/horizontal/pallas_call | solution.py:503
  30.8 10.1 %all_to_all.20 = bf16[4,32,2048]{2,1,0:T(8,128)(2,1)S(1)} all-to-all(bf16[4,32,2048]{2,1,0:T(8,128)(2,1)S(1)} %get-tuple-element.33), channel_id=1, replica_groups=mesh['mem'=8,'col'=4] {'col'}, dimensions={0} | all-to-all | bytes 1048576 | tf_op jit(solution)/shard_map/all_to_all | solution.py:543
  40.9 2.6 %forward.2 = (bf16[4,256,256]{2,1,0:T(8,128)(2,1)S(1)}, f32[1,8192]{1,0:T(1,128)S(1)}) custom-call(s32[65]{0:T(128)S(1)} %convert_reduce_fusion.refs_0_.starts_ref, f32[4,8192]{1,0:T(4,128)S(1)} %add_convert_fusion.refs_3_.keys_ref, f32[1,8192]{1,0:T(1,128)S(1)} %bitcast.81, bf16[128,2048]{1,0:T(8,128)(2,1)S(1)} %bitcast.79, bf16[128,2048]{1,0:T(8,128)(2,1)S(1)} %bitcast.76, ...), custom_call_target="tpu_custom_call" | custom-call | tf_op jit(solution)/shard_map/forward/pallas_call | solution.py:386
  43.6 1.2 %collective-permute-done = f32[64,128]{1,0:T(8,128)S(1)} collective-permute-done((f32[64,128]{1,0:T(8,128)S(1)}, f32[64,128]{1,0:T(8,128)S(1)}, u32[]{:S(2)}, u32[]{:S(2)}) %collective-permute-start) | collective-permute-done | bytes 32800 | tf_op jit(solution)/shard_map/ppermute | solution.py:399
  44.8 1.0 collective-permute-start.1
  45.7 0.6 collective-permute-start.2
  46.3 2.0 %collective-permute-start.3 = (bf16[64,128]{1,0:T(8,128)(2,1)S(1)}, bf16[64,128]{1,0:T(8,128)(2,1)S(1)}, u32[]{:S(2)}, u32[]{:S(2)}) collective-permute-start(bf16[64,128]{1,0:T(8,128)(2,1)S(1)} %add_convert_fusion.4), channel_id=1, source_target_pairs={{0,3},{1,2},{2,1},{3,0},{4,7},{5,6},{6,5},{7,4},{8,11},{9,10},{10,... | collective-permute-start | bytes 49160 | tf_op jit(solution)/shard_map/ppermute | solution.py:399
  48.3 0.2 collective-permute-done.1
  48.6 1.1 collective-permute-done.2
  49.7 1.3 %collective-permute-done.3 = bf16[64,128]{1,0:T(8,128)(2,1)S(1)} collective-permute-done((bf16[64,128]{1,0:T(8,128)(2,1)S(1)}, bf16[64,128]{1,0:T(8,128)(2,1)S(1)}, u32[]{:S(2)}, u32[]{:S(2)}) %collective-permute-start.3) | collective-permute-done | bytes 16416 | tf_op jit(solution)/shard_map/ppermute | solution.py:399
  51.0 3.7 %collective-permute-start.6 = (bf16[64,128]{1,0:T(8,128)(2,1)S(1)}, bf16[64,128]{1,0:T(8,128)(2,1)S(1)}, u32[]{:S(2)}, u32[]{:S(2)}) collective-permute-start(bf16[64,128]{1,0:T(8,128)(2,1)S(1)} %add_convert_fusion.3), channel_id=1, source_target_pairs={{0,24},{4,28},{8,16},{12,20},{16,8},{20,12},{24,0},{28,4},{1,25},{... | collective-permute-start | bytes 49160 | tf_op jit(solution)/shard_map/ppermute | solution.py:399
  54.7 0.8 collective-permute-start.4
  55.4 1.2 %collective-permute-done.6 = bf16[64,128]{1,0:T(8,128)(2,1)S(1)} collective-permute-done((bf16[64,128]{1,0:T(8,128)(2,1)S(1)}, bf16[64,128]{1,0:T(8,128)(2,1)S(1)}, u32[]{:S(2)}, u32[]{:S(2)}) %collective-permute-start.6) | collective-permute-done | bytes 16416 | tf_op jit(solution)/shard_map/ppermute | solution.py:399
  56.7 2.6 %collective-permute-done.5 = bf16[64,128]{1,0:T(8,128)(2,1)S(1)} collective-permute-done((bf16[64,128]{1,0:T(8,128)(2,1)S(1)}, bf16[64,128]{1,0:T(8,128)(2,1)S(1)}, u32[]{:S(2)}, u32[]{:S(2)}) %collective-permute-start.5) | collective-permute-done | bytes 16416 | tf_op jit(solution)/shard_map/ppermute | solution.py:399
  59.4 3.4 %adjoint.3 = (bf16[4,32,2048]{2,1,0:T(8,128)(2,1)S(1)}, f32[1,8192]{1,0:T(1,128)S(1)}, f32[1,128]{1,0:T(1,128)S(1)}, f32[1,128]{1,0:T(1,128)S(1)}, f32[1,8192]{1...) custom-call(s32[65]{0:T(128)S(1)} %convert_reduce_fusion.refs_0_.starts_ref, bf16[128,2048]{1,0:T(8,128)(2,1)} %bitcast.75, ...), custom_call_target="tpu_custom_call" | custom-call | tf_op jit(solution)/shard_map/adjoint/pallas_call | solution.py:386
  62.7 10.2 %all_to_all.21.moved_ref = bf16[4,32,2048]{2,1,0:T(8,128)(2,1)S(1)} all-to-all(bf16[4,32,2048]{2,1,0:T(8,128)(2,1)S(1)} %get-tuple-element.39), channel_id=1, replica_groups=mesh['mem'=8,'col'=4] {'col'}, dimensions={0} | all-to-all | bytes 1048576 | tf_op jit(solution)/shard_map/all_to_all | solution.py:541
  72.9 3.8 %horizontal.3 = (f32[32,8192]{1,0:T(8,128)S(1)}, bf16[4,32,2048]{2,1,0:T(8,128)(2,1)S(1)}) custom-call(s32[256]{0:T(256)S(1)} %reshape.63.spots_ref, f32[2,128]{1,0:T(2,128)S(1)} %bitcast.101, bf16[4,32,2048]{2,1,0:T(8,128)(2,1)S(1)} %all_to_all.21.moved_ref, bf16[64,128,128]{2,1,0:T(8,128)(2,1)S(1)} %bitcast.73), custom_call_target="tpu_custom_call" | custom-call | tf_op jit(solution)/shard_map/horizontal/pallas_call | solution.py:503
  76.7 9.5 %all_to_all.22 = bf16[4,32,2048]{2,1,0:T(8,128)(2,1)S(1)} all-to-all(bf16[4,32,2048]{2,1,0:T(8,128)(2,1)S(1)} %get-tuple-element.40), channel_id=1, replica_groups=mesh['mem'=8,'col'=4] {'col'}, dimensions={0} | all-to-all | bytes 1048576 | tf_op jit(solution)/shard_map/all_to_all | solution.py:543
  86.3 2.6 %forward.3 = (bf16[4,256,256]{2,1,0:T(8,128)(2,1)S(1)}, f32[1,8192]{1,0:T(1,128)S(1)}) custom-call(s32[65]{0:T(128)S(1)} %convert_reduce_fusion.refs_0_.starts_ref, f32[4,8192]{1,0:T(4,128)S(1)} %add_convert_fusion.refs_3_.keys_ref, f32[1,8192]{1,0:T(1,128)S(1)} %bitcast.83, bf16[128,2048]{1,0:T(8,128)(2,1)S(1)} %bitcast.78, bf16[128,2048]{1,0:T(8,128)(2,1)S(1)} %bitcast.77, ...), custom_call_target="tpu_custom_call" | custom-call | tf_op jit(solution)/shard_map/forward/pallas_call | solution.py:386
  88.9 1.2 %collective-permute-done.7 = f32[64,128]{1,0:T(8,128)S(1)} collective-permute-done((f32[64,128]{1,0:T(8,128)S(1)}, f32[64,128]{1,0:T(8,128)S(1)}, u32[]{:S(2)}, u32[]{:S(2)}) %collective-permute-start.7) | collective-permute-done | bytes 32800 | tf_op jit(solution)/shard_map/ppermute | solution.py:399
  90.1 1.0 collective-permute-start.10
  91.1 1.5 %collective-permute-start.8 = (bf16[64,128]{1,0:T(8,128)(2,1)S(1)}, bf16[64,128]{1,0:T(8,128)(2,1)S(1)}, u32[]{:S(2)}, u32[]{:S(2)}) collective-permute-start(bf16[64,128]{1,0:T(8,128)(2,1)S(1)} %add_convert_fusion.2), channel_id=1, source_target_pairs={{0,1},{1,0},{2,3},{3,2},{4,5},{5,4},{6,7},{7,6},{8,9},{9,8},{10,11... | collective-permute-start | bytes 49160 | tf_op jit(solution)/shard_map/ppermute | solution.py:399
  92.6 1.1 collective-permute-start.9
  93.7 1.2 collective-permute-done.10
  94.9 1.5 %collective-permute-done.9 = bf16[64,128]{1,0:T(8,128)(2,1)S(1)} collective-permute-done((bf16[64,128]{1,0:T(8,128)(2,1)S(1)}, bf16[64,128]{1,0:T(8,128)(2,1)S(1)}, u32[]{:S(2)}, u32[]{:S(2)}) %collective-permute-start.9) | collective-permute-done | bytes 16416 | tf_op jit(solution)/shard_map/ppermute | solution.py:399
  96.3 1.5 %collective-permute-start.13 = (bf16[64,128]{1,0:T(8,128)(2,1)S(1)}, bf16[64,128]{1,0:T(8,128)(2,1)S(1)}, u32[]{:S(2)}, u32[]{:S(2)}) collective-permute-start(bf16[64,128]{1,0:T(8,128)(2,1)S(1)} %add_convert_fusion.1), channel_id=1, source_target_pairs={{0,24},{4,28},{8,16},{12,20},{16,8},{20,12},{24,0},{28,4},{1,25},{... | collective-permute-start | bytes 49160 | tf_op jit(solution)/shard_map/ppermute | solution.py:399
  97.8 0.6 collective-permute-start.12
  98.5 2.3 %collective-permute-start.11 = (bf16[64,128]{1,0:T(8,128)(2,1)S(1)}, bf16[64,128]{1,0:T(8,128)(2,1)S(1)}, u32[]{:S(2)}, u32[]{:S(2)}) collective-permute-start(bf16[64,128]{1,0:T(8,128)(2,1)S(1)} %add_convert_fusion.1), channel_id=1, source_target_pairs={{0,8},{4,12},{8,0},{12,4},{16,24},{20,28},{24,16},{28,20},{1,9},{5... | collective-permute-start | bytes 49160 | tf_op jit(solution)/shard_map/ppermute | solution.py:399
  100.8 1.1 collective-permute-done.13
  102.0 0.5 collective-permute-done.12
  102.5 0.1 collective-permute-done.11
  102.7 0.9 finish.1
  103.7 1.5 %collective-permute-done.14 = bf16[4,16,2048]{2,1,0:T(8,128)(2,1)S(1)} collective-permute-done((bf16[4,16,2048]{2,1,0:T(8,128)(2,1)S(1)}, bf16[4,16,2048]{2,1,0:T(8,128)(2,1)S(1)}, u32[]{:S(2)}, u32[]{:S(2)}) %collective-permute-start.14) | collective-permute-done | bytes 262176 | tf_op jit(solution)/shard_map/ppermute | solution.py:399
  105.3 2.0 %collective-permute-start.15 = (bf16[16,2048]{1,0:T(8,128)(2,1)S(1)}, bf16[16,2048]{1,0:T(8,128)(2,1)S(1)}, u32[]{:S(2)}, u32[]{:S(2)}) collective-permute-start(bf16[16,2048]{1,0:T(8,128)(2,1)S(1)} %get-tuple-element.52), channel_id=1, source_target_pairs={{0,8},{4,12},{8,0},{12,4},{16,24},{20,28},{24,16},{28,20},{1,9},{5... | collective-permute-start | bytes 196616 | tf_op jit(solution)/shard_map/ppermute | solution.py:399
  107.3 1.1 collective-permute-start.16
  108.4 1.4 %collective-permute-start.17 = (bf16[16,2048]{1,0:T(8,128)(2,1)S(1)}, bf16[16,2048]{1,0:T(8,128)(2,1)S(1)}, u32[]{:S(2)}, u32[]{:S(2)}) collective-permute-start(bf16[16,2048]{1,0:T(8,128)(2,1)S(1)} %get-tuple-element.53), channel_id=1, source_target_pairs={{0,24},{4,28},{8,16},{12,20},{16,8},{20,12},{24,0},{28,4},{1,25},{... | collective-permute-start | bytes 196616 | tf_op jit(solution)/shard_map/ppermute | solution.py:399
  109.8 0.8 copy.38
  110.6 4.7 %collective-permute-done.16 = bf16[16,2048]{1,0:T(8,128)(2,1)S(1)} collective-permute-done((bf16[16,2048]{1,0:T(8,128)(2,1)S(1)}, bf16[16,2048]{1,0:T(8,128)(2,1)S(1)}, u32[]{:S(2)}, u32[]{:S(2)}) %collective-permute-start.16) | collective-permute-done | bytes 65568 | tf_op jit(solution)/shard_map/ppermute | solution.py:399
  115.3 0.7 fusion.2
  (40 shorter events, 0.8 us)
Async XLA Ops:
  0.6 18.3 %copy-start.6 = (s32[128,2]{0,1:T(2,128)S(1)}, s32[128,2]{0,1:T(2,128)}, u32[]{:S(2)}) copy-start(s32[128,2]{0,1:T(2,128)} %param.14) | copy-start | bytes 3076
  0.6 26.4 %copy-start.5 = (f32[128,2]{0,1:T(2,128)S(1)}, f32[128,2]{0,1:T(2,128)}, u32[]{:S(2)}) copy-start(f32[128,2]{0,1:T(2,128)} %param.13) | copy-start | bytes 3076
  0.7 26.3 %copy-start = (bf16[128,64,128]{2,1,0:T(8,128)(2,1)S(1)}, bf16[128,64,128]{2,1,0:T(8,128)(2,1)}, u32[]{:S(2)}) copy-start(bf16[128,64,128]{2,1,0:T(8,128)(2,1)} %param.12) | copy-start | bytes 6291460
  13.8 13.2 %all-to-all-start = ((bf16[4,32,2048]{2,1,0:T(8,128)(2,1)}), bf16[4,32,2048]{2,1,0:T(8,128)(2,1)S(1)}, u32[]{:S(2)}, u32[]{:S(2)}) async-start(bf16[4,32,2048]{2,1,0:T(8,128)(2,1)} %get-tuple-element.32), calls=%async_computation | async-start | bytes 1048576 | tf_op jit(solution)/shard_map/all_to_all | solution.py:541
  19.0 21.9 %copy-start.1 = (bf16[1,128,2048]{2,1,0:T(8,128)(2,1)S(1)}, bf16[1,128,2048]{2,1,0:T(8,128)(2,1)}, u32[]{:S(2)}) copy-start(bf16[1,128,2048]{2,1,0:T(8,128)(2,1)} %param.10) | copy-start | bytes 1572868
  19.0 21.9 %copy-start.3 = (bf16[128,128]{1,0:T(8,128)(2,1)S(1)}, bf16[128,128]{1,0:T(8,128)(2,1)}, u32[]{:S(2)}) copy-start(bf16[128,128]{1,0:T(8,128)(2,1)} %vert_ref.3) | copy-start | bytes 98308
  43.5 1.3 %collective-permute-start = (f32[64,128]{1,0:T(8,128)S(1)}, f32[64,128]{1,0:T(8,128)S(1)}, u32[]{:S(2)}, u32[]{:S(2)}) collective-permute-start(f32[64,128]{1,0:T(8,128)S(1)} %bitcast.97), channel_id=1, source_target_pairs={{0,4},{4,0},{8,12},{12,8},{16,20},{20,16},{24,28},{28,24},{1,5},{5... | collective-permute-start | bytes 98312 | tf_op jit(solution)/shard_map/ppermute | solution.py:399
  44.8 3.8 %collective-permute-start.1 = (bf16[64,128]{1,0:T(8,128)(2,1)S(1)}, bf16[64,128]{1,0:T(8,128)(2,1)S(1)}, u32[]{:S(2)}, u32[]{:S(2)}) collective-permute-start(bf16[64,128]{1,0:T(8,128)(2,1)S(1)} %add_convert_fusion.4), channel_id=1, source_target_pairs={{0,1},{1,0},{2,3},{3,2},{4,5},{5,4},{6,7},{7,6},{8,9},{9,8},{10,11... | collective-permute-start | bytes 49160 | tf_op jit(solution)/shard_map/ppermute | solution.py:399
  45.7 3.9 %collective-permute-start.2 = (bf16[64,128]{1,0:T(8,128)(2,1)S(1)}, bf16[64,128]{1,0:T(8,128)(2,1)S(1)}, u32[]{:S(2)}, u32[]{:S(2)}) collective-permute-start(bf16[64,128]{1,0:T(8,128)(2,1)S(1)} %add_convert_fusion.4), channel_id=1, source_target_pairs={{0,2},{1,3},{2,0},{3,1},{4,6},{5,7},{6,4},{7,5},{8,10},{9,11},{10,... | collective-permute-start | bytes 49160 | tf_op jit(solution)/shard_map/ppermute | solution.py:399
  46.3 4.6 %collective-permute-start.3 = (bf16[64,128]{1,0:T(8,128)(2,1)S(1)}, bf16[64,128]{1,0:T(8,128)(2,1)S(1)}, u32[]{:S(2)}, u32[]{:S(2)}) collective-permute-start(bf16[64,128]{1,0:T(8,128)(2,1)S(1)} %add_convert_fusion.4), channel_id=1, source_target_pairs={{0,3},{1,2},{2,1},{3,0},{4,7},{5,6},{6,5},{7,4},{8,11},{9,10},{10,... | collective-permute-start | bytes 49160 | tf_op jit(solution)/shard_map/ppermute | solution.py:399
  51.0 5.7 %collective-permute-start.6 = (bf16[64,128]{1,0:T(8,128)(2,1)S(1)}, bf16[64,128]{1,0:T(8,128)(2,1)S(1)}, u32[]{:S(2)}, u32[]{:S(2)}) collective-permute-start(bf16[64,128]{1,0:T(8,128)(2,1)S(1)} %add_convert_fusion.3), channel_id=1, source_target_pairs={{0,24},{4,28},{8,16},{12,20},{16,8},{20,12},{24,0},{28,4},{1,25},{... | collective-permute-start | bytes 49160 | tf_op jit(solution)/shard_map/ppermute | solution.py:399
  54.7 4.6 %collective-permute-start.5 = (bf16[64,128]{1,0:T(8,128)(2,1)S(1)}, bf16[64,128]{1,0:T(8,128)(2,1)S(1)}, u32[]{:S(2)}, u32[]{:S(2)}) collective-permute-start(bf16[64,128]{1,0:T(8,128)(2,1)S(1)} %add_convert_fusion.3), channel_id=1, source_target_pairs={{0,16},{4,20},{8,24},{12,28},{16,0},{20,4},{24,8},{28,12},{1,17},{... | collective-permute-start | bytes 49160 | tf_op jit(solution)/shard_map/ppermute | solution.py:399
  54.7 4.7 %collective-permute-start.4 = (bf16[64,128]{1,0:T(8,128)(2,1)S(1)}, bf16[64,128]{1,0:T(8,128)(2,1)S(1)}, u32[]{:S(2)}, u32[]{:S(2)}) collective-permute-start(bf16[64,128]{1,0:T(8,128)(2,1)S(1)} %add_convert_fusion.3), channel_id=1, source_target_pairs={{0,8},{4,12},{8,0},{12,4},{16,24},{20,28},{24,16},{28,20},{1,9},{5... | collective-permute-start | bytes 49160 | tf_op jit(solution)/shard_map/ppermute | solution.py:399
  72.9 13.3 %copy-start.2 = (bf16[1,128,2048]{2,1,0:T(8,128)(2,1)S(1)}, bf16[1,128,2048]{2,1,0:T(8,128)(2,1)}, u32[]{:S(2)}) copy-start(bf16[1,128,2048]{2,1,0:T(8,128)(2,1)} %param.10) | copy-start | bytes 1572868
  72.9 13.3 %copy-start.4 = (bf16[128,128]{1,0:T(8,128)(2,1)S(1)}, bf16[128,128]{1,0:T(8,128)(2,1)}, u32[]{:S(2)}) copy-start(bf16[128,128]{1,0:T(8,128)(2,1)} %vert_ref.3) | copy-start | bytes 98308
  88.9 1.3 %collective-permute-start.7 = (f32[64,128]{1,0:T(8,128)S(1)}, f32[64,128]{1,0:T(8,128)S(1)}, u32[]{:S(2)}, u32[]{:S(2)}) collective-permute-start(f32[64,128]{1,0:T(8,128)S(1)} %bitcast.95), channel_id=1, source_target_pairs={{0,4},{4,0},{8,12},{12,8},{16,20},{20,16},{24,28},{28,24},{1,5},{5... | collective-permute-start | bytes 98312 | tf_op jit(solution)/shard_map/ppermute | solution.py:399
  90.1 4.7 %collective-permute-start.10 = (bf16[64,128]{1,0:T(8,128)(2,1)S(1)}, bf16[64,128]{1,0:T(8,128)(2,1)S(1)}, u32[]{:S(2)}, u32[]{:S(2)}) collective-permute-start(bf16[64,128]{1,0:T(8,128)(2,1)S(1)} %add_convert_fusion.2), channel_id=1, source_target_pairs={{0,3},{1,2},{2,1},{3,0},{4,7},{5,6},{6,5},{7,4},{8,11},{9,10},{10,... | collective-permute-start | bytes 49160 | tf_op jit(solution)/shard_map/ppermute | solution.py:399
  91.1 3.7 %collective-permute-start.8 = (bf16[64,128]{1,0:T(8,128)(2,1)S(1)}, bf16[64,128]{1,0:T(8,128)(2,1)S(1)}, u32[]{:S(2)}, u32[]{:S(2)}) collective-permute-start(bf16[64,128]{1,0:T(8,128)(2,1)S(1)} %add_convert_fusion.2), channel_id=1, source_target_pairs={{0,1},{1,0},{2,3},{3,2},{4,5},{5,4},{6,7},{7,6},{8,9},{9,8},{10,11... | collective-permute-start | bytes 49160 | tf_op jit(solution)/shard_map/ppermute | solution.py:399
  92.6 3.7 %collective-permute-start.9 = (bf16[64,128]{1,0:T(8,128)(2,1)S(1)}, bf16[64,128]{1,0:T(8,128)(2,1)S(1)}, u32[]{:S(2)}, u32[]{:S(2)}) collective-permute-start(bf16[64,128]{1,0:T(8,128)(2,1)S(1)} %add_convert_fusion.2), channel_id=1, source_target_pairs={{0,2},{1,3},{2,0},{3,1},{4,6},{5,7},{6,4},{7,5},{8,10},{9,11},{10,... | collective-permute-start | bytes 49160 | tf_op jit(solution)/shard_map/ppermute | solution.py:399
  96.3 5.6 %collective-permute-start.13 = (bf16[64,128]{1,0:T(8,128)(2,1)S(1)}, bf16[64,128]{1,0:T(8,128)(2,1)S(1)}, u32[]{:S(2)}, u32[]{:S(2)}) collective-permute-start(bf16[64,128]{1,0:T(8,128)(2,1)S(1)} %add_convert_fusion.1), channel_id=1, source_target_pairs={{0,24},{4,28},{8,16},{12,20},{16,8},{20,12},{24,0},{28,4},{1,25},{... | collective-permute-start | bytes 49160 | tf_op jit(solution)/shard_map/ppermute | solution.py:399
  97.8 4.6 %collective-permute-start.12 = (bf16[64,128]{1,0:T(8,128)(2,1)S(1)}, bf16[64,128]{1,0:T(8,128)(2,1)S(1)}, u32[]{:S(2)}, u32[]{:S(2)}) collective-permute-start(bf16[64,128]{1,0:T(8,128)(2,1)S(1)} %add_convert_fusion.1), channel_id=1, source_target_pairs={{0,16},{4,20},{8,24},{12,28},{16,0},{20,4},{24,8},{28,12},{1,17},{... | collective-permute-start | bytes 49160 | tf_op jit(solution)/shard_map/ppermute | solution.py:399
  98.5 4.2 %collective-permute-start.11 = (bf16[64,128]{1,0:T(8,128)(2,1)S(1)}, bf16[64,128]{1,0:T(8,128)(2,1)S(1)}, u32[]{:S(2)}, u32[]{:S(2)}) collective-permute-start(bf16[64,128]{1,0:T(8,128)(2,1)S(1)} %add_convert_fusion.1), channel_id=1, source_target_pairs={{0,8},{4,12},{8,0},{12,4},{16,24},{20,28},{24,16},{28,20},{1,9},{5... | collective-permute-start | bytes 49160 | tf_op jit(solution)/shard_map/ppermute | solution.py:399
  103.6 1.6 %collective-permute-start.14 = (bf16[4,16,2048]{2,1,0:T(8,128)(2,1)S(1)}, bf16[4,16,2048]{2,1,0:T(8,128)(2,1)S(1)}, u32[]{:S(2)}, u32[]{:S(2)}) collective-permute-start(bf16[4,16,2048]{2,1,0:T(8,128)(2,1)S(1)} %slice_bitcast_fusion), channel_id=1, source_target_pairs={{0,4},{4,0},{8,12},{12,8},{16,20},{20,16},{24,28},{28,24},{1,5},{5... | collective-permute-start | bytes 786440 | tf_op jit(solution)/shard_map/ppermute | solution.py:399
  105.3 5.2 %collective-permute-start.15 = (bf16[16,2048]{1,0:T(8,128)(2,1)S(1)}, bf16[16,2048]{1,0:T(8,128)(2,1)S(1)}, u32[]{:S(2)}, u32[]{:S(2)}) collective-permute-start(bf16[16,2048]{1,0:T(8,128)(2,1)S(1)} %get-tuple-element.52), channel_id=1, source_target_pairs={{0,8},{4,12},{8,0},{12,4},{16,24},{20,28},{24,16},{28,20},{1,9},{5... | collective-permute-start | bytes 196616 | tf_op jit(solution)/shard_map/ppermute | solution.py:399
  107.3 8.0 %collective-permute-start.16 = (bf16[16,2048]{1,0:T(8,128)(2,1)S(1)}, bf16[16,2048]{1,0:T(8,128)(2,1)S(1)}, u32[]{:S(2)}, u32[]{:S(2)}) collective-permute-start(bf16[16,2048]{1,0:T(8,128)(2,1)S(1)} %get-tuple-element.54), channel_id=1, source_target_pairs={{0,16},{4,20},{8,24},{12,28},{16,0},{20,4},{24,8},{28,12},{1,17},{... | collective-permute-start | bytes 196616 | tf_op jit(solution)/shard_map/ppermute | solution.py:399
  108.4 6.9 %collective-permute-start.17 = (bf16[16,2048]{1,0:T(8,128)(2,1)S(1)}, bf16[16,2048]{1,0:T(8,128)(2,1)S(1)}, u32[]{:S(2)}, u32[]{:S(2)}) collective-permute-start(bf16[16,2048]{1,0:T(8,128)(2,1)S(1)} %get-tuple-element.53), channel_id=1, source_target_pairs={{0,24},{4,28},{8,16},{12,20},{16,8},{20,12},{24,0},{28,4},{1,25},{... | collective-permute-start | bytes 196616 | tf_op jit(solution)/shard_map/ppermute | solution.py:399
